TPU v7x, 256 devices: a whole 4x4x8 slice. The times are simulated.
256 devices in a mesh: gx: 8 (over y, core), gy: 32 (over x, z).
Axes of the slice: x: 4, y: 4, z: 8, core: 2. Of those that a mesh axis runs over, the one named last changes fastest.
Arguments:
- flow_field: float32 [16, 256, 256, 128], P(None, 'gx', 'gy'), may hold values from -6 to 6
- cotangent: float32 [16, 256, 256, 128], P(None, 'gx', 'gy'), may hold values from -6 to 6
- mode_weights: float32 [4, 16, 16, 256], replicated, may hold values from -3 to 3
- point_weights: float32 [16, 16], replicated, may hold values from -1.5 to 1.5
- point_bias: float32 [16], replicated, may hold values from -3 to 3
Outputs:
- output_field: float32 [16, 256, 256, 128], P(None, 'gx', 'gy')
- grad_field: float32 [16, 256, 256, 128], P(None, 'gx', 'gy')
- grad_modes: float32 [4, 16, 16, 256], replicated
- grad_point: float32 [16, 16], replicated
- grad_bias: float32 [16], replicated
All inputs are finite; a program needn't handle non-finite values.
Results may differ from a plain program's by a relative error of at most 0.00024.
Values sent between devices are 32-bit elements; how exact they have to be, the bound alone decides.
No kernel may reach another device: no remote copies, remote signals or barrier semaphores. Data moves between devices by JAX's collectives and lax.ppermute only.
A program may use at most 128 MiB of HBM per device.

v0:
```python
import math

import jax
import jax.numpy as jnp
from jax import lax
from jax.sharding import PartitionSpec as P

LOW_PASS = [
    0.23037781330885523,
    0.7148465705525415,
    0.6308807679295904,
    -0.02798376941698385,
    -0.18703481171888114,
    0.030841381835986965,
    0.032883011666982945,
    -0.010597401784997278,
]
HIGH_PASS = [(-1) ** position * LOW_PASS[7 - position] for position in range(8)]
GELU_SCALE = 0.7978845608028654
GELU_CUBE = 0.044715


def from_behind(value, axis, by):
    devices = lax.axis_size(axis)
    return lax.ppermute(value, axis, [(i, (i + by) % devices) for i in range(devices)])


def filter_table(filter_taps, out_count, in_count, periodic):
    row_index = lax.broadcasted_iota(jnp.int32, (out_count, in_count), 0)
    col_index = lax.broadcasted_iota(jnp.int32, (out_count, in_count), 1)
    offset = col_index - 2 * row_index
    if periodic:
        offset = offset % in_count
    matrix = jnp.zeros((out_count, in_count), jnp.float32)
    for position in range(8):
        matrix = matrix + filter_taps[position] * (offset == position).astype(jnp.float32)
    return matrix


def lifted_table(filter_taps, out_count, in_count):
    row_index = lax.broadcasted_iota(jnp.int32, (out_count, in_count), 0)
    col_index = lax.broadcasted_iota(jnp.int32, (out_count, in_count), 1)
    offset = row_index - 2 * col_index + 6
    matrix = jnp.zeros((out_count, in_count), jnp.float32)
    for position in range(8):
        matrix = matrix + filter_taps[position] * (offset == position).astype(jnp.float32)
    return matrix


def along_x(matrix, signal):
    return jnp.einsum("kr,arys->akys", matrix, signal, precision=lax.Precision.HIGHEST)


def along_y(matrix, signal):
    return jnp.einsum("kr,axrs->axks", matrix, signal, precision=lax.Precision.HIGHEST)


def plane_x(matrix, signal):
    return jnp.einsum("kr,ary->aky", matrix, signal, precision=lax.Precision.HIGHEST)


def plane_y(matrix, signal):
    return jnp.einsum("kr,axr->axk", matrix, signal, precision=lax.Precision.HIGHEST)


def to_lanes(signal):
    channels, extent_x, extent_y, planes = signal.shape
    return jnp.transpose(signal, (0, 3, 1, 2)).reshape(channels * planes, extent_x, extent_y)


def from_lanes(signal, channels):
    stacked, extent_x, extent_y = signal.shape
    return jnp.transpose(
        signal.reshape(channels, stacked // channels, extent_x, extent_y), (0, 2, 3, 1)
    )


def four_bands(signal):
    extent_x, extent_y = (signal.shape[1], signal.shape[2])
    low_x = plane_x(filter_table(LOW_PASS, extent_x // 2, extent_x, True), signal)
    high_x = plane_x(filter_table(HIGH_PASS, extent_x // 2, extent_x, True), signal)
    low_y = filter_table(LOW_PASS, extent_y // 2, extent_y, True)
    high_y = filter_table(HIGH_PASS, extent_y // 2, extent_y, True)
    return jnp.stack(
        [
            plane_y(low_y, low_x),
            plane_y(low_y, high_x),
            plane_y(high_y, low_x),
            plane_y(high_y, high_x),
        ]
    )


def join_bands(changes):
    modes_x, modes_y = (changes.shape[2], changes.shape[3])
    low_x = filter_table(LOW_PASS, modes_x, 2 * modes_x, True).T
    high_x = filter_table(HIGH_PASS, modes_x, 2 * modes_x, True).T
    low_y = filter_table(LOW_PASS, modes_y, 2 * modes_y, True).T
    high_y = filter_table(HIGH_PASS, modes_y, 2 * modes_y, True).T
    from_low = plane_y(low_y, changes[0]) + plane_y(high_y, changes[2])
    from_high = plane_y(low_y, changes[1]) + plane_y(high_y, changes[3])
    return plane_x(low_x, from_low) + plane_x(high_x, from_high)


def gelu_parts(signal):
    tangent = jnp.tanh(GELU_SCALE * (signal + GELU_CUBE * signal * signal * signal))
    activated = 0.5 * signal * (1.0 + tangent)
    gelu_slope = 0.5 * (1.0 + tangent) + 0.5 * signal * (1.0 - tangent * tangent) * GELU_SCALE * (
        1.0 + 3.0 * GELU_CUBE * signal * signal
    )
    return (activated, gelu_slope)


def wave_block(signal, weights_grid, transposed):
    x_index = lax.axis_index("gx")
    channels = signal.shape[0]
    extent_x, extent_y = (signal.shape[1], signal.shape[2])
    margin = from_behind(signal[:, :6], "gx", -1)
    halved = along_x(
        filter_table(LOW_PASS, extent_x // 2, extent_x + 6, False),
        jnp.concatenate([signal, margin], 1),
    )
    margin = from_behind(halved[:, :, :6], "gy", -1)
    level_one = along_y(
        filter_table(LOW_PASS, extent_y // 2, extent_y + 6, False),
        jnp.concatenate([halved, margin], 2),
    )
    level_one = to_lanes(lax.all_to_all(level_one, "gy", split_axis=3, concat_axis=2, tiled=True))
    rows_one, cols_one = (level_one.shape[1], level_one.shape[2])
    margin = from_behind(level_one[:, :6], "gx", -1)
    level_two = plane_x(
        filter_table(LOW_PASS, rows_one // 2, rows_one + 6, False),
        jnp.concatenate([level_one, margin], 1),
    )
    level_two = plane_y(filter_table(LOW_PASS, cols_one // 2, cols_one, True), level_two)
    rows_two, cols_two = (level_two.shape[1], level_two.shape[2])
    margin = from_behind(level_two[:, :6], "gx", -1)
    level_three = plane_x(
        filter_table(LOW_PASS, rows_two // 2, rows_two + 6, False),
        jnp.concatenate([level_two, margin], 1),
    )
    level_three = plane_y(filter_table(LOW_PASS, cols_two // 2, cols_two, True), level_three)
    gathered = lax.all_gather(level_three, "gx", axis=1, tiled=True)
    wave_bands = four_bands(gathered)
    stacked, modes_x, modes_y = (wave_bands.shape[1], wave_bands.shape[2], wave_bands.shape[3])
    split_bands = wave_bands.reshape(4, channels, stacked // channels, modes_x, modes_y)
    if transposed:
        mixed_bands = jnp.einsum(
            "bozxy,bioxy->bizxy", split_bands, weights_grid, precision=lax.Precision.HIGHEST
        )
    else:
        mixed_bands = jnp.einsum(
            "bizxy,bioxy->bozxy", split_bands, weights_grid, precision=lax.Precision.HIGHEST
        )
    delta_three = join_bands((mixed_bands - split_bands).reshape(4, stacked, modes_x, modes_y))
    own_rows = rows_two // 2
    own_part = lax.dynamic_slice_in_dim(delta_three, x_index * own_rows, own_rows, 1)
    margin = from_behind(own_part[:, own_rows - 3 :], "gx", 1)
    delta_two = plane_x(
        lifted_table(LOW_PASS, 2 * own_rows, own_rows + 3), jnp.concatenate([margin, own_part], 1)
    )
    cols_three = own_part.shape[2]
    delta_two = plane_y(filter_table(LOW_PASS, cols_three, 2 * cols_three, True).T, delta_two)
    margin = from_behind(delta_two[:, rows_two - 3 :], "gx", 1)
    delta_one = plane_x(
        lifted_table(LOW_PASS, 2 * rows_two, rows_two + 3), jnp.concatenate([margin, delta_two], 1)
    )
    delta_one = plane_y(filter_table(LOW_PASS, cols_two, 2 * cols_two, True).T, delta_one)
    returned = lax.all_to_all(
        from_lanes(delta_one, channels), "gy", split_axis=2, concat_axis=3, tiled=True
    )
    rows_back = returned.shape[1]
    margin = from_behind(returned[:, rows_back - 3 :], "gx", 1)
    widened = along_x(
        lifted_table(LOW_PASS, 2 * rows_back, rows_back + 3), jnp.concatenate([margin, returned], 1)
    )
    cols_back = widened.shape[2]
    margin = from_behind(widened[:, :, cols_back - 3 :], "gy", 1)
    delta_zero = along_y(
        lifted_table(LOW_PASS, 2 * cols_back, cols_back + 3), jnp.concatenate([margin, widened], 2)
    )
    return (signal + delta_zero, split_bands)


def local(flow_field, cotangent, mode_weights, point_weights, point_bias):
    channels = flow_field.shape[0]
    modes_x = flow_field.shape[1] * lax.axis_size("gx") // 16
    modes_y = flow_field.shape[2] * lax.axis_size("gy") // 16
    weights_grid = mode_weights.reshape(4, channels, channels, modes_x, modes_y)
    spectral_flow, bands_flow = wave_block(flow_field, weights_grid, False)
    pointwise = jnp.einsum(
        "io,ixys->oxys", point_weights, flow_field, precision=lax.Precision.HIGHEST
    )
    before_gelu = spectral_flow + pointwise + point_bias[:, None, None, None]
    output_field, gelu_slope = gelu_parts(before_gelu)
    grad_inner = cotangent * gelu_slope
    spectral_grad, bands_grad = wave_block(grad_inner, weights_grid, True)
    point_back = jnp.einsum(
        "io,oxys->ixys", point_weights, grad_inner, precision=lax.Precision.HIGHEST
    )
    grad_field = spectral_grad + point_back
    mode_local = jnp.einsum(
        "bizxy,bozxy->bioxy", bands_flow, bands_grad, precision=lax.Precision.HIGHEST
    )
    mode_local = mode_local.reshape(4, channels, channels, modes_x * modes_y)
    mode_total = lax.psum(mode_local, "gy")
    point_local = jnp.einsum(
        "ixys,oxys->io", flow_field, grad_inner, precision=lax.Precision.HIGHEST
    )
    bias_local = jnp.sum(grad_inner, axis=(1, 2, 3))
    point_total, bias_total = lax.psum((point_local, bias_local), ("gx", "gy"))
    plane_total = flow_field.shape[3]
    cell_count = (
        plane_total
        * flow_field.shape[1]
        * flow_field.shape[2]
        * lax.axis_size("gx")
        * lax.axis_size("gy")
    )
    grad_modes = mode_total / math.sqrt(plane_total)
    grad_point = point_total / math.sqrt(cell_count)
    grad_bias = bias_total / math.sqrt(cell_count)
    return (output_field, grad_field, grad_modes, grad_point, grad_bias)


def solution(mesh):
    in_specs = (P(None, "gx", "gy", None), P(None, "gx", "gy", None), P(), P(), P())
    out_specs = (P(None, "gx", "gy", None), P(None, "gx", "gy", None), P(), P(), P())
    return jax.shard_map(local, mesh=mesh, in_specs=in_specs, out_specs=out_specs, check_vma=False)
```

profile of v0, /device:TPU:1, one launch (start us, length us, event | category | flops | bytes accessed | tf_op | source)
XLA Modules:
  0.0 605.5 jit_solution(3356555167298708479)
XLA Ops:
  12.5 6.3 %collective-permute-done = f32[16,6,8,128]{3,1,2,0:T(8,128)S(1)} collective-permute-done((f32[16,6,8,128]{3,1,2,0:T(8,128)S(1)}, f32[16,6,8,128]{3,1,2,0:T(8,128)S(1)}, u32[]{:S(2)}, u32[]{:S(2)}) %collective-permute-start) | collective-permute-done | bytes 393248 | tf_op jit(solution)/shard_map/ppermute | solution.py:25
  20.7 7.8 %collective-permute-start.1 = (f32[16,16,6,128]{3,1,2,0:T(8,128)S(1)}, f32[16,16,6,128]{3,1,2,0:T(8,128)S(1)}, u32[]{:S(2)}, u32[]{:S(2)}) collective-permute-start(f32[16,16,6,128]{3,1,2,0:T(8,128)S(1)} %slice.105), channel_id=1, source_target_pairs={{0,31},{1,0},{2,1},{3,2},{4,3},{5,4},{6,5},{7,6},{8,7},{9,8},{10,9... | collective-permute-start | bytes 2359304 | tf_op jit(solution)/shard_map/ppermute | solution.py:25
  28.6 15.7 %collective-permute-done.1 = f32[16,16,6,128]{3,1,2,0:T(8,128)S(1)} collective-permute-done((f32[16,16,6,128]{3,1,2,0:T(8,128)S(1)}, f32[16,16,6,128]{3,1,2,0:T(8,128)S(1)}, u32[]{:S(2)}, u32[]{:S(2)}) %collective-permute-start.1) | collective-permute-done | bytes 786464 | tf_op jit(solution)/shard_map/ppermute | solution.py:25
  55.3 7.4 %all-to-all-start = ((f32[32,1,4096]{2,1,0:T(1,128)}), f32[32,1,4096]{2,1,0:T(1,128)S(1)}, u32[]{:S(2)}, u32[]{:S(2)}) async-start(f32[32,1,4096]{2,1,0:T(1,128)} %reshape.86), calls=%async_computation | async-start | bytes 1048576 | tf_op jit(solution)/shard_map/all_to_all | solution.py:128
  62.7 6.2 %copy.304 = f32[4,16,16,256]{2,1,3,0:T(8,128)} copy(f32[4,16,16,256]{3,2,1,0:T(8,128)S(1)} %copy-done.4) | data formatting | bytes 2097152 | tf_op jit(solution)/shard_map/reshape | solution.py:189
  68.9 6.5 %all-to-all-done = f32[32,1,4096]{2,1,0:T(1,128)S(1)} async-done(((f32[32,1,4096]{2,1,0:T(1,128)}), f32[32,1,4096]{2,1,0:T(1,128)S(1)}, u32[]{:S(2)}, u32[]{:S(2)}) %all-to-all-start) | async-done | bytes 524320 | tf_op jit(solution)/shard_map/all_to_all | solution.py:128
  94.3 5.6 collective-permute-done.2
  107.8 15.4 %all_gather.6 = f32[64,32,32]{0,2,1:T(8,128)S(1)} all-gather(f32[64,4,32]{0,2,1:T(8,128)S(1)} %fusion.123), channel_id=1, replica_groups=mesh['gx'=8,'gy'=32] {'gx'}, dimensions={1}, use_global_device_ids=true | all-gather | bytes 294912 | tf_op jit(solution)/shard_map/all_gather | solution.py:143
  129.6 14.9 %bitcast_subtract_fusion.1 = f32[4,16,4,16,16]{1,2,4,3,0:T(4,128)S(1)} fusion(f32[4,16,16,16,16]{2,1,4,3,0:T(8,128)} %bitcast.264, f32[1,16,4,16,16]{1,2,4,3,0:T(4,128)S(1)} %copy.227, f32[1,16,4,16,16]{1,2,4,3,0:T(4,128)S(1)} %copy.226, f32[1,16,4,16,16]{1,2,4,3,0:T(4,128)S(1)} %copy.225, f32[1,16,4,16,16]{1,2,4,3,0:T(4,128)S(1)} %copy.224), kind=kOutput, calls=%fused_computation.23 | convolution fusion | flops 13041664 | bytes 1572864 | tf_op jit(solution)/shard_map/bizxy,bioxy->bozxy/dot_general | solution.py:152
  175.8 17.0 %all_to_all.72 = f32[32,1,4096]{2,1,0:T(1,128)S(1)} all-to-all(f32[32,1,4096]{2,1,0:T(1,128)S(1)} %reshape.88), channel_id=1, replica_groups=mesh['gx'=8,'gy'=32] {'gy'}, dimensions={0} | all-to-all | bytes 1048576 | tf_op jit(solution)/shard_map/all_to_all | solution.py:169
  205.1 6.9 %collective-permute-start.6 = (f32[16,3,4,128]{3,1,2,0:T(4,128)S(1)}, f32[16,3,4,128]{3,1,2,0:T(4,128)S(1)}, u32[]{:S(2)}, u32[]{:S(2)}) collective-permute-start(f32[16,3,4,128]{3,1,2,0:T(4,128)S(1)} %slice.114), channel_id=1, source_target_pairs={{0,32},{32,64},{64,96},{96,128},{128,160},{160,192},{192,224},{224... | collective-permute-start | bytes 294920 | tf_op jit(solution)/shard_map/ppermute | solution.py:25
  220.0 13.4 %collective-permute-done.7 = f32[16,32,3,128]{3,1,2,0:T(8,128)S(1)} collective-permute-done((f32[16,32,3,128]{3,1,2,0:T(8,128)S(1)}, f32[16,32,3,128]{3,1,2,0:T(8,128)S(1)}, u32[]{:S(2)}, u32[]{:S(2)}) %collective-permute-start.7) | collective-permute-done | bytes 786464 | tf_op jit(solution)/shard_map/ppermute | solution.py:25
  233.6 6.6 %fusion.1133 = (f32[16]{0:T(128)}, f32[16,32,8,128]{3,2,1,0:T(8,128)S(1)}, f32[16,32,8,128]{3,2,1,0:T(8,128)}) fusion(f32[16,32,8,128]{3,2,1,0:T(8,128)S(1)} %copy-done.20, f32[16]{0:T(128)S(1)} %copy-done.21, f32[16,32,8,128]{3,0,2,1:T(8,128)S(1)} %fusion.27, f32[16,32,8,128]{3,2,1,0:T(8,128)S(1)} %copy-done.1, s32[7]{0:T(128)S(1)} %iota_multiply_fusion.2, ...), kind=kOutput, calls=%fused_computation.1198 | convolution fusion | flops 56100200 | bytes 12320924 | tf_op jit(solution)/shard_map/kr,axrs->axks/dot_general | solution.py:55
  252.4 16.0 %collective-permute-done.9 = f32[16,16,6,128]{3,1,2,0:T(8,128)S(1)} collective-permute-done((f32[16,16,6,128]{3,1,2,0:T(8,128)S(1)}, f32[16,16,6,128]{3,1,2,0:T(8,128)S(1)}, u32[]{:S(2)}, u32[]{:S(2)}) %collective-permute-start.9) | collective-permute-done | bytes 786464 | tf_op jit(solution)/shard_map/ppermute | solution.py:25
  278.6 19.1 %all_to_all.73 = f32[32,1,4096]{2,1,0:T(1,128)S(1)} all-to-all(f32[32,1,4096]{2,1,0:T(1,128)S(1)} %reshape.90), channel_id=1, replica_groups=mesh['gx'=8,'gy'=32] {'gy'}, dimensions={0} | all-to-all | bytes 1048576 | tf_op jit(solution)/shard_map/all_to_all | solution.py:128
  327.3 19.1 %all_gather.7 = f32[64,32,32]{0,2,1:T(8,128)S(1)} all-gather(f32[64,4,32]{0,2,1:T(8,128)S(1)} %fusion.119), channel_id=1, replica_groups=mesh['gx'=8,'gy'=32] {'gx'}, dimensions={1}, use_global_device_ids=true | all-gather | bytes 294912 | tf_op jit(solution)/shard_map/all_gather | solution.py:143
  354.4 18.2 %bitcast_subtract_fusion = f32[4,16,4,16,16]{1,2,4,3,0:T(4,128)S(1)} fusion(f32[4,16,16,16,16]{2,1,4,3,0:T(8,128)} %bitcast.265, f32[1,16,4,16,16]{1,2,4,3,0:T(4,128)} %copy.269, f32[1,16,4,16,16]{1,2,4,3,0:T(4,128)} %copy.268, f32[1,16,4,16,16]{1,2,4,3,0:T(4,128)} %copy.267, f32[1,16,4,16,16]{1,2,4,3,0:T(4,128)S(1)} %copy.266), kind=kOutput, calls=%fused_computation.19 | convolution fusion | flops 13041664 | bytes 1572864 | tf_op jit(solution)/shard_map/bozxy,bioxy->bizxy/dot_general | solution.py:148
  410.5 5.4 all-to-all-start.3
  416.0 17.6 %fusion.86 = f32[4,16,16,16,16]{4,3,2,1,0:T(8,128)} fusion(f32[1,16,4,16,16]{1,2,4,3,0:T(4,128)} %copy.269, f32[1,16,4,16,16]{1,2,4,3,0:T(4,128)} %copy.268, f32[1,16,4,16,16]{1,2,4,3,0:T(4,128)} %copy.267, f32[1,16,4,16,16]{1,2,4,3,0:T(4,128)} %copy-done.10, f32[1,16,4,16,16]{1,2,4,3,0:T(4,128)} %copy-done.9, f32[1,16,4,16,16]{1,2,4,3,0:T(4,128)} %copy-done.7, ...), kind=kOutput, calls=%fused_computation.106 | convolution fusion | flops 12976128 | bytes 1572864 | tf_op jit(solution)/shard_map/bizxy,bozxy->bioxy/dot_general | solution.py:202
  433.6 7.7 %copy.290 = f32[4,16,16,256]{3,2,1,0:T(8,128)} copy(f32[4,16,16,256]{1,2,3,0:T(8,128)} %bitcast.266) | data formatting | bytes 2097152 | tf_op jit(solution)/shard_map/reshape | solution.py:205
  441.4 6.3 %fusion.45 = f32[16,16]{0,1:T(8,128)S(1)} fusion(f32[16,32,8,128]{3,2,1,0:T(8,128)} %param.5, f32[16,32,8,128]{3,2,1,0:T(8,128)S(1)} %get-tuple-element.28), kind=kOutput, calls=%fused_computation.66 | convolution fusion | flops 100663296 | bytes 4195328 | tf_op jit(solution)/shard_map/ixys,oxys->io/dot_general | solution.py:207
  447.7 80.1 %all-reduce = (f32[16,16]{0,1:T(8,128)S(1)}, f32[16]{0:T(128)S(1)}) all-reduce(f32[16,16]{0,1:T(8,128)S(1)} %fusion.45, f32[16]{0:T(128)S(1)} %copy-done.19), channel_id=1, replica_groups=mesh['gx'=8,'gy'=32] {'gx','gy'}, use_global_device_ids=true, to_apply=%region_1.2 | all-reduce | flops 272 | bytes 2176 | tf_op jit(solution)/shard_map/psum | solution.py:211
  551.4 37.7 %all-reduce.3.cloned.1.call-done = f32[4,16,16,256]{3,2,1,0:T(8,128)} async-done(((f32[4,16,16,256]{3,2,1,0:T(8,128)}), f32[4,16,16,256]{3,2,1,0:T(8,128)}) %all-reduce.3.cloned.1.call-update) | async-done | bytes 1048592 | tf_op jit(solution)/shard_map/psum | solution.py:206
  593.3 5.2 bitcast_add_fusion
  (209 shorter events, 228.2 us)
Async XLA Ops:
  7.2 210.0 %copy-start = (f32[16,16]{1,0:T(8,128)S(1)}, f32[16,16]{1,0:T(8,128)}, u32[]{:S(2)}) copy-start(f32[16,16]{1,0:T(8,128)} %param.8) | copy-start | bytes 3076
  9.2 9.6 %collective-permute-start = (f32[16,6,8,128]{3,1,2,0:T(8,128)S(1)}, f32[16,6,8,128]{3,1,2,0:T(8,128)S(1)}, u32[]{:S(2)}, u32[]{:S(2)}) collective-permute-start(f32[16,6,8,128]{3,1,2,0:T(8,128)S(1)} %slice.104), channel_id=1, source_target_pairs={{0,224},{32,0},{64,32},{96,64},{128,96},{160,128},{192,160},{224,1... | collective-permute-start | bytes 1179656 | tf_op jit(solution)/shard_map/ppermute | solution.py:25
  20.7 23.6 %collective-permute-start.1 = (f32[16,16,6,128]{3,1,2,0:T(8,128)S(1)}, f32[16,16,6,128]{3,1,2,0:T(8,128)S(1)}, u32[]{:S(2)}, u32[]{:S(2)}) collective-permute-start(f32[16,16,6,128]{3,1,2,0:T(8,128)S(1)} %slice.105), channel_id=1, source_target_pairs={{0,31},{1,0},{2,1},{3,2},{4,3},{5,4},{6,5},{7,6},{8,7},{9,8},{10,9... | collective-permute-start | bytes 2359304 | tf_op jit(solution)/shard_map/ppermute | solution.py:25
  55.3 20.1 %all-to-all-start = ((f32[32,1,4096]{2,1,0:T(1,128)}), f32[32,1,4096]{2,1,0:T(1,128)S(1)}, u32[]{:S(2)}, u32[]{:S(2)}) async-start(f32[32,1,4096]{2,1,0:T(1,128)} %reshape.86), calls=%async_computation | async-start | bytes 1048576 | tf_op jit(solution)/shard_map/all_to_all | solution.py:128
  89.2 10.7 %collective-permute-start.2 = (f32[64,6,128]{2,1,0:T(8,128)S(1)}, f32[64,6,128]{2,1,0:T(8,128)S(1)}, u32[]{:S(2)}, u32[]{:S(2)}) collective-permute-start(f32[64,6,128]{2,1,0:T(8,128)S(1)} %slice.106), channel_id=1, source_target_pairs={{0,224},{32,0},{64,32},{96,64},{128,96},{160,128},{192,160},{224,1... | collective-permute-start | bytes 589832 | tf_op jit(solution)/shard_map/ppermute | solution.py:25
  101.0 5.8 collective-permute-start.3
  101.8 225.1 %copy-start.15 = (s32[32]{0:T(128)}, s32[32]{0:T(128)S(1)}, u32[]{:S(2)}) copy-start(s32[32]{0:T(128)S(1)} %iota_multiply_fusion.3) | copy-start | bytes 388
  154.7 1.4 collective-permute-start.4
  154.7 78.8 %copy-start.11 = (s32[7]{0:T(128)}, s32[7]{0:T(128)S(1)}, u32[]{:S(2)}) copy-start(s32[7]{0:T(128)S(1)} %iota_multiply_fusion.2) | copy-start | bytes 88
  157.0 4.5 collective-permute-start.5
  205.1 8.9 %collective-permute-start.6 = (f32[16,3,4,128]{3,1,2,0:T(4,128)S(1)}, f32[16,3,4,128]{3,1,2,0:T(4,128)S(1)}, u32[]{:S(2)}, u32[]{:S(2)}) collective-permute-start(f32[16,3,4,128]{3,1,2,0:T(4,128)S(1)} %slice.114), channel_id=1, source_target_pairs={{0,32},{32,64},{64,96},{96,128},{128,160},{160,192},{192,224},{224... | collective-permute-start | bytes 294920 | tf_op jit(solution)/shard_map/ppermute | solution.py:25
  215.2 18.2 %collective-permute-start.7 = (f32[16,32,3,128]{3,1,2,0:T(8,128)S(1)}, f32[16,32,3,128]{3,1,2,0:T(8,128)S(1)}, u32[]{:S(2)}, u32[]{:S(2)}) collective-permute-start(f32[16,32,3,128]{3,1,2,0:T(8,128)S(1)} %slice.115), channel_id=1, source_target_pairs={{0,1},{1,2},{2,3},{3,4},{4,5},{5,6},{6,7},{7,8},{8,9},{9,10},{10,1... | collective-permute-start | bytes 2359304 | tf_op jit(solution)/shard_map/ppermute | solution.py:25
  220.0 13.5 %copy-start.20 = (f32[16,32,8,128]{3,2,1,0:T(8,128)S(1)}, f32[16,32,8,128]{3,2,1,0:T(8,128)}, u32[]{:S(2)}) copy-start(f32[16,32,8,128]{3,2,1,0:T(8,128)} %param.6) | copy-start | bytes 6291460
  220.0 13.5 %copy-start.21 = (f32[16]{0:T(128)S(1)}, f32[16]{0:T(128)}, u32[]{:S(2)}) copy-start(f32[16]{0:T(128)} %param.9) | copy-start | bytes 196
  240.2 9.9 %collective-permute-start.8 = (f32[16,6,8,128]{3,2,1,0:T(8,128)S(1)}, f32[16,6,8,128]{3,2,1,0:T(8,128)S(1)}, u32[]{:S(2)}, u32[]{:S(2)}) collective-permute-start(f32[16,6,8,128]{3,2,1,0:T(8,128)S(1)} %slice.116), channel_id=1, source_target_pairs={{0,224},{32,0},{64,32},{96,64},{128,96},{160,128},{192,160},{224,1... | collective-permute-start | bytes 1179656 | tf_op jit(solution)/shard_map/ppermute | solution.py:25
  252.3 16.1 %collective-permute-start.9 = (f32[16,16,6,128]{3,1,2,0:T(8,128)S(1)}, f32[16,16,6,128]{3,1,2,0:T(8,128)S(1)}, u32[]{:S(2)}, u32[]{:S(2)}) collective-permute-start(f32[16,16,6,128]{3,1,2,0:T(8,128)S(1)} %slice.117), channel_id=1, source_target_pairs={{0,31},{1,0},{2,1},{3,2},{4,3},{5,4},{6,5},{7,6},{8,7},{9,8},{10,9... | collective-permute-start | bytes 2359304 | tf_op jit(solution)/shard_map/ppermute | solution.py:25
  310.9 8.0 %collective-permute-start.10 = (f32[64,6,128]{2,1,0:T(8,128)S(1)}, f32[64,6,128]{2,1,0:T(8,128)S(1)}, u32[]{:S(2)}, u32[]{:S(2)}) collective-permute-start(f32[64,6,128]{2,1,0:T(8,128)S(1)} %slice.118), channel_id=1, source_target_pairs={{0,224},{32,0},{64,32},{96,64},{128,96},{160,128},{192,160},{224,1... | collective-permute-start | bytes 589832 | tf_op jit(solution)/shard_map/ppermute | solution.py:25
  320.0 6.3 %collective-permute-start.11 = (f32[64,6,64]{2,1,0:T(8,128)S(1)}, f32[64,6,64]{2,1,0:T(8,128)S(1)}, u32[]{:S(2)}, u32[]{:S(2)}) collective-permute-start(f32[64,6,64]{2,1,0:T(8,128)S(1)} %bitcast.290), channel_id=1, source_target_pairs={{0,224},{32,0},{64,32},{96,64},{128,96},{160,128},{192,160},{224,1... | collective-permute-start | bytes 294920 | tf_op jit(solution)/shard_map/ppermute | solution.py:25
  388.7 1.4 collective-permute-start.12
  391.0 4.5 collective-permute-start.13
  410.5 117.2 %all-to-all-start.3 = ((f32[32,1,4096]{2,1,0:T(1,128)}), f32[32,1,4096]{2,1,0:T(1,128)S(1)}, u32[]{:S(2)}, u32[]{:S(2)}) async-start(f32[32,1,4096]{2,1,0:T(1,128)} %reshape.92), calls=%async_computation.3 | async-start | bytes 1048576 | tf_op jit(solution)/shard_map/all_to_all | solution.py:169
  415.9 173.2 %all-reduce.3.cloned.1.call-start = ((), (), s32[]{:S(2)}) async-start(), calls=%async_computation.4 | async-start | bytes 2097152 | tf_op jit(solution)/shard_map/psum | solution.py:206
  540.1 2.0 collective-permute-start.14
  545.2 46.2 %collective-permute-start.15 = (f32[16,32,3,128]{3,1,2,0:T(8,128)}, f32[16,32,3,128]{3,1,2,0:T(8,128)}, u32[]{:S(2)}, u32[]{:S(2)}) collective-permute-start(f32[16,32,3,128]{3,1,2,0:T(8,128)} %slice.127), channel_id=1, source_target_pairs={{0,1},{1,2},{2,3},{3,4},{4,5},{5,6},{6,7},{7,8},{8,9},{9,10},{10,1... | collective-permute-start | bytes 2359304 | tf_op jit(solution)/shard_map/ppermute | solution.py:25
  (17 other events, 96.9 us)
Sparse Core Ops, SparseCore 0:
  441.5 147.6 all-reduce.2
where the time goes:
time: 616 us; the launch traced here: 606 us
  blocking collectives  151 us (25%)
  waiting for transfers between devices  125 us (20%)
  local copies, waits for them, and re-layouts  122 us (20%)
  matrix products  119 us (19%)
  starting transfers between devices  60.4 us (10%)
  between operations  15.2 us (2%)
  other arithmetic  13.7 us (2%)
    ppermute x16, waiting for transfers between devices, from_behind(): lax.ppermute(value, axis, [(i, (i + by) % devices) for i in range(devices)])  80.7 us
    psum x1, blocking collectives, local(): point_total, bias_total = lax.psum((point_local, bias_local), ('gx', 'gy'))  80.1 us
    ppermute x16, starting transfers between devices, from_behind(): lax.ppermute(value, axis, [(i, (i + by) % devices) for i in range(devices)])  47.6 us
    unnamed x56, local copies, waits for them, and re-layouts  40.1 us
    psum x1, waiting for transfers between devices, local(): mode_total = lax.psum(mode_local, 'gy')  37.7 us
    all_gather x2, blocking collectives, wave_block(): gathered = lax.all_gather(level_three, 'gx', axis=1, tiled=True)  34.5 us
    dot_general x24, matrix products, plane_y(): jnp.einsum('kr,axr->axk', matrix, signal, precision=lax.Precision.HIGHEST)  20.3 us
    all_to_all x1, blocking collectives, wave_block(): lax.all_to_all(level_one, 'gy', split_axis=3, concat_axis=2, tiled=True)  19.1 us
  transfers between devices with their start and end apart: 19, of which 17 were waited for; matrix products, arithmetic and copies ran while one was open for 11% of the time, Pallas kernels for 0%

commit v1 on v0

v1 whole, which is shorter than its diff:
```python
import math

import jax
import jax.numpy as jnp
import numpy as np
from jax import lax
from jax.experimental import pallas as pl
from jax.experimental.pallas import tpu as pltpu
from jax.sharding import PartitionSpec as P

LOW_PASS = [
    0.23037781330885523,
    0.7148465705525415,
    0.6308807679295904,
    -0.02798376941698385,
    -0.18703481171888114,
    0.030841381835986965,
    0.032883011666982945,
    -0.010597401784997278,
]
HIGH_PASS = [(-1) ** position * LOW_PASS[7 - position] for position in range(8)]
GELU_SCALE = 0.7978845608028654
GELU_CUBE = 0.044715


def triple_low():
    taps = np.zeros(50)
    for p, hp in enumerate(LOW_PASS):
        for q, hq in enumerate(LOW_PASS):
            for r, hr in enumerate(LOW_PASS):
                taps[p + 2 * q + 4 * r] += hp * hq * hr
    return [float(t) for t in taps]


TRIPLE = triple_low()
HIGHEST = lax.Precision.HIGHEST
F32 = jnp.float32
VMEM = pltpu.CompilerParams(vmem_limit_bytes=56 * 1024 * 1024)


def tap(position, coef):
    at = position + 48 - 8 * coef
    return TRIPLE[at] if 0 <= at < 50 else None


def y_table():
    table = np.zeros((32, 8, 128), np.float32)
    for slab in range(32):
        for b in range(7):
            ky = (slab - 6 + b) % 32
            for mode in range(16):
                at = (ky - 2 * mode) % 32
                if at < 8:
                    table[slab, b, mode] = LOW_PASS[at]
                    table[slab, b, 16 + mode] = HIGH_PASS[at]
    return table.reshape(256, 128)


def gather_sum(pairs):
    total = None
    for weight, value in pairs:
        term = value * weight
        total = term if total is None else total + term
    return total


def swap_blocks(rows):
    lane = lax.broadcasted_iota(jnp.int32, (8, 128), 1)
    rows = list(rows)
    for bit in range(3):
        width = 16 << bit
        upper = (lane & width) != 0
        for lo in range(8):
            if lo & (1 << bit):
                continue
            hi = lo | (1 << bit)
            first, second = rows[lo], rows[hi]
            rows[lo] = jnp.where(upper, pltpu.roll(second, width, 1), first)
            rows[hi] = jnp.where(upper, second, pltpu.roll(first, 128 - width, 1))
    return rows


def partial_columns(x_scr, p_scr):
    def body(a, carry):
        cols = [x_scr[a, y] for y in range(8)]
        for b in range(7):
            pairs = [(tap(y, b), cols[y]) for y in range(8) if tap(y, b) is not None]
            p_scr[pl.ds(pl.multiple_of((a * 7 + b) * 16, 16), 16), :] = gather_sum(pairs)
        return carry

    lax.fori_loop(0, 10, body, 0)
    p_scr[pl.ds(1120, 32), :] = jnp.zeros((32, 128), F32)


def pack_planes(p_scr, s_ref):
    def body(octet, carry):
        for half in range(2):
            rows = [p_scr[pl.ds(octet * 128 + half * 8 + c, 8, stride=16), :] for c in range(8)]
            rows = swap_blocks(rows)
            for group in range(8):
                s_ref[group, half, pl.ds(pl.multiple_of(octet * 8, 8), 8), :] = rows[group]
        return carry

    lax.fori_loop(0, 9, body, 0)


def unpack_planes(r_ref, d_scr):
    def body(octet, carry):
        for half in range(2):
            rows = [
                r_ref[group, half, pl.ds(pl.multiple_of(octet * 8, 8), 8), :] for group in range(8)
            ]
            rows = swap_blocks(rows)
            for c in range(8):
                d_scr[pl.ds(octet * 128 + half * 8 + c, 8, stride=16), :] = rows[c]
        return carry

    lax.fori_loop(0, 9, body, 0)


def lift_columns(d_scr, e_scr):
    def body(a, carry):
        coefs = [d_scr[pl.ds(pl.multiple_of((a * 7 + b) * 16, 16), 16), :] for b in range(7)]
        for y in range(8):
            pairs = [(tap(y, b), coefs[b]) for b in range(7) if tap(y, b) is not None]
            e_scr[y, a] = gather_sum(pairs)
        return carry

    lax.fori_loop(0, 10, body, 0)


def analyse_kernel(flow_ref, s_ref, f_ref, x_scr, p_scr):
    def body(y, carry):
        sums = [None] * 10
        for x in range(32):
            value = flow_ref[pl.ds(x * 8 + y, 16, stride=256), :]
            f_ref[y, x * 16 : (x + 1) * 16, :] = value
            for a in range(10):
                weight = tap(x, a)
                if weight is not None:
                    term = value * weight
                    sums[a] = term if sums[a] is None else sums[a] + term
        for a in range(10):
            x_scr[a, y] = sums[a]
        return carry

    lax.fori_loop(0, 8, body, 0)
    partial_columns(x_scr, p_scr)
    pack_planes(p_scr, s_ref)


def rows_body(r_ref, l_scr, v_ref):
    def collect(q, carry):
        one = (q + 1) % 8
        two = (q + 2) % 8
        for t in range(4):
            for half in range(2):
                total = r_ref[q, half, 7 * (6 + t) : 7 * (6 + t) + 8, :]
                total = total + r_ref[one, half, 7 * (2 + t) : 7 * (2 + t) + 8, :]
                if t >= 2:
                    total = total + r_ref[two, half, 7 * (t - 2) : 7 * (t - 2) + 8, :]
                l_scr[q * 4 + t, half] = total
        return carry

    lax.fori_loop(0, 8, collect, 0)

    def bands(mode, carry):
        for half in range(2):
            parts = [l_scr[(2 * mode + n) % 32, half] for n in range(8)]
            v_ref[mode, half] = gather_sum(list(zip(LOW_PASS, parts)))
            v_ref[mode + 16, half] = gather_sum(list(zip(HIGH_PASS, parts)))
        return carry

    lax.fori_loop(0, 16, bands, 0)


def rows_kernel(r_ref, v_ref, l_scr):
    rows_body(r_ref, l_scr, v_ref)


def rows_grad_kernel(r_ref, v_ref, bias_ref, l_scr):
    rows_body(r_ref, l_scr, v_ref)
    first = r_ref[0, 0, 70:71, :]
    second = r_ref[0, 0, 71:72, :]
    bias = r_ref[0, 1, 70:71, :]
    for i in range(1, 8):
        first = first + r_ref[i, 0, 70:71, :]
        second = second + r_ref[i, 0, 71:72, :]
        bias = bias + r_ref[i, 1, 70:71, :]

    def put(coef, carry):
        v_ref[coef, 0, 7:8, :] = first
        v_ref[coef, 1, 7:8, :] = second
        return carry

    lax.fori_loop(0, 32, put, 0)
    bias_ref[...] = jnp.broadcast_to(bias, (8, 128))


def weights_kernel(index_ref, w_ref, o_ref):
    slab = index_ref[0]
    high = slab // 16
    mode = slab % 16
    right = mode // 8
    shift = (8 - mode % 8) * 16
    lane = lax.broadcasted_iota(jnp.int32, (256, 128), 1)
    low_y = jnp.where(right == 0, w_ref[high, :, 0:128], w_ref[high, :, 128:256])
    high_y = jnp.where(right == 0, w_ref[high + 2, :, 0:128], w_ref[high + 2, :, 128:256])
    low_y = pltpu.roll(low_y, shift % 128, 1)
    high_y = pltpu.roll(high_y, (shift + 16) % 128, 1)
    o_ref[...] = jnp.where(lane < 16, low_y, jnp.where(lane < 32, high_y, 0.0))


def column_bands(v_ref, q_ref, half):
    value = v_ref[:, half].reshape(256, 128)
    return lax.dot_general(
        value.T, q_ref[...], (((1,), (0,)), ((), ())), precision=HIGHEST,
        preferred_element_type=F32,
    )


def column_changes(d_scr, q_ref, o_ref):
    for half in range(2):
        value = lax.dot_general(
            q_ref[...], d_scr[half * 128 : (half + 1) * 128, :], (((1,), (1,)), ((), ())),
            precision=HIGHEST, preferred_element_type=F32,
        )
        o_ref[:, half] = value.reshape(32, 8, 128)


def mix_kernel(v_ref, q_ref, w_ref, o_ref, y_ref, d_scr):
    for half in range(2):
        y_ref[half * 128 : (half + 1) * 128, :] = column_bands(v_ref, q_ref, half)

    def body(o, carry):
        total = -y_ref[pl.ds(pl.multiple_of(o * 16, 16), 16), :]
        for i in range(16):
            total = total + y_ref[i * 16 : (i + 1) * 16, :] * w_ref[pl.ds(i * 16 + o, 1), :]
        d_scr[pl.ds(pl.multiple_of(o * 16, 16), 16), :] = total
        return carry

    lax.fori_loop(0, 16, body, 0)
    column_changes(d_scr, q_ref, o_ref)


def mix_grad_kernel(v_ref, q_ref, w_ref, y_ref, bias_ref, o_ref, g_ref, p_ref, b_scr, d_scr):
    for half in range(2):
        b_scr[half * 128 : (half + 1) * 128, :] = column_bands(v_ref, q_ref, half)

    def body(i, carry):
        flow = y_ref[pl.ds(pl.multiple_of(i * 16, 16), 16), :]
        total = -b_scr[pl.ds(pl.multiple_of(i * 16, 16), 16), :]
        for o in range(16):
            grad = b_scr[o * 16 : (o + 1) * 16, :]
            total = total + grad * w_ref[pl.ds(i * 16 + o, 1), :]
            g_ref[pl.ds(i * 16 + o, 1), :] = jnp.sum(flow * grad, axis=0, keepdims=True)
        d_scr[pl.ds(pl.multiple_of(i * 16, 16), 16), :] = total
        return carry

    lax.fori_loop(0, 16, body, 0)
    column_changes(d_scr, q_ref, o_ref)
    bias = bias_ref[0:1, :]
    first = v_ref[0, 0, 7:8, :]
    second = v_ref[0, 1, 7:8, :]
    for slab in range(32):
        o_ref[slab, 0, 7:8, :] = bias
        if slab > 0:
            first = first + v_ref[slab, 0, 7:8, :]
            second = second + v_ref[slab, 1, 7:8, :]
    p_ref[...] = jnp.zeros((8, 128), F32)
    p_ref[0:1, :] = first
    p_ref[1:2, :] = second


def spread_body(v_ref, l_scr, s_ref):
    def lift(mode, carry):
        for half in range(2):
            low = [v_ref[(mode + 16 - d) % 16, half] for d in range(4)]
            high = [v_ref[16 + (mode + 16 - d) % 16, half] for d in range(4)]
            for p in range(2):
                pairs = [(LOW_PASS[2 * d + p], low[d]) for d in range(4)]
                pairs += [(HIGH_PASS[2 * d + p], high[d]) for d in range(4)]
                l_scr[2 * mode + p, half] = gather_sum(pairs)
        return carry

    lax.fori_loop(0, 16, lift, 0)

    def send(i, carry):
        for half in range(2):
            s_ref[i, half, 64:72, :] = jnp.zeros((8, 128), F32)
            for a in range(10):
                s_ref[i, half, 7 * a : 7 * a + 8, :] = l_scr[(4 * i + 26 + a) % 32, half]
        return carry

    lax.fori_loop(0, 8, send, 0)


def spread_kernel(v_ref, s_ref, l_scr):
    spread_body(v_ref, l_scr, s_ref)


def spread_grad_kernel(v_ref, s_ref, bias_ref, l_scr):
    spread_body(v_ref, l_scr, s_ref)
    bias = v_ref[0, 0, 7:8, :]
    for slab in range(1, 32):
        bias = bias + v_ref[slab, 0, 7:8, :]
    bias_ref[...] = jnp.broadcast_to(bias, (8, 128))


def side_by_side(values):
    return jnp.concatenate(values, axis=1)


def centre_kernel(
    r_ref, f_ref, c_ref, w_ref, bias_ref, out_ref, g_ref, s_ref,
    d_scr, e_scr, pw_scr, x_scr, p_scr, sum_scr, pt_scr,
):
    unpack_planes(r_ref, d_scr)
    lift_columns(d_scr, e_scr)
    sum_scr[...] = jnp.zeros((16, 128), F32)
    pt_scr[...] = jnp.zeros((16, 16), F32)

    def body(y, carry):
        for part in range(4):
            fields = side_by_side(
                [f_ref[y, x * 16 : (x + 1) * 16, :] for x in range(part * 8, part * 8 + 8)]
            )
            pw_scr[:, part * 1024 : (part + 1) * 1024] = lax.dot_general(
                w_ref[...], fields, (((1,), (0,)), ((), ())), precision=HIGHEST,
                preferred_element_type=F32,
            )
        changes = [e_scr[y, a] for a in range(10)]
        bias = bias_ref[...]
        sums = [None] * 10
        total = sum_scr[...]
        for x in range(32):
            pairs = [(tap(x, a), changes[a]) for a in range(10) if tap(x, a) is not None]
            value = f_ref[y, x * 16 : (x + 1) * 16, :] + gather_sum(pairs)
            value = value + pw_scr[:, x * 128 : (x + 1) * 128] + bias
            square = value * value
            tangent = jnp.tanh(GELU_SCALE * (value + GELU_CUBE * square * value))
            half_up = 0.5 * (1.0 + tangent)
            out_ref[pl.ds(x * 8 + y, 16, stride=256), :] = value * half_up
            slope = half_up + (0.5 * GELU_SCALE) * value * (1.0 - tangent * tangent) * (
                1.0 + (3.0 * GELU_CUBE) * square
            )
            grad = c_ref[pl.ds(x * 8 + y, 16, stride=256), :] * slope
            g_ref[y, x * 16 : (x + 1) * 16, :] = grad
            total = total + grad
            for a in range(10):
                weight = tap(x, a)
                if weight is not None:
                    term = grad * weight
                    sums[a] = term if sums[a] is None else sums[a] + term
        sum_scr[...] = total
        for a in range(10):
            x_scr[a, y] = sums[a]
        point = pt_scr[...]
        for part in range(4):
            span = range(part * 8, part * 8 + 8)
            point = point + lax.dot_general(
                side_by_side([f_ref[y, x * 16 : (x + 1) * 16, :] for x in span]),
                side_by_side([g_ref[y, x * 16 : (x + 1) * 16, :] for x in span]),
                (((1,), (1,)), ((), ())), precision=HIGHEST, preferred_element_type=F32,
            )
        pt_scr[...] = point
        return carry

    lax.fori_loop(0, 8, body, 0)
    partial_columns(x_scr, p_scr)
    pack_planes(p_scr, s_ref)
    lane = lax.broadcasted_iota(jnp.int32, (16, 128), 1)
    row = lax.broadcasted_iota(jnp.int32, (16, 128), 0)
    repeat = (lane % 16 == row).astype(F32)
    wide = lax.dot_general(
        pt_scr[...], repeat, (((1,), (0,)), ((), ())), precision=HIGHEST,
        preferred_element_type=F32,
    )
    wide = jnp.where(lane // 16 == row % 8, wide, 0.0)
    first = jnp.sum(wide[0:8], axis=0, keepdims=True)
    second = jnp.sum(wide[8:16], axis=0, keepdims=True)
    totals = jnp.sum(sum_scr[...], axis=1, keepdims=True)
    bias_row = jnp.sum(jnp.where(lane == row, totals, 0.0), axis=0, keepdims=True)
    for group in range(8):
        s_ref[group, 0, 70:71, :] = first
        s_ref[group, 0, 71:72, :] = second
        s_ref[group, 1, 70:71, :] = bias_row


def finish_kernel(r_ref, g_ref, w_ref, out_ref, d_scr, e_scr, pw_scr):
    unpack_planes(r_ref, d_scr)
    lift_columns(d_scr, e_scr)

    def body(y, carry):
        for part in range(4):
            grads = side_by_side(
                [g_ref[y, x * 16 : (x + 1) * 16, :] for x in range(part * 8, part * 8 + 8)]
            )
            pw_scr[:, part * 1024 : (part + 1) * 1024] = lax.dot_general(
                w_ref[...], grads, (((1,), (0,)), ((), ())), precision=HIGHEST,
                preferred_element_type=F32,
            )
        changes = [e_scr[y, a] for a in range(10)]
        for x in range(32):
            pairs = [(tap(x, a), changes[a]) for a in range(10) if tap(x, a) is not None]
            value = g_ref[y, x * 16 : (x + 1) * 16, :] + gather_sum(pairs)
            value = value + pw_scr[:, x * 128 : (x + 1) * 128]
            out_ref[pl.ds(x * 8 + y, 16, stride=256), :] = value
        return carry

    lax.fori_loop(0, 8, body, 0)


def modes_sum_kernel(g_ref, o_ref):
    total = g_ref[0]
    for i in range(1, 8):
        total = total + g_ref[i]
    lane = lax.broadcasted_iota(jnp.int32, (8, 128), 1)
    packed = jnp.zeros((8, 128), F32)
    for k in range(4):
        rows = total[k * 8 : (k + 1) * 8, :]
        if k > 0:
            rows = pltpu.roll(rows, 32 * k, 1)
        packed = jnp.where(lane // 32 == k, rows, packed)

    def put(slab, carry):
        o_ref[slab] = packed
        return carry

    lax.fori_loop(0, 32, put, 0)


def modes_place_kernel(m_ref, o_ref):
    for high in range(2):
        for right in range(2):
            rows = [m_ref[high * 16 + right * 8 + m] for m in range(8)]
            rows = swap_blocks(rows)
            for k in range(4):
                for up in range(2):
                    for copy in range(8):
                        o_ref[
                            copy, high + 2 * up, k * 8 : (k + 1) * 8,
                            right * 128 : (right + 1) * 128,
                        ] = rows[2 * k + up]


def call(kernel, out_shapes, scratch=(), smem_first=False, n_in=1):
    single = not isinstance(out_shapes, list)
    shapes = [out_shapes] if single else out_shapes
    structs = [jax.ShapeDtypeStruct(s, F32) for s in shapes]
    specs = [pl.BlockSpec(memory_space=pltpu.VMEM)] * n_in
    if smem_first:
        specs[0] = pl.BlockSpec(memory_space=pltpu.SMEM)
    return pl.pallas_call(
        kernel,
        out_shape=structs[0] if single else structs,
        in_specs=specs,
        scratch_shapes=[pltpu.VMEM(s, F32) for s in scratch],
        compiler_params=VMEM,
    )


def local(flow_field, cotangent, mode_weights, point_weights, point_bias):
    swap_x = lambda v: lax.all_to_all(v, "gx", 0, 0, tiled=False)
    swap_y = lambda v: lax.all_to_all(v, "gy", 0, 0, tiled=False)
    packed = (8, 2, 72, 128)
    coefs = (32, 2, 8, 128)
    cells = (8, 512, 128)
    work_x = [(10, 8, 16, 128), (1152, 128)]
    work_lift = [(1152, 128), (8, 10, 16, 128), (16, 4096)]
    rows3 = [(32, 2, 8, 128)]
    table = jnp.asarray(y_table())
    slab = lax.axis_index("gy").astype(jnp.int32).reshape(1)

    weights = call(weights_kernel, (256, 128), smem_first=True, n_in=2)(
        slab, mode_weights.reshape(4, 256, 256)
    )
    sent, fields = call(analyse_kernel, [packed, cells], work_x)(flow_field.reshape(4096, 128))
    got = call(rows_kernel, coefs, rows3)(swap_x(sent))
    back, bands_flow = call(mix_kernel, [coefs, (256, 128)], [(256, 128)], n_in=3)(
        swap_y(got), table, weights
    )
    spread = call(spread_kernel, packed, rows3)(swap_y(back))
    output_field, grads, sent = call(
        centre_kernel, [(4096, 128), cells, packed],
        work_lift + work_x + [(16, 128), (16, 16)], n_in=5,
    )(
        swap_x(spread), fields, cotangent.reshape(4096, 128), point_weights.T,
        jnp.broadcast_to(point_bias[:, None], (16, 128)),
    )
    got, bias_part = call(rows_grad_kernel, [coefs, (8, 128)], rows3)(swap_x(sent))
    back, mode_part, point_total = call(
        mix_grad_kernel, [coefs, (256, 128), (8, 128)], [(256, 128)] * 2, n_in=5
    )(swap_y(got), table, weights, bands_flow, bias_part)
    spread, bias_total = call(spread_grad_kernel, [packed, (8, 128)], rows3)(swap_y(back))
    grad_field = call(finish_kernel, (4096, 128), work_lift, n_in=3)(
        swap_x(spread), grads, point_weights
    )
    part = call(modes_sum_kernel, (32, 8, 128))(swap_x(mode_part.reshape(8, 32, 128)))
    placed = call(modes_place_kernel, (8, 4, 32, 256))(swap_y(part))
    modes = jnp.transpose(swap_x(placed), (1, 0, 2, 3)).reshape(4, 16, 16, 256)

    planes = flow_field.shape[3]
    cell_count = planes * 256 * 256
    return (
        output_field.reshape(flow_field.shape),
        grad_field.reshape(flow_field.shape),
        modes / math.sqrt(planes),
        point_total[0:2].reshape(16, 16) / math.sqrt(cell_count),
        bias_total[0, :16] / math.sqrt(cell_count),
    )


def solution(mesh):
    in_specs = (P(None, "gx", "gy", None), P(None, "gx", "gy", None), P(), P(), P())
    out_specs = (P(None, "gx", "gy", None), P(None, "gx", "gy", None), P(), P(), P())
    return jax.shard_map(local, mesh=mesh, in_specs=in_specs, out_specs=out_specs, check_vma=False)
```

time: 616 us -> 223 us (0.36); the launches traced: 606 us -> 222 us
  matrix products: 119 us -> 0 us
  local copies, waits for them, and re-layouts: 122 us -> 3.97 us
  waiting for transfers between devices: 125 us -> 43 us
  blocking collectives: 151 us -> 76.1 us
  Pallas kernels: 0 us -> 57.8 us
  starting transfers between devices: 60.4 us -> 38.1 us
  between operations: 15.2 us -> 0.71 us
  other arithmetic: 13.7 us -> 1.96 us
    dot_general x54 -> x0, matrix products: 119 us -> none  [the longest x24 20.3 us: plane_y(): jnp.einsum('kr,axr->axk', matrix, signal, precision=lax.Precision.HIGHEST)]
    ppermute x16 -> x0, waiting for transfers between devices: 80.7 us -> none  [from_behind(): lax.ppermute(value, axis, [(i, (i + by) % devices) for i in range(devices)])]
    psum x1 -> x0, blocking collectives: 80.1 us -> none  [local(): point_total, bias_total = lax.psum((point_local, bias_local), ('gx', 'gy'))]
    pallas_call x0 -> x12, Pallas kernels: none -> 57.8 us  [the longest x1 19.3 us: local(): call(centre_kernel, [(4096, 128), cells, packed], work_lift + work_x + [(...]
    ppermute x16 -> x0, starting transfers between devices: 47.6 us -> none  [from_behind(): lax.ppermute(value, axis, [(i, (i + by) % devices) for i in range(devices)])]
    all_to_all x2 -> x5, blocking collectives: 36.1 us -> 76.1 us  [the longest x3 46 us: local(): swap_x = lambda v: lax.all_to_all(v, 'gx', 0, 0, tiled=False)]
    unnamed x56 -> x15, local copies, waits for them, and re-layouts: 40.1 us -> 1.46 us
    psum x1 -> x0, waiting for transfers between devices: 37.7 us -> none  [local(): mode_total = lax.psum(mode_local, 'gy')]
  transfers between devices with their start and end apart: 19 -> 6, of which waited for: 17 -> 6; matrix products, arithmetic and copies ran while one was open for 11% -> 1% of each run, Pallas kernels for 0% -> 8%
where the time goes in v1:
time: 223 us; the launch traced here: 222 us
  blocking collectives  76.1 us (34%)
  Pallas kernels  57.8 us (26%)
  waiting for transfers between devices  43 us (19%)
  starting transfers between devices  38.1 us (17%)
  local copies, waits for them, and re-layouts  3.97 us (2%)
    all_to_all x3, blocking collectives, local(): swap_x = lambda v: lax.all_to_all(v, 'gx', 0, 0, tiled=False)  46 us
    all_to_all x2, blocking collectives, local(): swap_y = lambda v: lax.all_to_all(v, 'gy', 0, 0, tiled=False)  30.1 us
    all_to_all x3, waiting for transfers between devices, local(): swap_y = lambda v: lax.all_to_all(v, 'gy', 0, 0, tiled=False)  22.3 us
    all_to_all x3, waiting for transfers between devices, local(): swap_x = lambda v: lax.all_to_all(v, 'gx', 0, 0, tiled=False)  20.8 us
    all_to_all x3, starting transfers between devices, local(): swap_y = lambda v: lax.all_to_all(v, 'gy', 0, 0, tiled=False)  19.9 us
    pallas_call x1, Pallas kernels, local(): call(centre_kernel, [(4096, 128), cells, packed], work_lift + work_x + [(...  19.3 us
    all_to_all x3, starting transfers between devices, local(): swap_x = lambda v: lax.all_to_all(v, 'gx', 0, 0, tiled=False)  18.2 us
    pallas_call x1, Pallas kernels, local(): call(finish_kernel, (4096, 128), work_lift, n_in=3)  9.36 us
  transfers between devices with their start and end apart: 6, of which 6 were waited for; matrix products, arithmetic and copies ran while one was open for 1% of the time, Pallas kernels for 8%

profile of v1, /device:TPU:1, one launch (start us, length us, event | category | flops | bytes accessed | tf_op | source)
XLA Modules:
  0.0 221.7 jit_solution(1393789617407606080)
XLA Ops:
  0.6 7.4 %shard_map.101 = (f32[8,2,72,128]{3,2,1,0:T(8,128)}, f32[8,512,128]{2,1,0:T(8,128)}) custom-call(f32[4096,128]{1,0:T(8,128)} %bitcast.15), custom_call_target="tpu_custom_call" | custom-call | tf_op jit(solution)/shard_map/pallas_call | solution.py:478
  8.0 17.8 %all_to_all.55.r_ref = f32[8,2,72,128]{3,2,1,0:T(8,128)} all-to-all(f32[8,2,72,128]{3,2,1,0:T(8,128)} %get-tuple-element.19), channel_id=1, replica_groups=mesh['gx'=8,'gy'=32] {'gx'}, dimensions={0} | all-to-all | bytes 1179648 | tf_op jit(solution)/shard_map/all_to_all | solution.py:464
  28.1 9.7 %all-to-all-start.1 = ((f32[32,2,8,128]{3,2,1,0:T(8,128)}), f32[32,2,8,128]{3,2,1,0:T(8,128)S(1)}, u32[]{:S(2)}, u32[]{:S(2)}) async-start(f32[32,2,8,128]{3,2,1,0:T(8,128)} %shard_map.102), calls=%async_computation.1 | async-start | bytes 524288 | tf_op jit(solution)/shard_map/all_to_all | solution.py:465
  39.9 7.6 %all-to-all-done.1.v_ref = f32[32,2,8,128]{3,2,1,0:T(8,128)S(1)} async-done(((f32[32,2,8,128]{3,2,1,0:T(8,128)}), f32[32,2,8,128]{3,2,1,0:T(8,128)S(1)}, u32[]{:S(2)}, u32[]{:S(2)}) %all-to-all-start.1) | async-done | bytes 262176 | tf_op jit(solution)/shard_map/all_to_all | solution.py:465
  48.2 2.9 %shard_map.104 = (f32[32,2,8,128]{3,2,1,0:T(8,128)}, f32[256,128]{1,0:T(8,128)}) custom-call(f32[32,2,8,128]{3,2,1,0:T(8,128)} %copy-done.2, f32[256,128]{1,0:T(8,128)} %constant.14.clone.q_ref, f32[256,128]{1,0:T(8,128)} %shard_map.103.w_ref), custom_call_target="tpu_custom_call" | custom-call | tf_op jit(solution)/shard_map/pallas_call | solution.py:480
  51.1 15.8 %all_to_all.56.v_ref = f32[32,2,8,128]{3,2,1,0:T(8,128)} all-to-all(f32[32,2,8,128]{3,2,1,0:T(8,128)} %get-tuple-element.20), channel_id=1, replica_groups=mesh['gx'=8,'gy'=32] {'gy'}, dimensions={0} | all-to-all | bytes 524288 | tf_op jit(solution)/shard_map/all_to_all | solution.py:465
  69.4 7.1 %all-to-all-start.3 = ((f32[8,2,72,128]{3,2,1,0:T(8,128)}), f32[8,2,72,128]{3,2,1,0:T(8,128)S(1)}, u32[]{:S(2)}, u32[]{:S(2)}) async-start(f32[8,2,72,128]{3,2,1,0:T(8,128)} %shard_map.105), calls=%async_computation.3 | async-start | bytes 1179648 | tf_op jit(solution)/shard_map/all_to_all | solution.py:464
  77.1 9.5 %all-to-all-done.3.r_ref = f32[8,2,72,128]{3,2,1,0:T(8,128)S(1)} async-done(((f32[8,2,72,128]{3,2,1,0:T(8,128)}), f32[8,2,72,128]{3,2,1,0:T(8,128)S(1)}, u32[]{:S(2)}, u32[]{:S(2)}) %all-to-all-start.3) | async-done | bytes 589856 | tf_op jit(solution)/shard_map/all_to_all | solution.py:464
  87.5 19.3 %shard_map.106 = (f32[4096,128]{1,0:T(8,128)}, f32[8,512,128]{2,1,0:T(8,128)}, f32[8,2,72,128]{3,2,1,0:T(8,128)}) custom-call(f32[8,2,72,128]{3,2,1,0:T(8,128)} %copy-done.1, f32[8,512,128]{2,1,0:T(8,128)} %get-tuple-element.21.f_ref, f32[4096,128]{1,0:T(8,128)} %bitcast.13, f32[16,16]{1,0:T(8,128)} %bitcast.19, f32[16,128]{1,0:T(8,128)} %broadcast_in_dim.2.bias_ref), custom_call_target="tpu_custom_call" | custom-call | tf_op jit(solution)/shard_map/pallas_call | solution.py:484
  106.8 15.4 %all_to_all.57.r_ref = f32[8,2,72,128]{3,2,1,0:T(8,128)} all-to-all(f32[8,2,72,128]{3,2,1,0:T(8,128)} %get-tuple-element.23), channel_id=1, replica_groups=mesh['gx'=8,'gy'=32] {'gx'}, dimensions={0} | all-to-all | bytes 1179648 | tf_op jit(solution)/shard_map/all_to_all | solution.py:464
  122.3 2.5 %shard_map.107 = (f32[32,2,8,128]{3,2,1,0:T(8,128)}, f32[8,128]{1,0:T(8,128)}) custom-call(f32[8,2,72,128]{3,2,1,0:T(8,128)} %all_to_all.57.r_ref), custom_call_target="tpu_custom_call" | custom-call | tf_op jit(solution)/shard_map/pallas_call | solution.py:491
  124.8 14.2 %all_to_all.58.v_ref = f32[32,2,8,128]{3,2,1,0:T(8,128)} all-to-all(f32[32,2,8,128]{3,2,1,0:T(8,128)} %get-tuple-element.24), channel_id=1, replica_groups=mesh['gx'=8,'gy'=32] {'gy'}, dimensions={0} | all-to-all | bytes 524288 | tf_op jit(solution)/shard_map/all_to_all | solution.py:465
  139.0 3.2 %shard_map.108 = (f32[32,2,8,128]{3,2,1,0:T(8,128)}, f32[256,128]{1,0:T(8,128)}, f32[8,128]{1,0:T(8,128)}) custom-call(f32[32,2,8,128]{3,2,1,0:T(8,128)} %all_to_all.58.v_ref, f32[256,128]{1,0:T(8,128)} %constant.14.clone.q_ref, f32[256,128]{1,0:T(8,128)} %shard_map.103.w_ref, f32[256,128]{1,0:T(8,128)} %get-tuple-element.25.y_ref, ...), custom_call_target="tpu_custom_call" | custom-call | tf_op jit(solution)/shard_map/pallas_call | solution.py:492
  142.2 12.8 %all_to_all.59.g_ref = f32[8,32,128]{2,1,0:T(8,128)} all-to-all(f32[8,32,128]{2,1,0:T(8,128)} %bitcast.18), channel_id=1, replica_groups=mesh['gx'=8,'gy'=32] {'gx'}, dimensions={0} | all-to-all | bytes 262144 | tf_op jit(solution)/shard_map/all_to_all | solution.py:464
  155.0 4.2 %all-to-all-start.6 = ((f32[32,2,8,128]{3,2,1,0:T(8,128)}), f32[32,2,8,128]{3,2,1,0:T(8,128)S(1)}, u32[]{:S(2)}, u32[]{:S(2)}) async-start(f32[32,2,8,128]{3,2,1,0:T(8,128)} %get-tuple-element.27), calls=%async_computation.6 | async-start | bytes 524288 | tf_op jit(solution)/shard_map/all_to_all | solution.py:465
  161.0 7.9 %all-to-all-done.6.v_ref = f32[32,2,8,128]{3,2,1,0:T(8,128)S(1)} async-done(((f32[32,2,8,128]{3,2,1,0:T(8,128)}), f32[32,2,8,128]{3,2,1,0:T(8,128)S(1)}, u32[]{:S(2)}, u32[]{:S(2)}) %all-to-all-start.6) | async-done | bytes 262176 | tf_op jit(solution)/shard_map/all_to_all | solution.py:465
  169.0 6.0 %all-to-all-start.9 = ((f32[32,8,128]{2,1,0:T(8,128)}), f32[32,8,128]{2,1,0:T(8,128)S(1)}, u32[]{:S(2)}, u32[]{:S(2)}) async-start(f32[32,8,128]{2,1,0:T(8,128)} %shard_map.111), calls=%async_computation.9 | async-start | bytes 262144 | tf_op jit(solution)/shard_map/all_to_all | solution.py:465
  175.0 2.4 %shard_map.109 = (f32[8,2,72,128]{3,2,1,0:T(8,128)}, f32[8,128]{1,0:T(8,128)}) custom-call(f32[32,2,8,128]{3,2,1,0:T(8,128)} %copy-done.3), custom_call_target="tpu_custom_call" | custom-call | tf_op jit(solution)/shard_map/pallas_call | solution.py:495
  177.4 6.7 %all-to-all-done.9.m_ref = f32[32,8,128]{2,1,0:T(8,128)S(1)} async-done(((f32[32,8,128]{2,1,0:T(8,128)}), f32[32,8,128]{2,1,0:T(8,128)S(1)}, u32[]{:S(2)}, u32[]{:S(2)}) %all-to-all-start.9) | async-done | bytes 131104 | tf_op jit(solution)/shard_map/all_to_all | solution.py:465
  184.1 6.7 %all-to-all-start.7 = ((f32[8,2,72,128]{3,2,1,0:T(8,128)}), f32[8,2,72,128]{3,2,1,0:T(8,128)S(1)}, u32[]{:S(2)}, u32[]{:S(2)}) async-start(f32[8,2,72,128]{3,2,1,0:T(8,128)} %get-tuple-element.28), calls=%async_computation.7 | async-start | bytes 1179648 | tf_op jit(solution)/shard_map/all_to_all | solution.py:464
  193.1 8.0 %all-to-all-done.7.r_ref = f32[8,2,72,128]{3,2,1,0:T(8,128)S(1)} async-done(((f32[8,2,72,128]{3,2,1,0:T(8,128)}), f32[8,2,72,128]{3,2,1,0:T(8,128)S(1)}, u32[]{:S(2)}, u32[]{:S(2)}) %all-to-all-start.7) | async-done | bytes 589856 | tf_op jit(solution)/shard_map/all_to_all | solution.py:464
  201.1 4.3 %all-to-all-start.10 = ((f32[8,4,32,256]{3,2,1,0:T(8,128)}), f32[8,4,32,256]{3,2,1,0:T(8,128)S(1)}, u32[]{:S(2)}, u32[]{:S(2)}) async-start(f32[8,4,32,256]{3,2,1,0:T(8,128)} %shard_map.112), calls=%async_computation.10 | async-start | bytes 2097152 | tf_op jit(solution)/shard_map/all_to_all | solution.py:464
  208.0 9.4 %shard_map.110 = f32[4096,128]{1,0:T(8,128)} custom-call(f32[8,2,72,128]{3,2,1,0:T(8,128)} %copy-done, f32[8,512,128]{2,1,0:T(8,128)} %get-tuple-element.29.g_ref, f32[16,16]{1,0:T(8,128)} %w_ref.1), custom_call_target="tpu_custom_call" | custom-call | tf_op jit(solution)/shard_map/pallas_call | solution.py:496
  217.3 3.2 %all-to-all-done.10 = f32[8,4,32,256]{3,2,1,0:T(8,128)S(1)} async-done(((f32[8,4,32,256]{3,2,1,0:T(8,128)}), f32[8,4,32,256]{3,2,1,0:T(8,128)S(1)}, u32[]{:S(2)}, u32[]{:S(2)}) %all-to-all-start.10) | async-done | bytes 1048608 | tf_op jit(solution)/shard_map/all_to_all | solution.py:464
  (26 shorter events, 16.7 us)
Async XLA Ops:
  28.1 19.4 %all-to-all-start.1 = ((f32[32,2,8,128]{3,2,1,0:T(8,128)}), f32[32,2,8,128]{3,2,1,0:T(8,128)S(1)}, u32[]{:S(2)}, u32[]{:S(2)}) async-start(f32[32,2,8,128]{3,2,1,0:T(8,128)} %shard_map.102), calls=%async_computation.1 | async-start | bytes 524288 | tf_op jit(solution)/shard_map/all_to_all | solution.py:465
  37.8 38.7 %copy-start.5 = (f32[16,16]{1,0:T(8,128)S(1)}, f32[16,16]{1,0:T(8,128)}, u32[]{:S(2)}) copy-start(f32[16,16]{1,0:T(8,128)} %w_ref.1) | copy-start | bytes 3076
  37.8 48.9 %copy-start.6 = (f32[16]{0:T(128)S(1)}, f32[16]{0:T(128)}, u32[]{:S(2)}) copy-start(f32[16]{0:T(128)} %param.10) | copy-start | bytes 196
  47.5 0.7 copy-start.2
  69.4 17.3 %all-to-all-start.3 = ((f32[8,2,72,128]{3,2,1,0:T(8,128)}), f32[8,2,72,128]{3,2,1,0:T(8,128)S(1)}, u32[]{:S(2)}, u32[]{:S(2)}) async-start(f32[8,2,72,128]{3,2,1,0:T(8,128)} %shard_map.105), calls=%async_computation.3 | async-start | bytes 1179648 | tf_op jit(solution)/shard_map/all_to_all | solution.py:464
  86.7 0.8 copy-start.1
  155.0 14.0 %all-to-all-start.6 = ((f32[32,2,8,128]{3,2,1,0:T(8,128)}), f32[32,2,8,128]{3,2,1,0:T(8,128)S(1)}, u32[]{:S(2)}, u32[]{:S(2)}) async-start(f32[32,2,8,128]{3,2,1,0:T(8,128)} %get-tuple-element.27), calls=%async_computation.6 | async-start | bytes 524288 | tf_op jit(solution)/shard_map/all_to_all | solution.py:465
  169.0 6.0 %copy-start.3 = (f32[32,2,8,128]{3,2,1,0:T(8,128)}, f32[32,2,8,128]{3,2,1,0:T(8,128)S(1)}, u32[]{:S(2)}) copy-start(f32[32,2,8,128]{3,2,1,0:T(8,128)S(1)} %all-to-all-done.6.v_ref) | copy-start | bytes 786436
  169.0 15.2 %all-to-all-start.9 = ((f32[32,8,128]{2,1,0:T(8,128)}), f32[32,8,128]{2,1,0:T(8,128)S(1)}, u32[]{:S(2)}, u32[]{:S(2)}) async-start(f32[32,8,128]{2,1,0:T(8,128)} %shard_map.111), calls=%async_computation.9 | async-start | bytes 262144 | tf_op jit(solution)/shard_map/all_to_all | solution.py:465
  184.1 6.8 %copy-start.4 = (f32[32,8,128]{2,1,0:T(8,128)}, f32[32,8,128]{2,1,0:T(8,128)S(1)}, u32[]{:S(2)}) copy-start(f32[32,8,128]{2,1,0:T(8,128)S(1)} %all-to-all-done.9.m_ref) | copy-start | bytes 393220
  184.1 17.0 %all-to-all-start.7 = ((f32[8,2,72,128]{3,2,1,0:T(8,128)}), f32[8,2,72,128]{3,2,1,0:T(8,128)S(1)}, u32[]{:S(2)}, u32[]{:S(2)}) async-start(f32[8,2,72,128]{3,2,1,0:T(8,128)} %get-tuple-element.28), calls=%async_computation.7 | async-start | bytes 1179648 | tf_op jit(solution)/shard_map/all_to_all | solution.py:464
  201.1 6.9 %copy-start = (f32[8,2,72,128]{3,2,1,0:T(8,128)}, f32[8,2,72,128]{3,2,1,0:T(8,128)S(1)}, u32[]{:S(2)}) copy-start(f32[8,2,72,128]{3,2,1,0:T(8,128)S(1)} %all-to-all-done.7.r_ref) | copy-start | bytes 1769476
  201.1 19.5 %all-to-all-start.10 = ((f32[8,4,32,256]{3,2,1,0:T(8,128)}), f32[8,4,32,256]{3,2,1,0:T(8,128)S(1)}, u32[]{:S(2)}, u32[]{:S(2)}) async-start(f32[8,4,32,256]{3,2,1,0:T(8,128)} %shard_map.112), calls=%async_computation.10 | async-start | bytes 2097152 | tf_op jit(solution)/shard_map/all_to_all | solution.py:464

commit v2 on v1

v2 whole, which is shorter than its diff:
```python
import math

import jax
import jax.numpy as jnp
import ml_dtypes
import numpy as np
from jax import lax
from jax.experimental import pallas as pl
from jax.experimental.pallas import tpu as pltpu
from jax.sharding import PartitionSpec as P

LOW_PASS = [
    0.23037781330885523,
    0.7148465705525415,
    0.6308807679295904,
    -0.02798376941698385,
    -0.18703481171888114,
    0.030841381835986965,
    0.032883011666982945,
    -0.010597401784997278,
]
HIGH_PASS = [(-1) ** position * LOW_PASS[7 - position] for position in range(8)]
GELU_SCALE = 0.7978845608028654
GELU_CUBE = 0.044715


def triple_low():
    taps = np.zeros(50)
    for p, hp in enumerate(LOW_PASS):
        for q, hq in enumerate(LOW_PASS):
            for r, hr in enumerate(LOW_PASS):
                taps[p + 2 * q + 4 * r] += hp * hq * hr
    return [float(t) for t in taps]


TRIPLE = triple_low()
HIGHEST = lax.Precision.HIGHEST
F32 = jnp.float32
BF16 = jnp.bfloat16


def cell_tables():
    table = np.zeros((80, 256))
    for a in range(10):
        for b in range(7):
            for x in range(32):
                for y in range(8):
                    at_x, at_y = x + 48 - 8 * a, y + 48 - 8 * b
                    if 0 <= at_x < 50 and 0 <= at_y < 50:
                        table[a * 7 + b, x * 8 + y] = TRIPLE[at_x] * TRIPLE[at_y]
    table = table.astype(np.float32)
    high = table.astype(ml_dtypes.bfloat16)
    low = (table - high.astype(np.float32)).astype(ml_dtypes.bfloat16)
    down = np.concatenate([high, low])
    pad = np.zeros((256, 16), ml_dtypes.bfloat16)
    up = np.concatenate([high.T, low.T, high.T, pad], 1)
    return down, up


def y_table():
    table = np.zeros((32, 8, 128), np.float32)
    for slab in range(32):
        for b in range(7):
            ky = (slab - 6 + b) % 32
            for mode in range(16):
                at = (ky - 2 * mode) % 32
                if at < 8:
                    table[slab, b, mode] = LOW_PASS[at]
                    table[slab, b, 16 + mode] = HIGH_PASS[at]
    return table.reshape(256, 128)


def gather_sum(pairs):
    total = None
    for weight, value in pairs:
        term = value * weight
        total = term if total is None else total + term
    return total


def swap_blocks(rows):
    lane = lax.broadcasted_iota(jnp.int32, (8, 128), 1)
    rows = list(rows)
    for bit in range(3):
        width = 16 << bit
        upper = (lane & width) != 0
        for lo in range(8):
            if lo & (1 << bit):
                continue
            hi = lo | (1 << bit)
            first, second = rows[lo], rows[hi]
            rows[lo] = jnp.where(upper, pltpu.roll(second, width, 1), first)
            rows[hi] = jnp.where(upper, second, pltpu.roll(first, 128 - width, 1))
    return rows


def split(value):
    high = value.astype(BF16)
    return high, (value - high.astype(F32)).astype(BF16)


def dot(left, right):
    return lax.dot_general(left, right, (((1,), (0,)), ((), ())), preferred_element_type=F32)


def exact_dot(left, right):
    return lax.dot_general(
        left, right, (((1,), (0,)), ((), ())), precision=HIGHEST, preferred_element_type=F32
    )


def side_by_side(values):
    return jnp.concatenate(values, axis=1)


def analyse_pair(field, pair, down_ref, p_scr):
    high, low = split(side_by_side([field[2 * pair], field[2 * pair + 1]]))
    wide = dot(down_ref[...], high)
    total = wide[0:80] + wide[80:160] + dot(down_ref[0:80, :], low)
    p_scr[2 * pair] = total[:, 0:128]
    p_scr[2 * pair + 1] = total[:, 128:256]


def pack_planes(p_scr, s_ref):
    def body(octet, carry):
        at = pl.ds(pl.multiple_of(octet * 8, 8), 8)
        for half in range(2):
            rows = swap_blocks([p_scr[half * 8 + c, at, :] for c in range(8)])
            for group in range(8):
                s_ref[group, half, at, :] = rows[group]
        return carry

    lax.fori_loop(0, 9, body, 0, unroll=True)


def unpack_planes(r_ref, d_scr):
    def body(octet, carry):
        at = pl.ds(pl.multiple_of(octet * 8, 8), 8)
        for half in range(2):
            rows = swap_blocks([r_ref[group, half, at, :] for group in range(8)])
            for c in range(8):
                d_scr[half * 8 + c, at, :] = rows[c]
        return carry

    lax.fori_loop(0, 9, body, 0, unroll=True)
    for c in range(16):
        d_scr[c, 72:80, :] = jnp.zeros((8, 128), F32)


def lift_pair(d_scr, pair, up_ref):
    high, low = split(side_by_side([d_scr[2 * pair], d_scr[2 * pair + 1]]))
    stacked = jnp.concatenate([high, high, low, jnp.zeros((16, 256), BF16)], axis=0)
    return dot(up_ref[...], stacked)


def analyse_kernel(flow_hbm, down_ref, s_ref, f_scr, p_scr, sems):
    copies = [
        pltpu.make_async_copy(flow_hbm.at[pl.ds(4 * k, 4)], f_scr.at[pl.ds(4 * k, 4)], sems.at[k])
        for k in range(4)
    ]
    for copy in copies:
        copy.start()
    for pair in range(8):
        if pair % 2 == 0:
            copies[pair // 2].wait()
        analyse_pair(f_scr, pair, down_ref, p_scr)
    pack_planes(p_scr, s_ref)


def rows_body(r_ref, l_scr, v_ref):
    def collect(q, carry):
        one = (q + 1) % 8
        two = (q + 2) % 8
        for t in range(4):
            for half in range(2):
                total = r_ref[q, half, 7 * (6 + t) : 7 * (6 + t) + 8, :]
                total = total + r_ref[one, half, 7 * (2 + t) : 7 * (2 + t) + 8, :]
                if t >= 2:
                    total = total + r_ref[two, half, 7 * (t - 2) : 7 * (t - 2) + 8, :]
                l_scr[q * 4 + t, half] = total
        return carry

    lax.fori_loop(0, 8, collect, 0)

    def bands(mode, carry):
        for half in range(2):
            parts = [l_scr[(2 * mode + n) % 32, half] for n in range(8)]
            v_ref[mode, half] = gather_sum(list(zip(LOW_PASS, parts)))
            v_ref[mode + 16, half] = gather_sum(list(zip(HIGH_PASS, parts)))
        return carry

    lax.fori_loop(0, 16, bands, 0)


def rows_kernel(r_ref, v_ref, l_scr):
    rows_body(r_ref, l_scr, v_ref)


def rows_grad_kernel(r_ref, v_ref, bias_ref, l_scr):
    rows_body(r_ref, l_scr, v_ref)
    first = r_ref[0, 0, 70:71, :]
    second = r_ref[0, 0, 71:72, :]
    bias = r_ref[0, 1, 70:71, :]
    for i in range(1, 8):
        first = first + r_ref[i, 0, 70:71, :]
        second = second + r_ref[i, 0, 71:72, :]
        bias = bias + r_ref[i, 1, 70:71, :]

    def put(coef, carry):
        v_ref[coef, 0, 7:8, :] = first
        v_ref[coef, 1, 7:8, :] = second
        return carry

    lax.fori_loop(0, 32, put, 0)
    bias_ref[...] = jnp.broadcast_to(bias, (8, 128))


def weights_kernel(index_ref, w_ref, pw_ref, o_ref, forward_ref, back_ref):
    slab = index_ref[0]
    high = slab // 16
    mode = slab % 16
    right = mode // 8
    shift = (8 - mode % 8) * 16
    lane = lax.broadcasted_iota(jnp.int32, (256, 128), 1)
    low_y = jnp.where(right == 0, w_ref[high, :, 0:128], w_ref[high, :, 128:256])
    high_y = jnp.where(right == 0, w_ref[high + 2, :, 0:128], w_ref[high + 2, :, 128:256])
    low_y = pltpu.roll(low_y, shift % 128, 1)
    high_y = pltpu.roll(high_y, (shift + 16) % 128, 1)
    o_ref[...] = jnp.where(lane < 16, low_y, jnp.where(lane < 32, high_y, 0.0))
    same_y = iota(128, 128, 0) % 8 == iota(128, 128, 1) % 8
    rows = (iota(128, 16, 0) // 8 == iota(128, 16, 1)).astype(F32)
    cols = (iota(16, 128, 1) // 8 == iota(16, 128, 0)).astype(F32)
    point = pw_ref[...]
    for ref, matrix in ((forward_ref, point.T), (back_ref, point)):
        wide = jnp.where(same_y, exact_dot(exact_dot(rows, matrix), cols), 0.0)
        upper, lower = split(wide)
        ref[...] = side_by_side([upper, lower, upper])


def iota(rows, cols, axis):
    return lax.broadcasted_iota(jnp.int32, (rows, cols), axis)


def column_bands(v_ref, q_ref, half):
    value = v_ref[:, half].reshape(256, 128)
    return lax.dot_general(
        value.T, q_ref[...], (((1,), (0,)), ((), ())), precision=HIGHEST,
        preferred_element_type=F32,
    )


def column_changes(d_scr, q_ref, o_ref):
    for half in range(2):
        value = lax.dot_general(
            q_ref[...], d_scr[half * 128 : (half + 1) * 128, :], (((1,), (1,)), ((), ())),
            precision=HIGHEST, preferred_element_type=F32,
        )
        o_ref[:, half] = value.reshape(32, 8, 128)


def mix_kernel(v_ref, q_ref, w_ref, o_ref, y_ref, d_scr):
    for half in range(2):
        y_ref[half * 128 : (half + 1) * 128, :] = column_bands(v_ref, q_ref, half)

    def body(o, carry):
        total = -y_ref[pl.ds(pl.multiple_of(o * 16, 16), 16), :]
        for i in range(16):
            total = total + y_ref[i * 16 : (i + 1) * 16, :] * w_ref[pl.ds(i * 16 + o, 1), :]
        d_scr[pl.ds(pl.multiple_of(o * 16, 16), 16), :] = total
        return carry

    lax.fori_loop(0, 16, body, 0)
    column_changes(d_scr, q_ref, o_ref)


def mix_grad_kernel(v_ref, q_ref, w_ref, y_ref, bias_ref, o_ref, g_ref, p_ref, b_scr, d_scr):
    for half in range(2):
        b_scr[half * 128 : (half + 1) * 128, :] = column_bands(v_ref, q_ref, half)

    def body(i, carry):
        flow = y_ref[pl.ds(pl.multiple_of(i * 16, 16), 16), :]
        total = -b_scr[pl.ds(pl.multiple_of(i * 16, 16), 16), :]
        for o in range(16):
            grad = b_scr[o * 16 : (o + 1) * 16, :]
            total = total + grad * w_ref[pl.ds(i * 16 + o, 1), :]
            g_ref[pl.ds(i * 16 + o, 1), :] = jnp.sum(flow * grad, axis=0, keepdims=True)
        d_scr[pl.ds(pl.multiple_of(i * 16, 16), 16), :] = total
        return carry

    lax.fori_loop(0, 16, body, 0)
    column_changes(d_scr, q_ref, o_ref)
    bias = bias_ref[0:1, :]
    first = v_ref[0, 0, 7:8, :]
    second = v_ref[0, 1, 7:8, :]
    for slab in range(32):
        o_ref[slab, 0, 7:8, :] = bias
        if slab > 0:
            first = first + v_ref[slab, 0, 7:8, :]
            second = second + v_ref[slab, 1, 7:8, :]
    p_ref[...] = jnp.zeros((8, 128), F32)
    p_ref[0:1, :] = first
    p_ref[1:2, :] = second


def spread_body(v_ref, l_scr, s_ref):
    def lift(mode, carry):
        for half in range(2):
            low = [v_ref[(mode + 16 - d) % 16, half] for d in range(4)]
            high = [v_ref[16 + (mode + 16 - d) % 16, half] for d in range(4)]
            for p in range(2):
                pairs = [(LOW_PASS[2 * d + p], low[d]) for d in range(4)]
                pairs += [(HIGH_PASS[2 * d + p], high[d]) for d in range(4)]
                l_scr[2 * mode + p, half] = gather_sum(pairs)
        return carry

    lax.fori_loop(0, 16, lift, 0)

    def send(i, carry):
        for half in range(2):
            s_ref[i, half, 64:72, :] = jnp.zeros((8, 128), F32)
            for a in range(10):
                s_ref[i, half, 7 * a : 7 * a + 8, :] = l_scr[(4 * i + 26 + a) % 32, half]
        return carry

    lax.fori_loop(0, 8, send, 0)


def spread_kernel(v_ref, s_ref, l_scr):
    spread_body(v_ref, l_scr, s_ref)


def spread_grad_kernel(v_ref, s_ref, bias_ref, l_scr):
    spread_body(v_ref, l_scr, s_ref)
    bias = v_ref[0, 0, 7:8, :]
    for slab in range(1, 32):
        bias = bias + v_ref[slab, 0, 7:8, :]
    bias_ref[...] = jnp.broadcast_to(bias, (8, 128))


def point_mix(w_ref, first, second):
    high, low = split(side_by_side([first, second]))
    return dot(w_ref[...], jnp.concatenate([high, high, low], axis=0)), high, low


def centre_kernel(
    r_ref, flow_hbm, cot_hbm, w_ref, bias_ref, down_ref, up_ref, out_hbm, g_hbm, s_ref,
    f_scr, c_scr, v_scr, g_scr, d_scr, p_scr, sum_scr, pt_scr, sems,
):
    load_flow = pltpu.make_async_copy(flow_hbm, f_scr, sems.at[0])
    load_cot = pltpu.make_async_copy(cot_hbm, c_scr, sems.at[1])
    load_flow.start()
    load_cot.start()
    unpack_planes(r_ref, d_scr)
    sum_scr[...] = jnp.zeros((128, 128), F32)
    pt_scr[...] = jnp.zeros((128, 128), F32)
    load_flow.wait()
    for pair in range(8):
        change = lift_pair(d_scr, pair, up_ref)
        for k in range(2):
            c = 2 * pair + k
            v_scr[c] = f_scr[c] + (change[:, 128 * k : 128 * k + 128] + bias_ref[c])
    load_cot.wait()
    stores = []
    for chunk in range(4):

        def body(step, carry):
            start = pl.multiple_of((chunk * 4 + step) * 16, 16)
            spans = [pl.ds(start, 8), pl.ds(pl.multiple_of(start + 8, 8), 8)]
            fields = [f_scr[:, span, :].reshape(128, 128) for span in spans]
            mixed, f_high, f_low = point_mix(w_ref, fields[0], fields[1])
            grads = []
            for k in range(2):
                value = v_scr[:, spans[k], :].reshape(128, 128) + mixed[:, 128 * k : 128 * k + 128]
                square = value * value
                tangent = jnp.tanh(value * (GELU_SCALE + (GELU_SCALE * GELU_CUBE) * square))
                half_up = 0.5 + 0.5 * tangent
                v_scr[:, spans[k], :] = (value * half_up).reshape(16, 8, 128)
                bend = value * ((0.5 * GELU_SCALE) + (1.5 * GELU_SCALE * GELU_CUBE) * square)
                slope = half_up + bend * (1.0 - tangent * tangent)
                grad = c_scr[:, spans[k], :].reshape(128, 128) * slope
                g_scr[:, spans[k], :] = grad.reshape(16, 8, 128)
                grads.append(grad)
            sum_scr[...] += grads[0] + grads[1]
            g_high, g_low = split(side_by_side(grads))
            pt_scr[...] += lax.dot_general(
                side_by_side([f_high, f_low, f_high]), side_by_side([g_high, g_high, g_low]),
                (((1,), (1,)), ((), ())), preferred_element_type=F32,
            )
            return carry

        lax.fori_loop(0, 4, body, 0, unroll=True)
        part = pl.ds(chunk * 64, 64)
        for k, (scr, hbm) in enumerate(((v_scr, out_hbm), (g_scr, g_hbm))):
            store = pltpu.make_async_copy(
                scr.at[:, part], hbm.at[:, part], sems.at[2 + 2 * chunk + k]
            )
            store.start()
            stores.append(store)
    for pair in range(8):
        analyse_pair(g_scr, pair, down_ref, p_scr)
    pack_planes(p_scr, s_ref)
    same_y = iota(128, 128, 0) % 8 == iota(128, 128, 1) % 8
    gather = (iota(16, 128, 1) // 8 == iota(16, 128, 0)).astype(F32)
    fold = (iota(128, 128, 0) // 8 == iota(128, 128, 1) % 16).astype(F32)
    wide = exact_dot(exact_dot(gather, jnp.where(same_y, pt_scr[...], 0.0)), fold)
    lane, row = iota(16, 128, 1), iota(16, 128, 0)
    wide = jnp.where(lane // 16 == row % 8, wide, 0.0)
    first = jnp.sum(wide[0:8], axis=0, keepdims=True)
    second = jnp.sum(wide[8:16], axis=0, keepdims=True)
    totals = jnp.sum(exact_dot(gather, sum_scr[...]), axis=1, keepdims=True)
    bias_row = jnp.sum(jnp.where(lane == row, totals, 0.0), axis=0, keepdims=True)
    for group in range(8):
        s_ref[group, 0, 70:71, :] = first
        s_ref[group, 0, 71:72, :] = second
        s_ref[group, 1, 70:71, :] = bias_row
    for store in stores:
        store.wait()


def finish_kernel(r_ref, g_hbm, w_ref, up_ref, out_hbm, g_scr, v_scr, d_scr, sems):
    load = pltpu.make_async_copy(g_hbm, g_scr, sems.at[0])
    load.start()
    unpack_planes(r_ref, d_scr)
    load.wait()
    for pair in range(8):
        change = lift_pair(d_scr, pair, up_ref)
        for k in range(2):
            v_scr[2 * pair + k] = g_scr[2 * pair + k] + change[:, 128 * k : 128 * k + 128]
    stores = []
    for chunk in range(4):

        def body(step, carry):
            start = pl.multiple_of((chunk * 4 + step) * 16, 16)
            spans = [pl.ds(start, 8), pl.ds(pl.multiple_of(start + 8, 8), 8)]
            fields = [g_scr[:, span, :].reshape(128, 128) for span in spans]
            mixed = point_mix(w_ref, fields[0], fields[1])[0]
            for k in range(2):
                value = v_scr[:, spans[k], :].reshape(128, 128) + mixed[:, 128 * k : 128 * k + 128]
                v_scr[:, spans[k], :] = value.reshape(16, 8, 128)
            return carry

        lax.fori_loop(0, 4, body, 0, unroll=True)
        part = pl.ds(chunk * 64, 64)
        store = pltpu.make_async_copy(v_scr.at[:, part], out_hbm.at[:, part], sems.at[1 + chunk])
        store.start()
        stores.append(store)
    for store in stores:
        store.wait()


def modes_sum_kernel(g_ref, o_ref):
    total = g_ref[0]
    for i in range(1, 8):
        total = total + g_ref[i]
    lane = lax.broadcasted_iota(jnp.int32, (8, 128), 1)
    packed = jnp.zeros((8, 128), F32)
    for k in range(4):
        rows = total[k * 8 : (k + 1) * 8, :]
        if k > 0:
            rows = pltpu.roll(rows, 32 * k, 1)
        packed = jnp.where(lane // 32 == k, rows, packed)

    def put(slab, carry):
        o_ref[slab] = packed
        return carry

    lax.fori_loop(0, 32, put, 0)


def modes_place_kernel(m_ref, o_ref):
    for high in range(2):
        for right in range(2):
            rows = [m_ref[high * 16 + right * 8 + m] for m in range(8)]
            rows = swap_blocks(rows)
            for k in range(4):
                for up in range(2):
                    for copy in range(8):
                        o_ref[
                            copy, high + 2 * up, k * 8 : (k + 1) * 8,
                            right * 128 : (right + 1) * 128,
                        ] = rows[2 * k + up]


def call(kernel, ins, outs, scratch=(), sems=0, mib=8):
    spaces = {"v": pltpu.VMEM, "s": pltpu.SMEM, "a": pltpu.HBM}
    structs = [jax.ShapeDtypeStruct(o[0], o[2] if len(o) > 2 else F32) for o in outs]
    scratches = [pltpu.VMEM(shape, F32) for shape in scratch]
    if sems:
        scratches.append(pltpu.SemaphoreType.DMA((sems,)))
    return pl.pallas_call(
        kernel,
        out_shape=structs,
        in_specs=[pl.BlockSpec(memory_space=spaces[k]) for k in ins],
        out_specs=[pl.BlockSpec(memory_space=spaces[o[1]]) for o in outs],
        scratch_shapes=scratches,
        compiler_params=pltpu.CompilerParams(vmem_limit_bytes=mib * 1024 * 1024),
    )


def local(flow_field, cotangent, mode_weights, point_weights, point_bias):
    swap_x = lambda v: lax.all_to_all(v, "gx", 0, 0, tiled=False)
    swap_y = lambda v: lax.all_to_all(v, "gy", 0, 0, tiled=False)
    packed = ((8, 2, 72, 128), "v")
    coefs = ((32, 2, 8, 128), "v")
    square = ((256, 128), "v")
    row = ((8, 128), "v")
    cells = (16, 256, 128)
    parts = (16, 80, 128)
    rows3 = [(32, 2, 8, 128)]
    table = jnp.asarray(y_table())
    down, up = (jnp.asarray(t) for t in cell_tables())
    slab = lax.axis_index("gy").astype(jnp.int32).reshape(1)
    flow_cells = flow_field.reshape(cells)
    kron = ((128, 384), "v", BF16)

    weights, mix_forward, mix_back = call(weights_kernel, "svv", [square, kron, kron])(
        slab, mode_weights.reshape(4, 256, 256), point_weights
    )
    (sent,) = call(analyse_kernel, "av", [packed], [cells, parts], 4, 58)(flow_cells, down)
    (got,) = call(rows_kernel, "v", [coefs], rows3)(swap_x(sent))
    back, bands_flow = call(mix_kernel, "vvv", [coefs, square], [(256, 128)])(
        swap_y(got), table, weights
    )
    (spread,) = call(spread_kernel, "v", [packed], rows3)(swap_y(back))
    output_field, grads, sent = call(
        centre_kernel, "vaavsvv", [(cells, "a"), (cells, "a"), packed],
        [cells] * 4 + [parts] * 2 + [(128, 128)] * 2, 10, 58,
    )(
        swap_x(spread), flow_cells, cotangent.reshape(cells), mix_forward, point_bias, down, up
    )
    got, bias_part = call(rows_grad_kernel, "v", [coefs, row], rows3)(swap_x(sent))
    back, mode_part, point_total = call(
        mix_grad_kernel, "vvvvv", [coefs, square, row], [(256, 128)] * 2
    )(swap_y(got), table, weights, bands_flow, bias_part)
    spread, bias_total = call(spread_grad_kernel, "v", [packed, row], rows3)(swap_y(back))
    (grad_field,) = call(
        finish_kernel, "vavv", [(cells, "a")], [cells] * 2 + [parts], 5, 58
    )(swap_x(spread), grads, mix_back, up)
    (part,) = call(modes_sum_kernel, "v", [((32, 8, 128), "v")])(
        swap_x(mode_part.reshape(8, 32, 128))
    )
    (placed,) = call(modes_place_kernel, "v", [((8, 4, 32, 256), "v")])(swap_y(part))
    modes = jnp.transpose(swap_x(placed), (1, 0, 2, 3)).reshape(4, 16, 16, 256)

    planes = flow_field.shape[3]
    cell_count = planes * 256 * 256
    return (
        output_field.reshape(flow_field.shape),
        grad_field.reshape(flow_field.shape),
        modes / math.sqrt(planes),
        point_total[0:2].reshape(16, 16) / math.sqrt(cell_count),
        bias_total[0, :16] / math.sqrt(cell_count),
    )


def solution(mesh):
    in_specs = (P(None, "gx", "gy", None), P(None, "gx", "gy", None), P(), P(), P())
    out_specs = (P(None, "gx", "gy", None), P(None, "gx", "gy", None), P(), P(), P())
    return jax.shard_map(local, mesh=mesh, in_specs=in_specs, out_specs=out_specs, check_vma=False)
```

time: 223 us -> 197 us (0.88)
  Pallas kernels: 57.8 us -> 28.7 us
  blocking collectives: 76.1 us -> 89.3 us
  starting transfers between devices: 38.1 us -> 31.6 us
    pallas_call x12, Pallas kernels: 57.8 us -> 28.7 us  [the longest x1 8.17 us: local(): call(centre_kernel, 'vaavsvv', [(cells, 'a'), (cells, 'a'), packed], [cel...]
    all_to_all x3 -> x4, blocking collectives: 46 us -> 60.2 us  [local(): swap_x = lambda v: lax.all_to_all(v, 'gx', 0, 0, tiled=False)]
    all_to_all x3 -> x2, starting transfers between devices: 18.2 us -> 11.1 us  [local(): swap_x = lambda v: lax.all_to_all(v, 'gx', 0, 0, tiled=False)]
    all_to_all x3 -> x2, waiting for transfers between devices: 20.8 us -> 18 us  [local(): swap_x = lambda v: lax.all_to_all(v, 'gx', 0, 0, tiled=False)]
  transfers between devices with their start and end apart: 6 -> 5, of which waited for: 6 -> 5; matrix products, arithmetic and copies ran while one was open for 1% -> 1% of each run, Pallas kernels for 8% -> 5%
where the time goes in v2:
time: 197 us; the launch traced here: 196 us
  blocking collectives  89.3 us (45%)
  waiting for transfers between devices  42.1 us (21%)
  starting transfers between devices  31.6 us (16%)
  Pallas kernels  28.7 us (15%)
  local copies, waits for them, and re-layouts  3.05 us (2%)
    all_to_all x4, blocking collectives, local(): swap_x = lambda v: lax.all_to_all(v, 'gx', 0, 0, tiled=False)  60.2 us
    all_to_all x2, blocking collectives, local(): swap_y = lambda v: lax.all_to_all(v, 'gy', 0, 0, tiled=False)  29.2 us
    all_to_all x3, waiting for transfers between devices, local(): swap_y = lambda v: lax.all_to_all(v, 'gy', 0, 0, tiled=False)  24.2 us
    all_to_all x3, starting transfers between devices, local(): swap_y = lambda v: lax.all_to_all(v, 'gy', 0, 0, tiled=False)  20.5 us
    all_to_all x2, waiting for transfers between devices, local(): swap_x = lambda v: lax.all_to_all(v, 'gx', 0, 0, tiled=False)  18 us
    all_to_all x2, starting transfers between devices, local(): swap_x = lambda v: lax.all_to_all(v, 'gx', 0, 0, tiled=False)  11.1 us
    pallas_call x1, Pallas kernels, local(): call(centre_kernel, 'vaavsvv', [(cells, 'a'), (cells, 'a'), packed], [cel...  8.17 us
    pallas_call x1, Pallas kernels, local(): call(analyse_kernel, 'av', [packed], [cells, parts], 4, 58)  5.32 us
  transfers between devices with their start and end apart: 5, of which 5 were waited for; matrix products, arithmetic and copies ran while one was open for 1% of the time, Pallas kernels for 5%

profile of v2, /device:TPU:1, one launch (start us, length us, event | category | flops | bytes accessed | tf_op | source)
XLA Modules:
  0.0 196.2 jit_solution(6949676450247525910)
XLA Ops:
  0.7 5.3 %shard_map.119 = f32[8,2,72,128]{3,2,1,0:T(8,128)} custom-call(f32[16,256,128]{2,1,0:T(8,128)} %bitcast.14, bf16[160,256]{1,0:T(8,128)(2,1)} %constant.19.clone.down_ref), custom_call_target="tpu_custom_call" | custom-call | tf_op jit(solution)/shard_map/pallas_call | solution.py:519
  6.0 17.2 %all_to_all.55.r_ref = f32[8,2,72,128]{3,2,1,0:T(8,128)S(1)} all-to-all(f32[8,2,72,128]{3,2,1,0:T(8,128)} %shard_map.119), channel_id=1, replica_groups=mesh['gx'=8,'gy'=32] {'gx'}, dimensions={0} | all-to-all | bytes 1179648 | tf_op jit(solution)/shard_map/all_to_all | solution.py:501
  23.2 1.3 shard_map.120
  24.5 10.3 %all-to-all-start.1 = ((f32[32,2,8,128]{3,2,1,0:T(8,128)}), f32[32,2,8,128]{3,2,1,0:T(8,128)S(1)}, u32[]{:S(2)}, u32[]{:S(2)}) async-start(f32[32,2,8,128]{3,2,1,0:T(8,128)} %shard_map.120), calls=%async_computation.1 | async-start | bytes 524288 | tf_op jit(solution)/shard_map/all_to_all | solution.py:502
  36.8 7.6 %all-to-all-done.1.v_ref = f32[32,2,8,128]{3,2,1,0:T(8,128)S(1)} async-done(((f32[32,2,8,128]{3,2,1,0:T(8,128)}), f32[32,2,8,128]{3,2,1,0:T(8,128)S(1)}, u32[]{:S(2)}, u32[]{:S(2)}) %all-to-all-start.1) | async-done | bytes 262176 | tf_op jit(solution)/shard_map/all_to_all | solution.py:502
  44.5 1.2 shard_map.122
  45.7 15.5 %all_to_all.56.v_ref = f32[32,2,8,128]{3,2,1,0:T(8,128)S(1)} all-to-all(f32[32,2,8,128]{3,2,1,0:T(8,128)S(1)} %get-tuple-element.21), channel_id=1, replica_groups=mesh['gx'=8,'gy'=32] {'gy'}, dimensions={0} | all-to-all | bytes 524288 | tf_op jit(solution)/shard_map/all_to_all | solution.py:502
  61.9 17.1 %all_to_all.57.r_ref = f32[8,2,72,128]{3,2,1,0:T(8,128)} all-to-all(f32[8,2,72,128]{3,2,1,0:T(8,128)S(1)} %shard_map.123), channel_id=1, replica_groups=mesh['gx'=8,'gy'=32] {'gx'}, dimensions={0} | all-to-all | bytes 1179648 | tf_op jit(solution)/shard_map/all_to_all | solution.py:501
  79.0 8.2 %shard_map.124 = (f32[16,256,128]{2,1,0:T(8,128)}, f32[16,256,128]{2,1,0:T(8,128)}, f32[8,2,72,128]{3,2,1,0:T(8,128)}) custom-call(f32[8,2,72,128]{3,2,1,0:T(8,128)} %all_to_all.57.r_ref, f32[16,256,128]{2,1,0:T(8,128)} %bitcast.15, f32[16,256,128]{2,1,0:T(8,128)} %bitcast.17, bf16[128,384]{1,0:T(8,128)(2,1)} %copy-done.3, f32[16]{0:T(128)} %bias_ref.1, ...), custom_call_target="tpu_custom_call" | custom-call | tf_op jit(solution)/shard_map/pallas_call | solution.py:525
  87.1 14.5 %all_to_all.58.r_ref = f32[8,2,72,128]{3,2,1,0:T(8,128)S(1)} all-to-all(f32[8,2,72,128]{3,2,1,0:T(8,128)} %get-tuple-element.24), channel_id=1, replica_groups=mesh['gx'=8,'gy'=32] {'gx'}, dimensions={0} | all-to-all | bytes 1179648 | tf_op jit(solution)/shard_map/all_to_all | solution.py:501
  102.5 13.6 %all_to_all.59.v_ref = f32[32,2,8,128]{3,2,1,0:T(8,128)S(1)} all-to-all(f32[32,2,8,128]{3,2,1,0:T(8,128)S(1)} %get-tuple-element.25), channel_id=1, replica_groups=mesh['gx'=8,'gy'=32] {'gy'}, dimensions={0} | all-to-all | bytes 524288 | tf_op jit(solution)/shard_map/all_to_all | solution.py:502
  116.1 2.1 %shard_map.126 = (f32[32,2,8,128]{3,2,1,0:T(8,128)}, f32[256,128]{1,0:T(8,128)S(1)}, f32[8,128]{1,0:T(8,128)S(1)}) custom-call(f32[32,2,8,128]{3,2,1,0:T(8,128)S(1)} %all_to_all.59.v_ref, f32[256,128]{1,0:T(8,128)S(1)} %copy-done.1, f32[256,128]{1,0:T(8,128)S(1)} %get-tuple-element.20.w_ref, f32[256,128]{1,0:T(8,128)S(1)} %get-tuple-element.26.y_ref, ...), custom_call_target="tpu_custom_call" | custom-call | tf_op jit(solution)/shard_map/pallas_call | solution.py:532
  118.2 11.3 %all_to_all.60.g_ref = f32[8,32,128]{2,1,0:T(8,128)S(1)} all-to-all(f32[8,32,128]{2,1,0:T(8,128)S(1)} %bitcast.13), channel_id=1, replica_groups=mesh['gx'=8,'gy'=32] {'gx'}, dimensions={0} | all-to-all | bytes 262144 | tf_op jit(solution)/shard_map/all_to_all | solution.py:501
  129.5 4.2 %all-to-all-start.6 = ((f32[32,2,8,128]{3,2,1,0:T(8,128)}), f32[32,2,8,128]{3,2,1,0:T(8,128)S(1)}, u32[]{:S(2)}, u32[]{:S(2)}) async-start(f32[32,2,8,128]{3,2,1,0:T(8,128)} %get-tuple-element.28), calls=%async_computation.6 | async-start | bytes 524288 | tf_op jit(solution)/shard_map/all_to_all | solution.py:502
  134.5 8.9 %all-to-all-done.6.v_ref = f32[32,2,8,128]{3,2,1,0:T(8,128)S(1)} async-done(((f32[32,2,8,128]{3,2,1,0:T(8,128)}), f32[32,2,8,128]{3,2,1,0:T(8,128)S(1)}, u32[]{:S(2)}, u32[]{:S(2)}) %all-to-all-start.6) | async-done | bytes 262176 | tf_op jit(solution)/shard_map/all_to_all | solution.py:502
  143.4 6.0 %all-to-all-start.9 = ((f32[32,8,128]{2,1,0:T(8,128)}), f32[32,8,128]{2,1,0:T(8,128)S(1)}, u32[]{:S(2)}, u32[]{:S(2)}) async-start(f32[32,8,128]{2,1,0:T(8,128)} %shard_map.129), calls=%async_computation.9 | async-start | bytes 262144 | tf_op jit(solution)/shard_map/all_to_all | solution.py:502
  149.4 1.5 shard_map.127
  150.9 7.7 %all-to-all-done.9.m_ref = f32[32,8,128]{2,1,0:T(8,128)S(1)} async-done(((f32[32,8,128]{2,1,0:T(8,128)}), f32[32,8,128]{2,1,0:T(8,128)S(1)}, u32[]{:S(2)}, u32[]{:S(2)}) %all-to-all-start.9) | async-done | bytes 131104 | tf_op jit(solution)/shard_map/all_to_all | solution.py:502
  158.6 6.7 %all-to-all-start.7 = ((f32[8,2,72,128]{3,2,1,0:T(8,128)}), f32[8,2,72,128]{3,2,1,0:T(8,128)S(1)}, u32[]{:S(2)}, u32[]{:S(2)}) async-start(f32[8,2,72,128]{3,2,1,0:T(8,128)} %get-tuple-element.29), calls=%async_computation.7 | async-start | bytes 1179648 | tf_op jit(solution)/shard_map/all_to_all | solution.py:501
  165.3 1.3 shard_map.130
  166.6 8.9 %all-to-all-done.7.r_ref = f32[8,2,72,128]{3,2,1,0:T(8,128)S(1)} async-done(((f32[8,2,72,128]{3,2,1,0:T(8,128)}), f32[8,2,72,128]{3,2,1,0:T(8,128)S(1)}, u32[]{:S(2)}, u32[]{:S(2)}) %all-to-all-start.7) | async-done | bytes 589856 | tf_op jit(solution)/shard_map/all_to_all | solution.py:501
  175.5 4.3 %all-to-all-start.10 = ((f32[8,4,32,256]{3,2,1,0:T(8,128)}), f32[8,4,32,256]{3,2,1,0:T(8,128)S(1)}, u32[]{:S(2)}, u32[]{:S(2)}) async-start(f32[8,4,32,256]{3,2,1,0:T(8,128)} %shard_map.130), calls=%async_computation.10 | async-start | bytes 2097152 | tf_op jit(solution)/shard_map/all_to_all | solution.py:501
  181.0 4.9 %shard_map.128 = f32[16,256,128]{2,1,0:T(8,128)} custom-call(f32[8,2,72,128]{3,2,1,0:T(8,128)} %copy-done.5, f32[16,256,128]{2,1,0:T(8,128)} %get-tuple-element.30.g_hbm, bf16[128,384]{1,0:T(8,128)(2,1)} %copy-done.2, bf16[256,256]{1,0:T(8,128)(2,1)} %constant.20.clone.up_ref), custom_call_target="tpu_custom_call" | custom-call | tf_op jit(solution)/shard_map/pallas_call | solution.py:536
  185.9 9.0 %all-to-all-done.10 = f32[8,4,32,256]{3,2,1,0:T(8,128)S(1)} async-done(((f32[8,4,32,256]{3,2,1,0:T(8,128)}), f32[8,4,32,256]{3,2,1,0:T(8,128)S(1)}, u32[]{:S(2)}, u32[]{:S(2)}) %all-to-all-start.10) | async-done | bytes 1048608 | tf_op jit(solution)/shard_map/all_to_all | solution.py:501
  (21 shorter events, 6.7 us)
Async XLA Ops:
  0.6 34.2 %copy-start = (f32[4,16,16,256]{3,2,1,0:T(8,128)S(1)}, f32[4,16,16,256]{3,2,1,0:T(8,128)}, u32[]{:S(2)}) copy-start(f32[4,16,16,256]{3,2,1,0:T(8,128)} %param.10) | copy-start | bytes 3145732
  0.6 34.2 %copy-start.4 = (f32[16,16]{1,0:T(8,128)S(1)}, f32[16,16]{1,0:T(8,128)}, u32[]{:S(2)}) copy-start(f32[16,16]{1,0:T(8,128)} %pw_ref.1) | copy-start | bytes 3076
  6.0 38.5 %copy-start.1 = (f32[256,128]{1,0:T(8,128)S(1)}, f32[256,128]{1,0:T(8,128)}, u32[]{:S(2)}) copy-start(f32[256,128]{1,0:T(8,128)} %constant.18.clone.q_ref) | copy-start | bytes 393220
  24.5 20.0 %all-to-all-start.1 = ((f32[32,2,8,128]{3,2,1,0:T(8,128)}), f32[32,2,8,128]{3,2,1,0:T(8,128)S(1)}, u32[]{:S(2)}, u32[]{:S(2)}) async-start(f32[32,2,8,128]{3,2,1,0:T(8,128)} %shard_map.120), calls=%async_computation.1 | async-start | bytes 524288 | tf_op jit(solution)/shard_map/all_to_all | solution.py:502
  35.6 0.6 copy-start.2
  36.2 0.6 copy-start.3
  129.5 13.9 %all-to-all-start.6 = ((f32[32,2,8,128]{3,2,1,0:T(8,128)}), f32[32,2,8,128]{3,2,1,0:T(8,128)S(1)}, u32[]{:S(2)}, u32[]{:S(2)}) async-start(f32[32,2,8,128]{3,2,1,0:T(8,128)} %get-tuple-element.28), calls=%async_computation.6 | async-start | bytes 524288 | tf_op jit(solution)/shard_map/all_to_all | solution.py:502
  143.4 15.2 %all-to-all-start.9 = ((f32[32,8,128]{2,1,0:T(8,128)}), f32[32,8,128]{2,1,0:T(8,128)S(1)}, u32[]{:S(2)}, u32[]{:S(2)}) async-start(f32[32,8,128]{2,1,0:T(8,128)} %shard_map.129), calls=%async_computation.9 | async-start | bytes 262144 | tf_op jit(solution)/shard_map/all_to_all | solution.py:502
  158.6 17.0 %all-to-all-start.7 = ((f32[8,2,72,128]{3,2,1,0:T(8,128)}), f32[8,2,72,128]{3,2,1,0:T(8,128)S(1)}, u32[]{:S(2)}, u32[]{:S(2)}) async-start(f32[8,2,72,128]{3,2,1,0:T(8,128)} %get-tuple-element.29), calls=%async_computation.7 | async-start | bytes 1179648 | tf_op jit(solution)/shard_map/all_to_all | solution.py:501
  175.5 5.5 %copy-start.5 = (f32[8,2,72,128]{3,2,1,0:T(8,128)}, f32[8,2,72,128]{3,2,1,0:T(8,128)S(1)}, u32[]{:S(2)}) copy-start(f32[8,2,72,128]{3,2,1,0:T(8,128)S(1)} %all-to-all-done.7.r_ref) | copy-start | bytes 1769476
  175.5 19.5 %all-to-all-start.10 = ((f32[8,4,32,256]{3,2,1,0:T(8,128)}), f32[8,4,32,256]{3,2,1,0:T(8,128)S(1)}, u32[]{:S(2)}, u32[]{:S(2)}) async-start(f32[8,4,32,256]{3,2,1,0:T(8,128)} %shard_map.130), calls=%async_computation.10 | async-start | bytes 2097152 | tf_op jit(solution)/shard_map/all_to_all | solution.py:501

commit v3 on v2

--- a/solution.py
+++ b/solution.py
@@ -273,33 +273,57 @@
     column_changes(d_scr, q_ref, o_ref)
 
 
-def mix_grad_kernel(v_ref, q_ref, w_ref, y_ref, bias_ref, o_ref, g_ref, p_ref, b_scr, d_scr):
+def grad_bands_kernel(v_ref, q_ref, y_ref, b_ref, g_ref, p_ref, g_scr):
     for half in range(2):
-        b_scr[half * 128 : (half + 1) * 128, :] = column_bands(v_ref, q_ref, half)
+        b_ref[half * 128 : (half + 1) * 128, :] = column_bands(v_ref, q_ref, half)
 
     def body(i, carry):
         flow = y_ref[pl.ds(pl.multiple_of(i * 16, 16), 16), :]
-        total = -b_scr[pl.ds(pl.multiple_of(i * 16, 16), 16), :]
         for o in range(16):
-            grad = b_scr[o * 16 : (o + 1) * 16, :]
-            total = total + grad * w_ref[pl.ds(i * 16 + o, 1), :]
-            g_ref[pl.ds(i * 16 + o, 1), :] = jnp.sum(flow * grad, axis=0, keepdims=True)
-        d_scr[pl.ds(pl.multiple_of(i * 16, 16), 16), :] = total
+            grad = b_ref[o * 16 : (o + 1) * 16, :]
+            g_scr[pl.ds(i * 16 + o, 1), :] = jnp.sum(flow * grad, axis=0, keepdims=True)
         return carry
 
     lax.fori_loop(0, 16, body, 0)
-    column_changes(d_scr, q_ref, o_ref)
-    bias = bias_ref[0:1, :]
+    lane = lax.broadcasted_iota(jnp.int32, (8, 128), 1)
+    for group in range(8):
+        packed = g_scr[group * 32 : group * 32 + 8, :]
+        for k in range(1, 4):
+            rows = g_scr[group * 32 + k * 8 : group * 32 + k * 8 + 8, :]
+            packed = jnp.where(lane // 32 == k, pltpu.roll(rows, 32 * k, 1), packed)
+        g_ref[group] = packed
     first = v_ref[0, 0, 7:8, :]
     second = v_ref[0, 1, 7:8, :]
-    for slab in range(32):
-        o_ref[slab, 0, 7:8, :] = bias
-        if slab > 0:
-            first = first + v_ref[slab, 0, 7:8, :]
-            second = second + v_ref[slab, 1, 7:8, :]
+    for slab in range(1, 32):
+        first = first + v_ref[slab, 0, 7:8, :]
+        second = second + v_ref[slab, 1, 7:8, :]
     p_ref[...] = jnp.zeros((8, 128), F32)
     p_ref[0:1, :] = first
     p_ref[1:2, :] = second
+
+
+def mix_grad_kernel(b_ref, q_ref, w_ref, bias_ref, o_ref, d_scr):
+    def body(i, carry):
+        total = -b_ref[pl.ds(pl.multiple_of(i * 16, 16), 16), :]
+        for o in range(16):
+            total = total + b_ref[o * 16 : (o + 1) * 16, :] * w_ref[pl.ds(i * 16 + o, 1), :]
+        d_scr[pl.ds(pl.multiple_of(i * 16, 16), 16), :] = total
+        return carry
+
+    lax.fori_loop(0, 16, body, 0)
+    column_changes(d_scr, q_ref, o_ref)
+    for slab in range(32):
+        o_ref[slab, 0, 7:8, :] = bias_ref[0:1, :]
+
+
+def join_kernel(v_ref, g_ref, o_ref):
+    total = g_ref[0]
+    for i in range(1, 8):
+        total = total + g_ref[i]
+    total = total * (1.0 / math.sqrt(128.0))
+    for slab in range(32):
+        o_ref[slab, 0:2] = v_ref[slab]
+        o_ref[slab, 2] = total
 
 
 def spread_body(v_ref, l_scr, s_ref):
@@ -448,29 +472,10 @@
         store.wait()
 
 
-def modes_sum_kernel(g_ref, o_ref):
-    total = g_ref[0]
-    for i in range(1, 8):
-        total = total + g_ref[i]
-    lane = lax.broadcasted_iota(jnp.int32, (8, 128), 1)
-    packed = jnp.zeros((8, 128), F32)
-    for k in range(4):
-        rows = total[k * 8 : (k + 1) * 8, :]
-        if k > 0:
-            rows = pltpu.roll(rows, 32 * k, 1)
-        packed = jnp.where(lane // 32 == k, rows, packed)
-
-    def put(slab, carry):
-        o_ref[slab] = packed
-        return carry
-
-    lax.fori_loop(0, 32, put, 0)
-
-
 def modes_place_kernel(m_ref, o_ref):
     for high in range(2):
         for right in range(2):
-            rows = [m_ref[high * 16 + right * 8 + m] for m in range(8)]
+            rows = [m_ref[high * 16 + right * 8 + m, 2] for m in range(8)]
             rows = swap_blocks(rows)
             for k in range(4):
                 for up in range(2):
@@ -529,25 +534,26 @@
         swap_x(spread), flow_cells, cotangent.reshape(cells), mix_forward, point_bias, down, up
     )
     got, bias_part = call(rows_grad_kernel, "v", [coefs, row], rows3)(swap_x(sent))
-    back, mode_part, point_total = call(
-        mix_grad_kernel, "vvvvv", [coefs, square, row], [(256, 128)] * 2
-    )(swap_y(got), table, weights, bands_flow, bias_part)
-    spread, bias_total = call(spread_grad_kernel, "v", [packed, row], rows3)(swap_y(back))
+    bands_grad, mode_part, point_total = call(
+        grad_bands_kernel, "vvv", [square, ((8, 8, 128), "v"), row], [(256, 128)]
+    )(swap_y(got), table, bands_flow)
+    (back,) = call(mix_grad_kernel, "vvvv", [coefs], [(256, 128)])(
+        bands_grad, table, weights, bias_part
+    )
+    (joined,) = call(join_kernel, "vv", [((32, 3, 8, 128), "v")])(back, swap_x(mode_part))
+    joined = swap_y(joined)
+    spread, bias_total = call(spread_grad_kernel, "v", [packed, row], rows3)(joined)
     (grad_field,) = call(
         finish_kernel, "vavv", [(cells, "a")], [cells] * 2 + [parts], 5, 58
     )(swap_x(spread), grads, mix_back, up)
-    (part,) = call(modes_sum_kernel, "v", [((32, 8, 128), "v")])(
-        swap_x(mode_part.reshape(8, 32, 128))
-    )
-    (placed,) = call(modes_place_kernel, "v", [((8, 4, 32, 256), "v")])(swap_y(part))
+    (placed,) = call(modes_place_kernel, "v", [((8, 4, 32, 256), "v")])(joined)
     modes = jnp.transpose(swap_x(placed), (1, 0, 2, 3)).reshape(4, 16, 16, 256)
 
-    planes = flow_field.shape[3]
-    cell_count = planes * 256 * 256
+    cell_count = flow_field.shape[3] * 256 * 256
     return (
         output_field.reshape(flow_field.shape),
         grad_field.reshape(flow_field.shape),
-        modes / math.sqrt(planes),
+        modes,
         point_total[0:2].reshape(16, 16) / math.sqrt(cell_count),
         bias_total[0, :16] / math.sqrt(cell_count),
     )

time: 197 us -> 185 us (0.939)
  waiting for transfers between devices: 42.1 us -> 29.6 us
  blocking collectives: 89.3 us -> 93.4 us
  starting transfers between devices: 31.6 us -> 29.2 us
    all_to_all x3 -> x1, waiting for transfers between devices: 24.2 us -> 7.63 us  [local(): swap_y = lambda v: lax.all_to_all(v, 'gy', 0, 0, tiled=False)]
    all_to_all x2 -> x3, blocking collectives: 29.2 us -> 44.5 us  [local(): swap_y = lambda v: lax.all_to_all(v, 'gy', 0, 0, tiled=False)]
    all_to_all x4 -> x3, blocking collectives: 60.2 us -> 48.8 us  [local(): swap_x = lambda v: lax.all_to_all(v, 'gx', 0, 0, tiled=False)]
    all_to_all x3 -> x1, starting transfers between devices: 20.5 us -> 10.3 us  [local(): swap_y = lambda v: lax.all_to_all(v, 'gy', 0, 0, tiled=False)]
    all_to_all x2 -> x3, starting transfers between devices: 11.1 us -> 18.8 us  [local(): swap_x = lambda v: lax.all_to_all(v, 'gx', 0, 0, tiled=False)]
    all_to_all x2 -> x3, waiting for transfers between devices: 18 us -> 22 us  [local(): swap_x = lambda v: lax.all_to_all(v, 'gx', 0, 0, tiled=False)]
    pallas_call x4 -> x5, Pallas kernels: 5.66 us -> 5.02 us  [the longest x1 1.53 us: local(): call(grad_bands_kernel, 'vvv', [square, ((8, 8, 128), 'v'), row], [(256,...]
  transfers between devices with their start and end apart: 5 -> 4, of which waited for: 5 -> 4; matrix products, arithmetic and copies ran while one was open for 1% -> 1% of each run, Pallas kernels for 5% -> 4%
where the time goes in v3:
time: 185 us; the launch traced here: 184 us
  blocking collectives  93.4 us (50%)
  waiting for transfers between devices  29.6 us (16%)
  starting transfers between devices  29.2 us (16%)
  Pallas kernels  28 us (15%)
  local copies, waits for them, and re-layouts  3.01 us (2%)
    all_to_all x3, blocking collectives, local(): swap_x = lambda v: lax.all_to_all(v, 'gx', 0, 0, tiled=False)  48.8 us
    all_to_all x3, blocking collectives, local(): swap_y = lambda v: lax.all_to_all(v, 'gy', 0, 0, tiled=False)  44.5 us
    all_to_all x3, waiting for transfers between devices, local(): swap_x = lambda v: lax.all_to_all(v, 'gx', 0, 0, tiled=False)  22 us
    all_to_all x3, starting transfers between devices, local(): swap_x = lambda v: lax.all_to_all(v, 'gx', 0, 0, tiled=False)  18.8 us
    all_to_all x1, starting transfers between devices, local(): swap_y = lambda v: lax.all_to_all(v, 'gy', 0, 0, tiled=False)  10.3 us
    pallas_call x1, Pallas kernels, local(): call(centre_kernel, 'vaavsvv', [(cells, 'a'), (cells, 'a'), packed], [cel...  8.18 us
    all_to_all x1, waiting for transfers between devices, local(): swap_y = lambda v: lax.all_to_all(v, 'gy', 0, 0, tiled=False)  7.63 us
    pallas_call x1, Pallas kernels, local(): call(analyse_kernel, 'av', [packed], [cells, parts], 4, 58)  5.32 us
  transfers between devices with their start and end apart: 4, of which 4 were waited for; matrix products, arithmetic and copies ran while one was open for 1% of the time, Pallas kernels for 4%

profile of v3, /device:TPU:1, one launch (start us, length us, event | category | flops | bytes accessed | tf_op | source)
XLA Modules:
  0.0 184.5 jit_solution(6154150486962540701)
XLA Ops:
  0.7 5.3 %shard_map.119 = f32[8,2,72,128]{3,2,1,0:T(8,128)} custom-call(f32[16,256,128]{2,1,0:T(8,128)} %bitcast.11, bf16[160,256]{1,0:T(8,128)(2,1)} %constant.16.clone.down_ref), custom_call_target="tpu_custom_call" | custom-call | tf_op jit(solution)/shard_map/pallas_call | solution.py:524
  6.0 17.2 %all_to_all.50.r_ref = f32[8,2,72,128]{3,2,1,0:T(8,128)S(1)} all-to-all(f32[8,2,72,128]{3,2,1,0:T(8,128)} %shard_map.119), channel_id=1, replica_groups=mesh['gx'=8,'gy'=32] {'gx'}, dimensions={0} | all-to-all | bytes 1179648 | tf_op jit(solution)/shard_map/all_to_all | solution.py:506
  23.2 1.3 shard_map.120
  24.5 10.3 %all-to-all-start.1 = ((f32[32,2,8,128]{3,2,1,0:T(8,128)}), f32[32,2,8,128]{3,2,1,0:T(8,128)S(1)}, u32[]{:S(2)}, u32[]{:S(2)}) async-start(f32[32,2,8,128]{3,2,1,0:T(8,128)} %shard_map.120), calls=%async_computation.1 | async-start | bytes 524288 | tf_op jit(solution)/shard_map/all_to_all | solution.py:507
  36.8 7.6 %all-to-all-done.1.v_ref = f32[32,2,8,128]{3,2,1,0:T(8,128)S(1)} async-done(((f32[32,2,8,128]{3,2,1,0:T(8,128)}), f32[32,2,8,128]{3,2,1,0:T(8,128)S(1)}, u32[]{:S(2)}, u32[]{:S(2)}) %all-to-all-start.1) | async-done | bytes 262176 | tf_op jit(solution)/shard_map/all_to_all | solution.py:507
  44.5 1.2 shard_map.122
  45.7 15.5 %all_to_all.51.v_ref = f32[32,2,8,128]{3,2,1,0:T(8,128)S(1)} all-to-all(f32[32,2,8,128]{3,2,1,0:T(8,128)S(1)} %get-tuple-element.21), channel_id=1, replica_groups=mesh['gx'=8,'gy'=32] {'gy'}, dimensions={0} | all-to-all | bytes 524288 | tf_op jit(solution)/shard_map/all_to_all | solution.py:507
  61.8 17.1 %all_to_all.52.r_ref = f32[8,2,72,128]{3,2,1,0:T(8,128)} all-to-all(f32[8,2,72,128]{3,2,1,0:T(8,128)S(1)} %shard_map.123), channel_id=1, replica_groups=mesh['gx'=8,'gy'=32] {'gx'}, dimensions={0} | all-to-all | bytes 1179648 | tf_op jit(solution)/shard_map/all_to_all | solution.py:506
  79.0 8.2 %shard_map.124 = (f32[16,256,128]{2,1,0:T(8,128)}, f32[16,256,128]{2,1,0:T(8,128)}, f32[8,2,72,128]{3,2,1,0:T(8,128)}) custom-call(f32[8,2,72,128]{3,2,1,0:T(8,128)} %all_to_all.52.r_ref, f32[16,256,128]{2,1,0:T(8,128)} %bitcast.12, f32[16,256,128]{2,1,0:T(8,128)} %bitcast.15, bf16[128,384]{1,0:T(8,128)(2,1)} %copy-done.3, f32[16]{0:T(128)} %bias_ref.1, ...), custom_call_target="tpu_custom_call" | custom-call | tf_op jit(solution)/shard_map/pallas_call | solution.py:530
  87.1 14.6 %all_to_all.53.r_ref = f32[8,2,72,128]{3,2,1,0:T(8,128)S(1)} all-to-all(f32[8,2,72,128]{3,2,1,0:T(8,128)} %get-tuple-element.24), channel_id=1, replica_groups=mesh['gx'=8,'gy'=32] {'gx'}, dimensions={0} | all-to-all | bytes 1179648 | tf_op jit(solution)/shard_map/all_to_all | solution.py:506
  101.7 0.8 shard_map.125
  102.5 13.6 %all_to_all.54.v_ref = f32[32,2,8,128]{3,2,1,0:T(8,128)S(1)} all-to-all(f32[32,2,8,128]{3,2,1,0:T(8,128)S(1)} %get-tuple-element.25), channel_id=1, replica_groups=mesh['gx'=8,'gy'=32] {'gy'}, dimensions={0} | all-to-all | bytes 524288 | tf_op jit(solution)/shard_map/all_to_all | solution.py:507
  116.1 1.5 shard_map.126
  117.7 6.9 %all-to-all-start.6 = ((f32[8,8,128]{2,1,0:T(8,128)}), f32[8,8,128]{2,1,0:T(8,128)S(1)}, u32[]{:S(2)}, u32[]{:S(2)}) async-start(f32[8,8,128]{2,1,0:T(8,128)} %get-tuple-element.29), calls=%async_computation.6 | async-start | bytes 65536 | tf_op jit(solution)/shard_map/all_to_all | solution.py:506
  125.3 4.0 %all-to-all-done.6.g_ref = f32[8,8,128]{2,1,0:T(8,128)S(1)} async-done(((f32[8,8,128]{2,1,0:T(8,128)}), f32[8,8,128]{2,1,0:T(8,128)S(1)}, u32[]{:S(2)}, u32[]{:S(2)}) %all-to-all-start.6) | async-done | bytes 32800 | tf_op jit(solution)/shard_map/all_to_all | solution.py:506
  129.4 15.4 %all_to_all.55.v_ref.m_ref = f32[32,3,8,128]{3,2,1,0:T(8,128)S(1)} all-to-all(f32[32,3,8,128]{3,2,1,0:T(8,128)S(1)} %shard_map.128), channel_id=1, replica_groups=mesh['gx'=8,'gy'=32] {'gy'}, dimensions={0} | all-to-all | bytes 786432 | tf_op jit(solution)/shard_map/all_to_all | solution.py:507
  144.7 1.5 shard_map.129
  146.2 7.6 %all-to-all-start.8 = ((f32[8,2,72,128]{3,2,1,0:T(8,128)}), f32[8,2,72,128]{3,2,1,0:T(8,128)S(1)}, u32[]{:S(2)}, u32[]{:S(2)}) async-start(f32[8,2,72,128]{3,2,1,0:T(8,128)} %get-tuple-element.30), calls=%async_computation.8 | async-start | bytes 1179648 | tf_op jit(solution)/shard_map/all_to_all | solution.py:506
  153.8 1.3 shard_map.131
  155.0 8.9 %all-to-all-done.8.r_ref = f32[8,2,72,128]{3,2,1,0:T(8,128)S(1)} async-done(((f32[8,2,72,128]{3,2,1,0:T(8,128)}), f32[8,2,72,128]{3,2,1,0:T(8,128)S(1)}, u32[]{:S(2)}, u32[]{:S(2)}) %all-to-all-start.8) | async-done | bytes 589856 | tf_op jit(solution)/shard_map/all_to_all | solution.py:506
  164.0 4.3 %all-to-all-start.9 = ((f32[8,4,32,256]{3,2,1,0:T(8,128)}), f32[8,4,32,256]{3,2,1,0:T(8,128)S(1)}, u32[]{:S(2)}, u32[]{:S(2)}) async-start(f32[8,4,32,256]{3,2,1,0:T(8,128)} %shard_map.131), calls=%async_computation.9 | async-start | bytes 2097152 | tf_op jit(solution)/shard_map/all_to_all | solution.py:506
  169.5 4.9 %shard_map.130 = f32[16,256,128]{2,1,0:T(8,128)} custom-call(f32[8,2,72,128]{3,2,1,0:T(8,128)} %copy-done.5, f32[16,256,128]{2,1,0:T(8,128)} %get-tuple-element.31.g_hbm, bf16[128,384]{1,0:T(8,128)(2,1)} %copy-done.2, bf16[256,256]{1,0:T(8,128)(2,1)} %constant.17.clone.up_ref), custom_call_target="tpu_custom_call" | custom-call | tf_op jit(solution)/shard_map/pallas_call | solution.py:546
  174.4 9.0 %all-to-all-done.9 = f32[8,4,32,256]{3,2,1,0:T(8,128)S(1)} async-done(((f32[8,4,32,256]{3,2,1,0:T(8,128)}), f32[8,4,32,256]{3,2,1,0:T(8,128)S(1)}, u32[]{:S(2)}, u32[]{:S(2)}) %all-to-all-start.9) | async-done | bytes 1048608 | tf_op jit(solution)/shard_map/all_to_all | solution.py:506
  183.4 1.0 copy.13
  (19 shorter events, 4.6 us)
Async XLA Ops:
  0.6 34.2 %copy-start.1 = (f32[4,16,16,256]{3,2,1,0:T(8,128)S(1)}, f32[4,16,16,256]{3,2,1,0:T(8,128)}, u32[]{:S(2)}) copy-start(f32[4,16,16,256]{3,2,1,0:T(8,128)} %param.10) | copy-start | bytes 3145732
  0.6 34.2 %copy-start.4 = (f32[16,16]{1,0:T(8,128)S(1)}, f32[16,16]{1,0:T(8,128)}, u32[]{:S(2)}) copy-start(f32[16,16]{1,0:T(8,128)} %pw_ref.1) | copy-start | bytes 3076
  6.0 38.5 %copy-start = (f32[256,128]{1,0:T(8,128)S(1)}, f32[256,128]{1,0:T(8,128)}, u32[]{:S(2)}) copy-start(f32[256,128]{1,0:T(8,128)} %constant.15.clone.q_ref) | copy-start | bytes 393220
  24.5 20.0 %all-to-all-start.1 = ((f32[32,2,8,128]{3,2,1,0:T(8,128)}), f32[32,2,8,128]{3,2,1,0:T(8,128)S(1)}, u32[]{:S(2)}, u32[]{:S(2)}) async-start(f32[32,2,8,128]{3,2,1,0:T(8,128)} %shard_map.120), calls=%async_computation.1 | async-start | bytes 524288 | tf_op jit(solution)/shard_map/all_to_all | solution.py:507
  35.6 0.6 copy-start.2
  36.2 0.6 copy-start.3
  117.7 11.7 %all-to-all-start.6 = ((f32[8,8,128]{2,1,0:T(8,128)}), f32[8,8,128]{2,1,0:T(8,128)S(1)}, u32[]{:S(2)}, u32[]{:S(2)}) async-start(f32[8,8,128]{2,1,0:T(8,128)} %get-tuple-element.29), calls=%async_computation.6 | async-start | bytes 65536 | tf_op jit(solution)/shard_map/all_to_all | solution.py:506
  146.2 17.8 %all-to-all-start.8 = ((f32[8,2,72,128]{3,2,1,0:T(8,128)}), f32[8,2,72,128]{3,2,1,0:T(8,128)S(1)}, u32[]{:S(2)}, u32[]{:S(2)}) async-start(f32[8,2,72,128]{3,2,1,0:T(8,128)} %get-tuple-element.30), calls=%async_computation.8 | async-start | bytes 1179648 | tf_op jit(solution)/shard_map/all_to_all | solution.py:506
  164.0 5.5 %copy-start.5 = (f32[8,2,72,128]{3,2,1,0:T(8,128)}, f32[8,2,72,128]{3,2,1,0:T(8,128)S(1)}, u32[]{:S(2)}) copy-start(f32[8,2,72,128]{3,2,1,0:T(8,128)S(1)} %all-to-all-done.8.r_ref) | copy-start | bytes 1769476
  164.0 19.5 %all-to-all-start.9 = ((f32[8,4,32,256]{3,2,1,0:T(8,128)}), f32[8,4,32,256]{3,2,1,0:T(8,128)S(1)}, u32[]{:S(2)}, u32[]{:S(2)}) async-start(f32[8,4,32,256]{3,2,1,0:T(8,128)} %shard_map.131), calls=%async_computation.9 | async-start | bytes 2097152 | tf_op jit(solution)/shard_map/all_to_all | solution.py:506

commit v4 on v3

--- a/solution.py
+++ b/solution.py
@@ -291,7 +291,8 @@
         for k in range(1, 4):
             rows = g_scr[group * 32 + k * 8 : group * 32 + k * 8 + 8, :]
             packed = jnp.where(lane // 32 == k, pltpu.roll(rows, 32 * k, 1), packed)
-        g_ref[group] = packed
+        for copy in range(8):
+            g_ref[copy, group] = packed
     first = v_ref[0, 0, 7:8, :]
     second = v_ref[0, 1, 7:8, :]
     for slab in range(1, 32):
@@ -317,13 +318,17 @@
 
 
 def join_kernel(v_ref, g_ref, o_ref):
-    total = g_ref[0]
-    for i in range(1, 8):
-        total = total + g_ref[i]
-    total = total * (1.0 / math.sqrt(128.0))
-    for slab in range(32):
-        o_ref[slab, 0:2] = v_ref[slab]
-        o_ref[slab, 2] = total
+    for quarter in range(4):
+        totals = []
+        for group in (2 * quarter, 2 * quarter + 1):
+            total = g_ref[0, group]
+            for i in range(1, 8):
+                total = total + g_ref[i, group]
+            totals.append(total * (1.0 / math.sqrt(128.0)))
+        for slab in range(8 * quarter, 8 * quarter + 8):
+            o_ref[slab, 0:2] = v_ref[slab]
+            o_ref[slab, 2] = totals[0]
+            o_ref[slab, 3] = totals[1]
 
 
 def spread_body(v_ref, l_scr, s_ref):
@@ -475,15 +480,27 @@
 def modes_place_kernel(m_ref, o_ref):
     for high in range(2):
         for right in range(2):
-            rows = [m_ref[high * 16 + right * 8 + m, 2] for m in range(8)]
-            rows = swap_blocks(rows)
-            for k in range(4):
-                for up in range(2):
-                    for copy in range(8):
+            for group in range(2):
+                rows = [m_ref[high * 16 + right * 8 + m, 2 + group] for m in range(8)]
+                rows = swap_blocks(rows)
+                for k in range(4):
+                    at = group * 32 + k * 8
+                    for up in range(2):
                         o_ref[
-                            copy, high + 2 * up, k * 8 : (k + 1) * 8,
-                            right * 128 : (right + 1) * 128,
+                            high + 2 * up, at : at + 8, right * 128 : (right + 1) * 128
                         ] = rows[2 * k + up]
+
+
+def gather_kernel(index_ref, first, second, third, fourth, out_hbm, sems):
+    copies = []
+    for k, part in enumerate((first, second, third, fourth)):
+        owner = (index_ref[0] // 8 + 4 - k) % 4
+        to = out_hbm.at[:, pl.ds(pl.multiple_of(owner * 64, 64), 64), :]
+        copies.append(pltpu.make_async_copy(part, to, sems.at[k]))
+    for copy in copies:
+        copy.start()
+    for copy in copies:
+        copy.wait()
 
 
 def call(kernel, ins, outs, scratch=(), sems=0, mib=8):
@@ -529,31 +546,35 @@
     (spread,) = call(spread_kernel, "v", [packed], rows3)(swap_y(back))
     output_field, grads, sent = call(
         centre_kernel, "vaavsvv", [(cells, "a"), (cells, "a"), packed],
-        [cells] * 4 + [parts] * 2 + [(128, 128)] * 2, 10, 58,
+        [cells] * 4 + [parts] * 2 + [(128, 128)] * 2, 10, 52,
     )(
         swap_x(spread), flow_cells, cotangent.reshape(cells), mix_forward, point_bias, down, up
     )
     got, bias_part = call(rows_grad_kernel, "v", [coefs, row], rows3)(swap_x(sent))
     bands_grad, mode_part, point_total = call(
-        grad_bands_kernel, "vvv", [square, ((8, 8, 128), "v"), row], [(256, 128)]
+        grad_bands_kernel, "vvv", [square, ((8, 8, 8, 128), "v"), row], [(256, 128)]
     )(swap_y(got), table, bands_flow)
     (back,) = call(mix_grad_kernel, "vvvv", [coefs], [(256, 128)])(
         bands_grad, table, weights, bias_part
     )
-    (joined,) = call(join_kernel, "vv", [((32, 3, 8, 128), "v")])(back, swap_x(mode_part))
+    (joined,) = call(join_kernel, "vv", [((32, 4, 8, 128), "v")])(back, swap_x(mode_part))
     joined = swap_y(joined)
     spread, bias_total = call(spread_grad_kernel, "v", [packed, row], rows3)(joined)
     (grad_field,) = call(
-        finish_kernel, "vavv", [(cells, "a")], [cells] * 2 + [parts], 5, 58
+        finish_kernel, "vavv", [(cells, "a")], [cells] * 2 + [parts], 5, 52
     )(swap_x(spread), grads, mix_back, up)
-    (placed,) = call(modes_place_kernel, "v", [((8, 4, 32, 256), "v")])(joined)
-    modes = jnp.transpose(swap_x(placed), (1, 0, 2, 3)).reshape(4, 16, 16, 256)
+    (placed,) = call(modes_place_kernel, "v", [((4, 64, 256), "v")])(joined)
+    shifted = [
+        lax.ppermute(placed, "gy", [(j, (j + 8 * k) % 32) for j in range(32)]) for k in (1, 2, 3)
+    ]
+    slab, grad_field = lax.optimization_barrier((slab, grad_field))
+    (modes,) = call(gather_kernel, "saaaa", [((4, 256, 256), "a")], (), 4)(slab, placed, *shifted)
 
     cell_count = flow_field.shape[3] * 256 * 256
     return (
         output_field.reshape(flow_field.shape),
         grad_field.reshape(flow_field.shape),
-        modes,
+        modes.reshape(4, 16, 16, 256),
         point_total[0:2].reshape(16, 16) / math.sqrt(cell_count),
         bias_total[0, :16] / math.sqrt(cell_count),
     )

time: 185 us -> 175 us (0.946)
  waiting for transfers between devices: 29.6 us -> 22.4 us
  starting transfers between devices: 29.2 us -> 26.9 us
  local copies, waits for them, and re-layouts: 3.01 us -> 0.72 us
    all_to_all x3 -> x2, waiting for transfers between devices: 22 us -> 12.6 us  [local(): swap_x = lambda v: lax.all_to_all(v, 'gx', 0, 0, tiled=False)]
    all_to_all x3 -> x2, starting transfers between devices: 18.8 us -> 14.8 us  [local(): swap_x = lambda v: lax.all_to_all(v, 'gx', 0, 0, tiled=False)]
    all_to_all x3, blocking collectives: 44.5 us -> 47.1 us  [local(): swap_y = lambda v: lax.all_to_all(v, 'gy', 0, 0, tiled=False)]
    pallas_call x4 -> x5, Pallas kernels: 7.71 us -> 8.16 us  [the longest x1 5.13 us: local(): call(finish_kernel, 'vavv', [(cells, 'a')], [cells] * 2 + [parts], 5, 52)]
  transfers between devices with their start and end apart: 4 -> 6, of which waited for: 4 -> 4; matrix products, arithmetic and copies ran while one was open for 1% -> 1% of each run, Pallas kernels for 4% -> 4%
where the time goes in v4:
time: 175 us; the launch traced here: 174 us
  blocking collectives  94.2 us (54%)
  Pallas kernels  28.7 us (16%)
  starting transfers between devices  26.9 us (15%)
  waiting for transfers between devices  22.4 us (13%)
    all_to_all x3, blocking collectives, local(): swap_y = lambda v: lax.all_to_all(v, 'gy', 0, 0, tiled=False)  47.1 us
    all_to_all x3, blocking collectives, local(): swap_x = lambda v: lax.all_to_all(v, 'gx', 0, 0, tiled=False)  47.1 us
    all_to_all x2, starting transfers between devices, local(): swap_x = lambda v: lax.all_to_all(v, 'gx', 0, 0, tiled=False)  14.8 us
    all_to_all x2, waiting for transfers between devices, local(): swap_x = lambda v: lax.all_to_all(v, 'gx', 0, 0, tiled=False)  12.6 us
    all_to_all x1, starting transfers between devices, local(): swap_y = lambda v: lax.all_to_all(v, 'gy', 0, 0, tiled=False)  10.3 us
    all_to_all x1, waiting for transfers between devices, local(): swap_y = lambda v: lax.all_to_all(v, 'gy', 0, 0, tiled=False)  8.87 us
    pallas_call x1, Pallas kernels, local(): call(centre_kernel, 'vaavsvv', [(cells, 'a'), (cells, 'a'), packed], [cel...  8.38 us
    pallas_call x1, Pallas kernels, local(): call(analyse_kernel, 'av', [packed], [cells, parts], 4, 58)  5.32 us
  transfers between devices with their start and end apart: 6, of which 4 were waited for; matrix products, arithmetic and copies ran while one was open for 1% of the time, Pallas kernels for 4%

profile of v4, /device:TPU:1, one launch (start us, length us, event | category | flops | bytes accessed | tf_op | source)
XLA Modules:
  0.0 174.2 jit_solution(3692931537829504269)
XLA Ops:
  0.7 5.3 %shard_map.119 = f32[8,2,72,128]{3,2,1,0:T(8,128)} custom-call(f32[16,256,128]{2,1,0:T(8,128)} %bitcast.10, bf16[160,256]{1,0:T(8,128)(2,1)} %constant.16.clone.down_ref), custom_call_target="tpu_custom_call" | custom-call | tf_op jit(solution)/shard_map/pallas_call | solution.py:541
  6.0 17.2 %all_to_all.45.r_ref = f32[8,2,72,128]{3,2,1,0:T(8,128)S(1)} all-to-all(f32[8,2,72,128]{3,2,1,0:T(8,128)} %shard_map.119), channel_id=1, replica_groups=mesh['gx'=8,'gy'=32] {'gx'}, dimensions={0} | all-to-all | bytes 1179648 | tf_op jit(solution)/shard_map/all_to_all | solution.py:523
  23.2 1.3 shard_map.120
  24.5 10.3 %all-to-all-start.1 = ((f32[32,2,8,128]{3,2,1,0:T(8,128)}), f32[32,2,8,128]{3,2,1,0:T(8,128)S(1)}, u32[]{:S(2)}, u32[]{:S(2)}) async-start(f32[32,2,8,128]{3,2,1,0:T(8,128)} %shard_map.120), calls=%async_computation.1 | async-start | bytes 524288 | tf_op jit(solution)/shard_map/all_to_all | solution.py:524
  34.9 0.7 shard_map.121
  35.6 8.9 %all-to-all-done.1.v_ref = f32[32,2,8,128]{3,2,1,0:T(8,128)S(1)} async-done(((f32[32,2,8,128]{3,2,1,0:T(8,128)}), f32[32,2,8,128]{3,2,1,0:T(8,128)S(1)}, u32[]{:S(2)}, u32[]{:S(2)}) %all-to-all-start.1) | async-done | bytes 262176 | tf_op jit(solution)/shard_map/all_to_all | solution.py:524
  44.5 1.2 shard_map.122
  45.7 15.5 %all_to_all.46.v_ref = f32[32,2,8,128]{3,2,1,0:T(8,128)S(1)} all-to-all(f32[32,2,8,128]{3,2,1,0:T(8,128)S(1)} %get-tuple-element.23), channel_id=1, replica_groups=mesh['gx'=8,'gy'=32] {'gy'}, dimensions={0} | all-to-all | bytes 524288 | tf_op jit(solution)/shard_map/all_to_all | solution.py:524
  61.8 16.4 %all_to_all.47.r_ref = f32[8,2,72,128]{3,2,1,0:T(8,128)S(1)} all-to-all(f32[8,2,72,128]{3,2,1,0:T(8,128)S(1)} %shard_map.123), channel_id=1, replica_groups=mesh['gx'=8,'gy'=32] {'gx'}, dimensions={0} | all-to-all | bytes 1179648 | tf_op jit(solution)/shard_map/all_to_all | solution.py:523
  78.3 8.4 %shard_map.124 = (f32[16,256,128]{2,1,0:T(8,128)}, f32[16,256,128]{2,1,0:T(8,128)}, f32[8,2,72,128]{3,2,1,0:T(8,128)S(1)}) custom-call(f32[8,2,72,128]{3,2,1,0:T(8,128)S(1)} %all_to_all.47.r_ref, f32[16,256,128]{2,1,0:T(8,128)} %bitcast.11, f32[16,256,128]{2,1,0:T(8,128)} %bitcast.13, bf16[128,384]{1,0:T(8,128)(2,1)S(1)} %get-tuple-element.24.w_ref, ...), custom_call_target="tpu_custom_call" | custom-call | tf_op jit(solution)/shard_map/pallas_call | solution.py:547
  86.6 13.5 %all_to_all.48.r_ref = f32[8,2,72,128]{3,2,1,0:T(8,128)S(1)} all-to-all(f32[8,2,72,128]{3,2,1,0:T(8,128)S(1)} %get-tuple-element.26), channel_id=1, replica_groups=mesh['gx'=8,'gy'=32] {'gx'}, dimensions={0} | all-to-all | bytes 1179648 | tf_op jit(solution)/shard_map/all_to_all | solution.py:523
  100.1 0.8 shard_map.125
  100.9 13.6 %all_to_all.49.v_ref = f32[32,2,8,128]{3,2,1,0:T(8,128)S(1)} all-to-all(f32[32,2,8,128]{3,2,1,0:T(8,128)S(1)} %get-tuple-element.27), channel_id=1, replica_groups=mesh['gx'=8,'gy'=32] {'gy'}, dimensions={0} | all-to-all | bytes 524288 | tf_op jit(solution)/shard_map/all_to_all | solution.py:524
  114.6 1.6 shard_map.126
  116.2 7.0 %all-to-all-start.6 = ((f32[8,8,8,128]{3,2,1,0:T(8,128)}), f32[8,8,8,128]{3,2,1,0:T(8,128)S(1)}, u32[]{:S(2)}, u32[]{:S(2)}) async-start(f32[8,8,8,128]{3,2,1,0:T(8,128)} %get-tuple-element.31), calls=%async_computation.6 | async-start | bytes 524288 | tf_op jit(solution)/shard_map/all_to_all | solution.py:523
  123.9 5.8 %all-to-all-done.6.g_ref = f32[8,8,8,128]{3,2,1,0:T(8,128)S(1)} async-done(((f32[8,8,8,128]{3,2,1,0:T(8,128)}), f32[8,8,8,128]{3,2,1,0:T(8,128)S(1)}, u32[]{:S(2)}, u32[]{:S(2)}) %all-to-all-start.6) | async-done | bytes 262176 | tf_op jit(solution)/shard_map/all_to_all | solution.py:523
  129.8 18.0 %all_to_all.50.v_ref.m_ref = f32[32,4,8,128]{3,2,1,0:T(8,128)S(1)} all-to-all(f32[32,4,8,128]{3,2,1,0:T(8,128)S(1)} %shard_map.128), channel_id=1, replica_groups=mesh['gx'=8,'gy'=32] {'gy'}, dimensions={0} | all-to-all | bytes 1048576 | tf_op jit(solution)/shard_map/all_to_all | solution.py:524
  147.7 1.5 shard_map.129
  149.2 7.8 %all-to-all-start.8 = ((f32[8,2,72,128]{3,2,1,0:T(8,128)}), f32[8,2,72,128]{3,2,1,0:T(8,128)S(1)}, u32[]{:S(2)}, u32[]{:S(2)}) async-start(f32[8,2,72,128]{3,2,1,0:T(8,128)} %get-tuple-element.32), calls=%async_computation.8 | async-start | bytes 1179648 | tf_op jit(solution)/shard_map/all_to_all | solution.py:523
  157.9 1.0 collective-permute-start.1
  160.3 6.8 %all-to-all-done.8.r_ref = f32[8,2,72,128]{3,2,1,0:T(8,128)S(1)} async-done(((f32[8,2,72,128]{3,2,1,0:T(8,128)}), f32[8,2,72,128]{3,2,1,0:T(8,128)S(1)}, u32[]{:S(2)}, u32[]{:S(2)}) %all-to-all-start.8) | async-done | bytes 589856 | tf_op jit(solution)/shard_map/all_to_all | solution.py:523
  167.2 5.1 %shard_map.130 = f32[16,256,128]{2,1,0:T(8,128)} custom-call(f32[8,2,72,128]{3,2,1,0:T(8,128)S(1)} %all-to-all-done.8.r_ref, f32[16,256,128]{2,1,0:T(8,128)} %get-tuple-element.33.g_hbm, bf16[128,384]{1,0:T(8,128)(2,1)S(1)} %get-tuple-element.34.w_ref, bf16[256,256]{1,0:T(8,128)(2,1)S(1)} %copy-done.2), custom_call_target="tpu_custom_call" | custom-call | tf_op jit(solution)/shard_map/pallas_call | solution.py:563
  172.3 0.9 collective-permute-done.second
  173.2 1.0 shard_map.132
  (23 shorter events, 3.8 us)
Async XLA Ops:
  0.6 34.2 %copy-start.1 = (f32[4,16,16,256]{3,2,1,0:T(8,128)S(1)}, f32[4,16,16,256]{3,2,1,0:T(8,128)}, u32[]{:S(2)}) copy-start(f32[4,16,16,256]{3,2,1,0:T(8,128)} %param.10) | copy-start | bytes 3145732
  0.6 34.2 %copy-start.4 = (f32[16,16]{1,0:T(8,128)S(1)}, f32[16,16]{1,0:T(8,128)}, u32[]{:S(2)}) copy-start(f32[16,16]{1,0:T(8,128)} %pw_ref.1) | copy-start | bytes 3076
  6.0 38.5 %copy-start = (f32[256,128]{1,0:T(8,128)S(1)}, f32[256,128]{1,0:T(8,128)}, u32[]{:S(2)}) copy-start(f32[256,128]{1,0:T(8,128)} %constant.15.clone.q_ref) | copy-start | bytes 393220
  24.5 20.0 %all-to-all-start.1 = ((f32[32,2,8,128]{3,2,1,0:T(8,128)}), f32[32,2,8,128]{3,2,1,0:T(8,128)S(1)}, u32[]{:S(2)}, u32[]{:S(2)}) async-start(f32[32,2,8,128]{3,2,1,0:T(8,128)} %shard_map.120), calls=%async_computation.1 | async-start | bytes 524288 | tf_op jit(solution)/shard_map/all_to_all | solution.py:524
  34.8 43.5 %copy-start.2 = (bf16[256,256]{1,0:T(8,128)(2,1)S(1)}, bf16[256,256]{1,0:T(8,128)(2,1)}, u32[]{:S(2)}) copy-start(bf16[256,256]{1,0:T(8,128)(2,1)} %constant.17.clone.up_ref) | copy-start | bytes 393220
  34.8 43.5 %copy-start.3 = (bf16[160,256]{1,0:T(8,128)(2,1)S(1)}, bf16[160,256]{1,0:T(8,128)(2,1)}, u32[]{:S(2)}) copy-start(bf16[160,256]{1,0:T(8,128)(2,1)} %constant.16.clone.down_ref) | copy-start | bytes 245764
  34.8 43.4 %copy-start.5 = (f32[16]{0:T(128)S(1)}, f32[16]{0:T(128)}, u32[]{:S(2)}) copy-start(f32[16]{0:T(128)} %bias_ref.1) | copy-start | bytes 196
  116.2 13.5 %all-to-all-start.6 = ((f32[8,8,8,128]{3,2,1,0:T(8,128)}), f32[8,8,8,128]{3,2,1,0:T(8,128)S(1)}, u32[]{:S(2)}, u32[]{:S(2)}) async-start(f32[8,8,8,128]{3,2,1,0:T(8,128)} %get-tuple-element.31), calls=%async_computation.6 | async-start | bytes 524288 | tf_op jit(solution)/shard_map/all_to_all | solution.py:523
  149.2 18.0 %all-to-all-start.8 = ((f32[8,2,72,128]{3,2,1,0:T(8,128)}), f32[8,2,72,128]{3,2,1,0:T(8,128)S(1)}, u32[]{:S(2)}, u32[]{:S(2)}) async-start(f32[8,2,72,128]{3,2,1,0:T(8,128)} %get-tuple-element.32), calls=%async_computation.8 | async-start | bytes 1179648 | tf_op jit(solution)/shard_map/all_to_all | solution.py:523
  157.3 15.0 %collective-permute-start.2 = (f32[4,64,256]{2,1,0:T(8,128)S(1)}, f32[4,64,256]{2,1,0:T(8,128)S(1)}, u32[]{:S(2)}, u32[]{:S(2)}) collective-permute-start(f32[4,64,256]{2,1,0:T(8,128)S(1)} %shard_map.131.first), channel_id=1, source_target_pairs={{0,24},{1,25},{2,26},{3,27},{4,28},{5,29},{6,30},{7,31},{8,0},{9,1... | collective-permute-start | bytes 786440 | tf_op jit(solution)/shard_map/ppermute | solution.py:568
  157.9 14.4 %collective-permute-start.1 = (f32[4,64,256]{2,1,0:T(8,128)S(1)}, f32[4,64,256]{2,1,0:T(8,128)S(1)}, u32[]{:S(2)}, u32[]{:S(2)}) collective-permute-start(f32[4,64,256]{2,1,0:T(8,128)S(1)} %shard_map.131.first), channel_id=1, source_target_pairs={{0,16},{1,17},{2,18},{3,19},{4,20},{5,21},{6,22},{7,23},{8,24},{9,... | collective-permute-start | bytes 786440 | tf_op jit(solution)/shard_map/ppermute | solution.py:568
  158.9 14.3 %collective-permute-start = (f32[4,64,256]{2,1,0:T(8,128)S(1)}, f32[4,64,256]{2,1,0:T(8,128)S(1)}, u32[]{:S(2)}, u32[]{:S(2)}) collective-permute-start(f32[4,64,256]{2,1,0:T(8,128)S(1)} %shard_map.131.first), channel_id=1, source_target_pairs={{0,8},{1,9},{2,10},{3,11},{4,12},{5,13},{6,14},{7,15},{8,16},{9,17... | collective-permute-start | bytes 786440 | tf_op jit(solution)/shard_map/ppermute | solution.py:568

commit v5 on v3

--- a/solution.py
+++ b/solution.py
@@ -80,18 +80,13 @@
 
 def swap_blocks(rows):
     lane = lax.broadcasted_iota(jnp.int32, (8, 128), 1)
-    rows = list(rows)
+    rows = [rows[0]] + [pltpu.roll(rows[c], 16 * c, 1) for c in range(1, 8)]
     for bit in range(3):
-        width = 16 << bit
-        upper = (lane & width) != 0
-        for lo in range(8):
-            if lo & (1 << bit):
-                continue
-            hi = lo | (1 << bit)
-            first, second = rows[lo], rows[hi]
-            rows[lo] = jnp.where(upper, pltpu.roll(second, width, 1), first)
-            rows[hi] = jnp.where(upper, second, pltpu.roll(first, 128 - width, 1))
-    return rows
+        step = 1 << bit
+        chosen = (lane & (16 * step)) != 0
+        rows = [jnp.where(chosen, rows[(m + step) % 8], rows[m]) for m in range(8)]
+    rows = [rows[(8 - k) % 8] for k in range(8)]
+    return [rows[0]] + [pltpu.roll(rows[k], 128 - 16 * k, 1) for k in range(1, 8)]
 
 
 def split(value):
@@ -291,7 +286,8 @@
         for k in range(1, 4):
             rows = g_scr[group * 32 + k * 8 : group * 32 + k * 8 + 8, :]
             packed = jnp.where(lane // 32 == k, pltpu.roll(rows, 32 * k, 1), packed)
-        g_ref[group] = packed
+        for copy in range(group // 4, 8, 2):
+            g_ref[copy, group % 4] = packed
     first = v_ref[0, 0, 7:8, :]
     second = v_ref[0, 1, 7:8, :]
     for slab in range(1, 32):
@@ -317,13 +313,14 @@
 
 
 def join_kernel(v_ref, g_ref, o_ref):
-    total = g_ref[0]
-    for i in range(1, 8):
-        total = total + g_ref[i]
-    total = total * (1.0 / math.sqrt(128.0))
-    for slab in range(32):
-        o_ref[slab, 0:2] = v_ref[slab]
-        o_ref[slab, 2] = total
+    for quarter in range(4):
+        total = g_ref[0, quarter]
+        for i in range(1, 8):
+            total = total + g_ref[i, quarter]
+        total = total * (1.0 / math.sqrt(128.0))
+        for slab in range(8 * quarter, 8 * quarter + 8):
+            o_ref[slab, 0:2] = v_ref[slab]
+            o_ref[slab, 2] = total
 
 
 def spread_body(v_ref, l_scr, s_ref):
@@ -475,15 +472,28 @@
 def modes_place_kernel(m_ref, o_ref):
     for high in range(2):
         for right in range(2):
-            rows = [m_ref[high * 16 + right * 8 + m, 2] for m in range(8)]
-            rows = swap_blocks(rows)
+            rows = swap_blocks([m_ref[high * 16 + right * 8 + m, 2] for m in range(8)])
             for k in range(4):
                 for up in range(2):
-                    for copy in range(8):
-                        o_ref[
-                            copy, high + 2 * up, k * 8 : (k + 1) * 8,
-                            right * 128 : (right + 1) * 128,
-                        ] = rows[2 * k + up]
+                    o_ref[
+                        high + 2 * up, k * 8 : k * 8 + 8, right * 128 : (right + 1) * 128
+                    ] = rows[2 * k + up]
+
+
+def gather_kernel(index_ref, *refs):
+    parts, out_hbm, sems = refs[:8], refs[8], refs[9]
+    copies = []
+    for flip in range(2):
+        for shift in range(4):
+            core = (index_ref[1] + flip) % 2
+            owner = core * 4 + (index_ref[0] // 8 + 4 - shift) % 4
+            to = out_hbm.at[:, pl.ds(pl.multiple_of(owner * 32, 32), 32), :]
+            k = flip * 4 + shift
+            copies.append(pltpu.make_async_copy(parts[k], to, sems.at[k]))
+    for copy in copies:
+        copy.start()
+    for copy in copies:
+        copy.wait()
 
 
 def call(kernel, ins, outs, scratch=(), sems=0, mib=8):
@@ -529,13 +539,13 @@
     (spread,) = call(spread_kernel, "v", [packed], rows3)(swap_y(back))
     output_field, grads, sent = call(
         centre_kernel, "vaavsvv", [(cells, "a"), (cells, "a"), packed],
-        [cells] * 4 + [parts] * 2 + [(128, 128)] * 2, 10, 58,
+        [cells] * 4 + [parts] * 2 + [(128, 128)] * 2, 10, 52,
     )(
         swap_x(spread), flow_cells, cotangent.reshape(cells), mix_forward, point_bias, down, up
     )
     got, bias_part = call(rows_grad_kernel, "v", [coefs, row], rows3)(swap_x(sent))
     bands_grad, mode_part, point_total = call(
-        grad_bands_kernel, "vvv", [square, ((8, 8, 128), "v"), row], [(256, 128)]
+        grad_bands_kernel, "vvv", [square, ((8, 4, 8, 128), "v"), row], [(256, 128)]
     )(swap_y(got), table, bands_flow)
     (back,) = call(mix_grad_kernel, "vvvv", [coefs], [(256, 128)])(
         bands_grad, table, weights, bias_part
@@ -544,16 +554,27 @@
     joined = swap_y(joined)
     spread, bias_total = call(spread_grad_kernel, "v", [packed, row], rows3)(joined)
     (grad_field,) = call(
-        finish_kernel, "vavv", [(cells, "a")], [cells] * 2 + [parts], 5, 58
+        finish_kernel, "vavv", [(cells, "a")], [cells] * 2 + [parts], 5, 52
     )(swap_x(spread), grads, mix_back, up)
-    (placed,) = call(modes_place_kernel, "v", [((8, 4, 32, 256), "v")])(joined)
-    modes = jnp.transpose(swap_x(placed), (1, 0, 2, 3)).reshape(4, 16, 16, 256)
+    (placed,) = call(modes_place_kernel, "v", [((4, 32, 256), "v")])(joined)
+    parts = [placed]
+    for flip, shift in [(f, k) for f in range(2) for k in range(4)][1:]:
+        routes = [
+            (i * 32 + j, (i ^ flip) * 32 + (j + 8 * shift) % 32)
+            for i in range(8)
+            for j in range(32)
+        ]
+        parts.append(lax.ppermute(placed, ("gx", "gy"), routes))
+    place, grad_field = lax.optimization_barrier(
+        (jnp.stack([lax.axis_index("gy"), lax.axis_index("gx")]).astype(jnp.int32), grad_field)
+    )
+    (modes,) = call(gather_kernel, "s" + "a" * 8, [((4, 256, 256), "a")], (), 8)(place, *parts)
 
     cell_count = flow_field.shape[3] * 256 * 256
     return (
         output_field.reshape(flow_field.shape),
         grad_field.reshape(flow_field.shape),
-        modes,
+        modes.reshape(4, 16, 16, 256),
         point_total[0:2].reshape(16, 16) / math.sqrt(cell_count),
         bias_total[0, :16] / math.sqrt(cell_count),
     )

time: 185 us -> 171 us (0.924)
  blocking collectives: 93.4 us -> 76.2 us
  starting transfers between devices: 29.2 us -> 36.5 us
  local copies, waits for them, and re-layouts: 3.01 us -> 0.72 us
  waiting for transfers between devices: 29.6 us -> 27.6 us
    all_to_all x3 -> x2, waiting for transfers between devices: 22 us -> 4.55 us  [local(): swap_x = lambda v: lax.all_to_all(v, 'gx', 0, 0, tiled=False)]
    all_to_all x3 -> x2, blocking collectives: 44.5 us -> 29.2 us  [local(): swap_y = lambda v: lax.all_to_all(v, 'gy', 0, 0, tiled=False)]
    all_to_all x1 -> x2, waiting for transfers between devices: 7.63 us -> 19.9 us  [local(): swap_y = lambda v: lax.all_to_all(v, 'gy', 0, 0, tiled=False)]
    ppermute x0 -> x7, starting transfers between devices: none -> 7.1 us  [local(): parts.append(lax.ppermute(placed, ('gx', 'gy'), routes))]
    all_to_all x1 -> x2, starting transfers between devices: 10.3 us -> 14.5 us  [local(): swap_y = lambda v: lax.all_to_all(v, 'gy', 0, 0, tiled=False)]
    all_to_all x3 -> x2, starting transfers between devices: 18.8 us -> 14.9 us  [local(): swap_x = lambda v: lax.all_to_all(v, 'gx', 0, 0, tiled=False)]
    ppermute x0 -> x7, waiting for transfers between devices: none -> 3.1 us  [local(): parts.append(lax.ppermute(placed, ('gx', 'gy'), routes))]
    pallas_call x3 -> x4, Pallas kernels: 7.68 us -> 7.72 us  [the longest x1 4.39 us: local(): call(finish_kernel, 'vavv', [(cells, 'a')], [cells] * 2 + [parts], 5, 52)]
  transfers between devices with their start and end apart: 4 -> 11, of which waited for: 4 -> 5; matrix products, arithmetic and copies ran while one was open for 1% -> 1% of each run, Pallas kernels for 4% -> 4%
where the time goes in v5:
time: 171 us; the launch traced here: 170 us
  blocking collectives  76.2 us (45%)
  starting transfers between devices  36.5 us (21%)
  waiting for transfers between devices  27.6 us (16%)
  Pallas kernels  27.4 us (16%)
    all_to_all x3, blocking collectives, local(): swap_x = lambda v: lax.all_to_all(v, 'gx', 0, 0, tiled=False)  47.1 us
    all_to_all x2, blocking collectives, local(): swap_y = lambda v: lax.all_to_all(v, 'gy', 0, 0, tiled=False)  29.2 us
    all_to_all x2, waiting for transfers between devices, local(): swap_y = lambda v: lax.all_to_all(v, 'gy', 0, 0, tiled=False)  19.9 us
    all_to_all x2, starting transfers between devices, local(): swap_x = lambda v: lax.all_to_all(v, 'gx', 0, 0, tiled=False)  14.9 us
    all_to_all x2, starting transfers between devices, local(): swap_y = lambda v: lax.all_to_all(v, 'gy', 0, 0, tiled=False)  14.5 us
    pallas_call x1, Pallas kernels, local(): call(centre_kernel, 'vaavsvv', [(cells, 'a'), (cells, 'a'), packed], [cel...  7.73 us
    ppermute x7, starting transfers between devices, local(): parts.append(lax.ppermute(placed, ('gx', 'gy'), routes))  7.1 us
    all_to_all x2, waiting for transfers between devices, local(): swap_x = lambda v: lax.all_to_all(v, 'gx', 0, 0, tiled=False)  4.55 us
  transfers between devices with their start and end apart: 11, of which 5 were waited for; matrix products, arithmetic and copies ran while one was open for 1% of the time, Pallas kernels for 4%

profile of v5, /device:TPU:1, one launch (start us, length us, event | category | flops | bytes accessed | tf_op | source)
XLA Modules:
  0.0 169.9 jit_solution(11432242660335988083)
XLA Ops:
  0.7 4.3 %shard_map.119 = f32[8,2,72,128]{3,2,1,0:T(8,128)} custom-call(f32[16,256,128]{2,1,0:T(8,128)} %bitcast.11, bf16[160,256]{1,0:T(8,128)(2,1)} %constant.21.clone.down_ref), custom_call_target="tpu_custom_call" | custom-call | tf_op jit(solution)/shard_map/pallas_call | solution.py:534
  5.0 17.2 %all_to_all.45.r_ref = f32[8,2,72,128]{3,2,1,0:T(8,128)S(1)} all-to-all(f32[8,2,72,128]{3,2,1,0:T(8,128)} %shard_map.119), channel_id=1, replica_groups=mesh['gx'=8,'gy'=32] {'gx'}, dimensions={0} | all-to-all | bytes 1179648 | tf_op jit(solution)/shard_map/all_to_all | solution.py:516
  22.1 1.3 shard_map.120
  23.4 10.3 %all-to-all-start.1 = ((f32[32,2,8,128]{3,2,1,0:T(8,128)}), f32[32,2,8,128]{3,2,1,0:T(8,128)S(1)}, u32[]{:S(2)}, u32[]{:S(2)}) async-start(f32[32,2,8,128]{3,2,1,0:T(8,128)} %shard_map.120), calls=%async_computation.1 | async-start | bytes 524288 | tf_op jit(solution)/shard_map/all_to_all | solution.py:517
  34.6 8.9 %all-to-all-done.1.v_ref = f32[32,2,8,128]{3,2,1,0:T(8,128)S(1)} async-done(((f32[32,2,8,128]{3,2,1,0:T(8,128)}), f32[32,2,8,128]{3,2,1,0:T(8,128)S(1)}, u32[]{:S(2)}, u32[]{:S(2)}) %all-to-all-start.1) | async-done | bytes 262176 | tf_op jit(solution)/shard_map/all_to_all | solution.py:517
  44.6 15.5 %all_to_all.46.v_ref = f32[32,2,8,128]{3,2,1,0:T(8,128)S(1)} all-to-all(f32[32,2,8,128]{3,2,1,0:T(8,128)S(1)} %get-tuple-element.23), channel_id=1, replica_groups=mesh['gx'=8,'gy'=32] {'gy'}, dimensions={0} | all-to-all | bytes 524288 | tf_op jit(solution)/shard_map/all_to_all | solution.py:517
  60.8 16.4 %all_to_all.47.r_ref = f32[8,2,72,128]{3,2,1,0:T(8,128)S(1)} all-to-all(f32[8,2,72,128]{3,2,1,0:T(8,128)S(1)} %shard_map.123), channel_id=1, replica_groups=mesh['gx'=8,'gy'=32] {'gx'}, dimensions={0} | all-to-all | bytes 1179648 | tf_op jit(solution)/shard_map/all_to_all | solution.py:516
  77.2 7.7 %shard_map.124 = (f32[16,256,128]{2,1,0:T(8,128)}, f32[16,256,128]{2,1,0:T(8,128)}, f32[8,2,72,128]{3,2,1,0:T(8,128)S(1)}) custom-call(f32[8,2,72,128]{3,2,1,0:T(8,128)S(1)} %all_to_all.47.r_ref, f32[16,256,128]{2,1,0:T(8,128)} %bitcast.12, f32[16,256,128]{2,1,0:T(8,128)} %bitcast.14, bf16[128,384]{1,0:T(8,128)(2,1)S(1)} %get-tuple-element.24.w_ref, ...), custom_call_target="tpu_custom_call" | custom-call | tf_op jit(solution)/shard_map/pallas_call | solution.py:540
  85.0 13.5 %all_to_all.48.r_ref = f32[8,2,72,128]{3,2,1,0:T(8,128)S(1)} all-to-all(f32[8,2,72,128]{3,2,1,0:T(8,128)S(1)} %get-tuple-element.26), channel_id=1, replica_groups=mesh['gx'=8,'gy'=32] {'gx'}, dimensions={0} | all-to-all | bytes 1179648 | tf_op jit(solution)/shard_map/all_to_all | solution.py:516
  99.2 13.6 %all_to_all.49.v_ref = f32[32,2,8,128]{3,2,1,0:T(8,128)S(1)} all-to-all(f32[32,2,8,128]{3,2,1,0:T(8,128)S(1)} %get-tuple-element.27), channel_id=1, replica_groups=mesh['gx'=8,'gy'=32] {'gy'}, dimensions={0} | all-to-all | bytes 524288 | tf_op jit(solution)/shard_map/all_to_all | solution.py:517
  112.9 1.6 shard_map.126
  114.4 7.0 %all-to-all-start.6 = ((f32[8,4,8,128]{3,2,1,0:T(8,128)}), f32[8,4,8,128]{3,2,1,0:T(8,128)S(1)}, u32[]{:S(2)}, u32[]{:S(2)}) async-start(f32[8,4,8,128]{3,2,1,0:T(8,128)} %get-tuple-element.31), calls=%async_computation.6 | async-start | bytes 262144 | tf_op jit(solution)/shard_map/all_to_all | solution.py:516
  122.2 4.5 %all-to-all-done.6.g_ref = f32[8,4,8,128]{3,2,1,0:T(8,128)S(1)} async-done(((f32[8,4,8,128]{3,2,1,0:T(8,128)}), f32[8,4,8,128]{3,2,1,0:T(8,128)S(1)}, u32[]{:S(2)}, u32[]{:S(2)}) %all-to-all-start.6) | async-done | bytes 131104 | tf_op jit(solution)/shard_map/all_to_all | solution.py:516
  127.5 4.2 %all-to-all-start.7 = ((f32[32,3,8,128]{3,2,1,0:T(8,128)}), f32[32,3,8,128]{3,2,1,0:T(8,128)S(1)}, u32[]{:S(2)}, u32[]{:S(2)}) async-start(f32[32,3,8,128]{3,2,1,0:T(8,128)} %shard_map.128), calls=%async_computation.7 | async-start | bytes 786432 | tf_op jit(solution)/shard_map/all_to_all | solution.py:517
  131.7 11.1 %all-to-all-done.7.v_ref.m_ref = f32[32,3,8,128]{3,2,1,0:T(8,128)S(1)} async-done(((f32[32,3,8,128]{3,2,1,0:T(8,128)}), f32[32,3,8,128]{3,2,1,0:T(8,128)S(1)}, u32[]{:S(2)}, u32[]{:S(2)}) %all-to-all-start.7) | async-done | bytes 393248 | tf_op jit(solution)/shard_map/all_to_all | solution.py:517
  142.7 1.5 shard_map.129
  144.2 7.9 %all-to-all-start.8 = ((f32[8,2,72,128]{3,2,1,0:T(8,128)}), f32[8,2,72,128]{3,2,1,0:T(8,128)S(1)}, u32[]{:S(2)}, u32[]{:S(2)}) async-start(f32[8,2,72,128]{3,2,1,0:T(8,128)} %get-tuple-element.32), calls=%async_computation.8 | async-start | bytes 1179648 | tf_op jit(solution)/shard_map/all_to_all | solution.py:516
  152.8 1.8 %collective-permute-start.1 = (f32[4,32,256]{2,1,0:T(8,128)S(1)}, f32[4,32,256]{2,1,0:T(8,128)S(1)}, u32[]{:S(2)}, u32[]{:S(2)}) collective-permute-start(f32[4,32,256]{2,1,0:T(8,128)S(1)} %shard_map.131.refs_0_), channel_id=1, source_target_pairs={{0,16},{1,17},{2,18},{3,19},{4,20},{5,21},{6,22},{7,23},{8,24},{9,... | collective-permute-start | bytes 393224 | tf_op jit(solution)/shard_map/ppermute | solution.py:567
  155.3 1.2 collective-permute-start.2
  157.5 1.6 collective-permute-done.refs_1_
  159.6 1.4 collective-permute-done.1.refs_2_
  161.0 2.2 %collective-permute-start.6 = (f32[4,32,256]{2,1,0:T(8,128)S(1)}, f32[4,32,256]{2,1,0:T(8,128)S(1)}, u32[]{:S(2)}, u32[]{:S(2)}) collective-permute-start(f32[4,32,256]{2,1,0:T(8,128)S(1)} %shard_map.131.refs_0_), channel_id=1, source_target_pairs={{0,56},{1,57},{2,58},{3,59},{4,60},{5,61},{6,62},{7,63},{8,32},{9,... | collective-permute-start | bytes 393224 | tf_op jit(solution)/shard_map/ppermute | solution.py:567
  163.7 4.4 %shard_map.130 = f32[16,256,128]{2,1,0:T(8,128)} custom-call(f32[8,2,72,128]{3,2,1,0:T(8,128)S(1)} %all-to-all-done.8.r_ref, f32[16,256,128]{2,1,0:T(8,128)} %get-tuple-element.33.g_hbm, bf16[128,384]{1,0:T(8,128)(2,1)S(1)} %get-tuple-element.34.w_ref, bf16[256,256]{1,0:T(8,128)(2,1)S(1)} %copy-done.2), custom_call_target="tpu_custom_call" | custom-call | tf_op jit(solution)/shard_map/pallas_call | solution.py:556
  168.2 1.6 shard_map.132
  (33 shorter events, 8.2 us)
Async XLA Ops:
  0.6 33.2 %copy-start.1 = (f32[4,16,16,256]{3,2,1,0:T(8,128)S(1)}, f32[4,16,16,256]{3,2,1,0:T(8,128)}, u32[]{:S(2)}) copy-start(f32[4,16,16,256]{3,2,1,0:T(8,128)} %param.10) | copy-start | bytes 3145732
  0.6 33.2 %copy-start.4 = (f32[16,16]{1,0:T(8,128)S(1)}, f32[16,16]{1,0:T(8,128)}, u32[]{:S(2)}) copy-start(f32[16,16]{1,0:T(8,128)} %pw_ref.1) | copy-start | bytes 3076
  4.9 38.5 %copy-start = (f32[256,128]{1,0:T(8,128)S(1)}, f32[256,128]{1,0:T(8,128)}, u32[]{:S(2)}) copy-start(f32[256,128]{1,0:T(8,128)} %constant.20.clone.q_ref) | copy-start | bytes 393220
  23.4 20.0 %all-to-all-start.1 = ((f32[32,2,8,128]{3,2,1,0:T(8,128)}), f32[32,2,8,128]{3,2,1,0:T(8,128)S(1)}, u32[]{:S(2)}, u32[]{:S(2)}) async-start(f32[32,2,8,128]{3,2,1,0:T(8,128)} %shard_map.120), calls=%async_computation.1 | async-start | bytes 524288 | tf_op jit(solution)/shard_map/all_to_all | solution.py:517
  33.8 43.5 %copy-start.2 = (bf16[256,256]{1,0:T(8,128)(2,1)S(1)}, bf16[256,256]{1,0:T(8,128)(2,1)}, u32[]{:S(2)}) copy-start(bf16[256,256]{1,0:T(8,128)(2,1)} %constant.22.clone.up_ref) | copy-start | bytes 393220
  33.8 43.5 %copy-start.3 = (bf16[160,256]{1,0:T(8,128)(2,1)S(1)}, bf16[160,256]{1,0:T(8,128)(2,1)}, u32[]{:S(2)}) copy-start(bf16[160,256]{1,0:T(8,128)(2,1)} %constant.21.clone.down_ref) | copy-start | bytes 245764
  33.8 43.5 %copy-start.5 = (f32[16]{0:T(128)S(1)}, f32[16]{0:T(128)}, u32[]{:S(2)}) copy-start(f32[16]{0:T(128)} %bias_ref.1) | copy-start | bytes 196
  114.4 12.3 %all-to-all-start.6 = ((f32[8,4,8,128]{3,2,1,0:T(8,128)}), f32[8,4,8,128]{3,2,1,0:T(8,128)S(1)}, u32[]{:S(2)}, u32[]{:S(2)}) async-start(f32[8,4,8,128]{3,2,1,0:T(8,128)} %get-tuple-element.31), calls=%async_computation.6 | async-start | bytes 262144 | tf_op jit(solution)/shard_map/all_to_all | solution.py:516
  127.5 15.2 %all-to-all-start.7 = ((f32[32,3,8,128]{3,2,1,0:T(8,128)}), f32[32,3,8,128]{3,2,1,0:T(8,128)S(1)}, u32[]{:S(2)}, u32[]{:S(2)}) async-start(f32[32,3,8,128]{3,2,1,0:T(8,128)} %shard_map.128), calls=%async_computation.7 | async-start | bytes 786432 | tf_op jit(solution)/shard_map/all_to_all | solution.py:517
  144.2 19.6 %all-to-all-start.8 = ((f32[8,2,72,128]{3,2,1,0:T(8,128)}), f32[8,2,72,128]{3,2,1,0:T(8,128)S(1)}, u32[]{:S(2)}, u32[]{:S(2)}) async-start(f32[8,2,72,128]{3,2,1,0:T(8,128)} %get-tuple-element.32), calls=%async_computation.8 | async-start | bytes 1179648 | tf_op jit(solution)/shard_map/all_to_all | solution.py:516
  152.3 6.8 %collective-permute-start = (f32[4,32,256]{2,1,0:T(8,128)S(1)}, f32[4,32,256]{2,1,0:T(8,128)S(1)}, u32[]{:S(2)}, u32[]{:S(2)}) collective-permute-start(f32[4,32,256]{2,1,0:T(8,128)S(1)} %shard_map.131.refs_0_), channel_id=1, source_target_pairs={{0,8},{1,9},{2,10},{3,11},{4,12},{5,13},{6,14},{7,15},{8,16},{9,17... | collective-permute-start | bytes 393224 | tf_op jit(solution)/shard_map/ppermute | solution.py:567
  152.8 8.2 %collective-permute-start.1 = (f32[4,32,256]{2,1,0:T(8,128)S(1)}, f32[4,32,256]{2,1,0:T(8,128)S(1)}, u32[]{:S(2)}, u32[]{:S(2)}) collective-permute-start(f32[4,32,256]{2,1,0:T(8,128)S(1)} %shard_map.131.refs_0_), channel_id=1, source_target_pairs={{0,16},{1,17},{2,18},{3,19},{4,20},{5,21},{6,22},{7,23},{8,24},{9,... | collective-permute-start | bytes 393224 | tf_op jit(solution)/shard_map/ppermute | solution.py:567
  155.3 12.9 %collective-permute-start.2 = (f32[4,32,256]{2,1,0:T(8,128)S(1)}, f32[4,32,256]{2,1,0:T(8,128)S(1)}, u32[]{:S(2)}, u32[]{:S(2)}) collective-permute-start(f32[4,32,256]{2,1,0:T(8,128)S(1)} %shard_map.131.refs_0_), channel_id=1, source_target_pairs={{0,24},{1,25},{2,26},{3,27},{4,28},{5,29},{6,30},{7,31},{8,0},{9,1... | collective-permute-start | bytes 393224 | tf_op jit(solution)/shard_map/ppermute | solution.py:567
  156.5 11.6 %collective-permute-start.3 = (f32[4,32,256]{2,1,0:T(8,128)S(1)}, f32[4,32,256]{2,1,0:T(8,128)S(1)}, u32[]{:S(2)}, u32[]{:S(2)}) collective-permute-start(f32[4,32,256]{2,1,0:T(8,128)S(1)} %shard_map.131.refs_0_), channel_id=1, source_target_pairs={{0,32},{1,33},{2,34},{3,35},{4,36},{5,37},{6,38},{7,39},{8,40},{9,... | collective-permute-start | bytes 393224 | tf_op jit(solution)/shard_map/ppermute | solution.py:567
  157.4 10.7 %collective-permute-start.4 = (f32[4,32,256]{2,1,0:T(8,128)S(1)}, f32[4,32,256]{2,1,0:T(8,128)S(1)}, u32[]{:S(2)}, u32[]{:S(2)}) collective-permute-start(f32[4,32,256]{2,1,0:T(8,128)S(1)} %shard_map.131.refs_0_), channel_id=1, source_target_pairs={{0,40},{1,41},{2,42},{3,43},{4,44},{5,45},{6,46},{7,47},{8,48},{9,... | collective-permute-start | bytes 393224 | tf_op jit(solution)/shard_map/ppermute | solution.py:567
  159.2 9.0 %collective-permute-start.5 = (f32[4,32,256]{2,1,0:T(8,128)S(1)}, f32[4,32,256]{2,1,0:T(8,128)S(1)}, u32[]{:S(2)}, u32[]{:S(2)}) collective-permute-start(f32[4,32,256]{2,1,0:T(8,128)S(1)} %shard_map.131.refs_0_), channel_id=1, source_target_pairs={{0,48},{1,49},{2,50},{3,51},{4,52},{5,53},{6,54},{7,55},{8,56},{9,... | collective-permute-start | bytes 393224 | tf_op jit(solution)/shard_map/ppermute | solution.py:567
  161.0 7.2 %collective-permute-start.6 = (f32[4,32,256]{2,1,0:T(8,128)S(1)}, f32[4,32,256]{2,1,0:T(8,128)S(1)}, u32[]{:S(2)}, u32[]{:S(2)}) collective-permute-start(f32[4,32,256]{2,1,0:T(8,128)S(1)} %shard_map.131.refs_0_), channel_id=1, source_target_pairs={{0,56},{1,57},{2,58},{3,59},{4,60},{5,61},{6,62},{7,63},{8,32},{9,... | collective-permute-start | bytes 393224 | tf_op jit(solution)/shard_map/ppermute | solution.py:567

commit v6 on v5

--- a/solution.py
+++ b/solution.py
@@ -116,30 +116,22 @@
     p_scr[2 * pair + 1] = total[:, 128:256]
 
 
-def pack_planes(p_scr, s_ref):
-    def body(octet, carry):
-        at = pl.ds(pl.multiple_of(octet * 8, 8), 8)
-        for half in range(2):
-            rows = swap_blocks([p_scr[half * 8 + c, at, :] for c in range(8)])
-            for group in range(8):
-                s_ref[group, half, at, :] = rows[group]
-        return carry
-
-    lax.fori_loop(0, 9, body, 0, unroll=True)
-
-
-def unpack_planes(r_ref, d_scr):
-    def body(octet, carry):
-        at = pl.ds(pl.multiple_of(octet * 8, 8), 8)
-        for half in range(2):
-            rows = swap_blocks([r_ref[group, half, at, :] for group in range(8)])
-            for c in range(8):
-                d_scr[half * 8 + c, at, :] = rows[c]
-        return carry
-
-    lax.fori_loop(0, 9, body, 0, unroll=True)
-    for c in range(16):
-        d_scr[c, 72:80, :] = jnp.zeros((8, 128), F32)
+def pack_planes(p_scr, s_ref, half):
+    for octet in range(9):
+        at = slice(octet * 8, octet * 8 + 8)
+        rows = swap_blocks([p_scr[half * 8 + c, at, :] for c in range(8)])
+        for group in range(8):
+            s_ref[group, half, at, :] = rows[group]
+
+
+def unpack_planes(r_ref, d_scr, half):
+    for octet in range(9):
+        at = slice(octet * 8, octet * 8 + 8)
+        rows = swap_blocks([r_ref[group, half, at, :] for group in range(8)])
+        for c in range(8):
+            d_scr[half * 8 + c, at, :] = rows[c]
+    for c in range(8):
+        d_scr[half * 8 + c, 72:80, :] = jnp.zeros((8, 128), F32)
 
 
 def lift_pair(d_scr, pair, up_ref):
@@ -159,7 +151,8 @@
         if pair % 2 == 0:
             copies[pair // 2].wait()
         analyse_pair(f_scr, pair, down_ref, p_scr)
-    pack_planes(p_scr, s_ref)
+        if pair % 4 == 3:
+            pack_planes(p_scr, s_ref, pair // 4)
 
 
 def rows_body(r_ref, l_scr, v_ref):
@@ -371,11 +364,13 @@
     load_cot = pltpu.make_async_copy(cot_hbm, c_scr, sems.at[1])
     load_flow.start()
     load_cot.start()
-    unpack_planes(r_ref, d_scr)
+    unpack_planes(r_ref, d_scr, 0)
     sum_scr[...] = jnp.zeros((128, 128), F32)
     pt_scr[...] = jnp.zeros((128, 128), F32)
     load_flow.wait()
     for pair in range(8):
+        if pair == 1:
+            unpack_planes(r_ref, d_scr, 1)
         change = lift_pair(d_scr, pair, up_ref)
         for k in range(2):
             c = 2 * pair + k
@@ -419,7 +414,8 @@
             stores.append(store)
     for pair in range(8):
         analyse_pair(g_scr, pair, down_ref, p_scr)
-    pack_planes(p_scr, s_ref)
+        if pair % 4 == 3:
+            pack_planes(p_scr, s_ref, pair // 4)
     same_y = iota(128, 128, 0) % 8 == iota(128, 128, 1) % 8
     gather = (iota(16, 128, 1) // 8 == iota(16, 128, 0)).astype(F32)
     fold = (iota(128, 128, 0) // 8 == iota(128, 128, 1) % 16).astype(F32)
@@ -441,9 +437,11 @@
 def finish_kernel(r_ref, g_hbm, w_ref, up_ref, out_hbm, g_scr, v_scr, d_scr, sems):
     load = pltpu.make_async_copy(g_hbm, g_scr, sems.at[0])
     load.start()
-    unpack_planes(r_ref, d_scr)
+    unpack_planes(r_ref, d_scr, 0)
     load.wait()
     for pair in range(8):
+        if pair == 1:
+            unpack_planes(r_ref, d_scr, 1)
         change = lift_pair(d_scr, pair, up_ref)
         for k in range(2):
             v_scr[2 * pair + k] = g_scr[2 * pair + k] + change[:, 128 * k : 128 * k + 128]
@@ -531,7 +529,7 @@
     weights, mix_forward, mix_back = call(weights_kernel, "svv", [square, kron, kron])(
         slab, mode_weights.reshape(4, 256, 256), point_weights
     )
-    (sent,) = call(analyse_kernel, "av", [packed], [cells, parts], 4, 58)(flow_cells, down)
+    (sent,) = call(analyse_kernel, "av", [packed], [cells, parts], 4, 52)(flow_cells, down)
     (got,) = call(rows_kernel, "v", [coefs], rows3)(swap_x(sent))
     back, bands_flow = call(mix_kernel, "vvv", [coefs, square], [(256, 128)])(
         swap_y(got), table, weights

time: 171 us -> 168 us (0.982)
  Pallas kernels: 27.4 us -> 23.8 us
    pallas_call x1, Pallas kernels: 4.28 us -> 2.48 us  [local(): call(analyse_kernel, 'av', [packed], [cells, parts], 4, 52)]
  transfers between devices with their start and end apart: 11 -> 11, of which waited for: 5 -> 5; matrix products, arithmetic and copies ran while one was open for 1% -> 1% of each run, Pallas kernels for 4% -> 3%
where the time goes in v6:
time: 168 us; the launch traced here: 167 us
  blocking collectives  75.3 us (45%)
  starting transfers between devices  37.2 us (22%)
  waiting for transfers between devices  27.6 us (16%)
  Pallas kernels  23.8 us (14%)
    all_to_all x3, blocking collectives, local(): swap_x = lambda v: lax.all_to_all(v, 'gx', 0, 0, tiled=False)  46.1 us
    all_to_all x2, blocking collectives, local(): swap_y = lambda v: lax.all_to_all(v, 'gy', 0, 0, tiled=False)  29.2 us
    all_to_all x2, waiting for transfers between devices, local(): swap_y = lambda v: lax.all_to_all(v, 'gy', 0, 0, tiled=False)  19.9 us
    all_to_all x2, starting transfers between devices, local(): swap_y = lambda v: lax.all_to_all(v, 'gy', 0, 0, tiled=False)  15.2 us
    all_to_all x2, starting transfers between devices, local(): swap_x = lambda v: lax.all_to_all(v, 'gx', 0, 0, tiled=False)  14.9 us
    ppermute x7, starting transfers between devices, local(): parts.append(lax.ppermute(placed, ('gx', 'gy'), routes))  7.1 us
    pallas_call x1, Pallas kernels, local(): call(centre_kernel, 'vaavsvv', [(cells, 'a'), (cells, 'a'), packed], [cel...  6.78 us
    all_to_all x2, waiting for transfers between devices, local(): swap_x = lambda v: lax.all_to_all(v, 'gx', 0, 0, tiled=False)  4.58 us
  transfers between devices with their start and end apart: 11, of which 5 were waited for; matrix products, arithmetic and copies ran while one was open for 1% of the time, Pallas kernels for 3%

profile of v6, /device:TPU:1, one launch (start us, length us, event | category | flops | bytes accessed | tf_op | source)
XLA Modules:
  0.0 167.1 jit_solution(15836422875729604416)
XLA Ops:
  1.5 2.5 %shard_map.119 = f32[8,2,72,128]{3,2,1,0:T(8,128)S(1)} custom-call(f32[16,256,128]{2,1,0:T(8,128)} %bitcast.11, bf16[160,256]{1,0:T(8,128)(2,1)S(1)} %copy-done.3), custom_call_target="tpu_custom_call" | custom-call | tf_op jit(solution)/shard_map/pallas_call | solution.py:532
  4.0 16.3 %all_to_all.45.r_ref = f32[8,2,72,128]{3,2,1,0:T(8,128)S(1)} all-to-all(f32[8,2,72,128]{3,2,1,0:T(8,128)S(1)} %shard_map.119), channel_id=1, replica_groups=mesh['gx'=8,'gy'=32] {'gx'}, dimensions={0} | all-to-all | bytes 1179648 | tf_op jit(solution)/shard_map/all_to_all | solution.py:514
  20.3 1.3 shard_map.120
  21.6 11.0 %all-to-all-start.1 = ((f32[32,2,8,128]{3,2,1,0:T(8,128)}), f32[32,2,8,128]{3,2,1,0:T(8,128)S(1)}, u32[]{:S(2)}, u32[]{:S(2)}) async-start(f32[32,2,8,128]{3,2,1,0:T(8,128)} %shard_map.120), calls=%async_computation.1 | async-start | bytes 524288 | tf_op jit(solution)/shard_map/all_to_all | solution.py:515
  33.4 8.9 %all-to-all-done.1.v_ref = f32[32,2,8,128]{3,2,1,0:T(8,128)S(1)} async-done(((f32[32,2,8,128]{3,2,1,0:T(8,128)}), f32[32,2,8,128]{3,2,1,0:T(8,128)S(1)}, u32[]{:S(2)}, u32[]{:S(2)}) %all-to-all-start.1) | async-done | bytes 262176 | tf_op jit(solution)/shard_map/all_to_all | solution.py:515
  43.5 15.5 %all_to_all.46.v_ref = f32[32,2,8,128]{3,2,1,0:T(8,128)S(1)} all-to-all(f32[32,2,8,128]{3,2,1,0:T(8,128)S(1)} %get-tuple-element.23), channel_id=1, replica_groups=mesh['gx'=8,'gy'=32] {'gy'}, dimensions={0} | all-to-all | bytes 524288 | tf_op jit(solution)/shard_map/all_to_all | solution.py:515
  59.6 16.4 %all_to_all.47.r_ref = f32[8,2,72,128]{3,2,1,0:T(8,128)S(1)} all-to-all(f32[8,2,72,128]{3,2,1,0:T(8,128)S(1)} %shard_map.123), channel_id=1, replica_groups=mesh['gx'=8,'gy'=32] {'gx'}, dimensions={0} | all-to-all | bytes 1179648 | tf_op jit(solution)/shard_map/all_to_all | solution.py:514
  76.1 6.8 %shard_map.124 = (f32[16,256,128]{2,1,0:T(8,128)}, f32[16,256,128]{2,1,0:T(8,128)}, f32[8,2,72,128]{3,2,1,0:T(8,128)S(1)}) custom-call(f32[8,2,72,128]{3,2,1,0:T(8,128)S(1)} %all_to_all.47.r_ref, f32[16,256,128]{2,1,0:T(8,128)} %bitcast.12, f32[16,256,128]{2,1,0:T(8,128)} %bitcast.14, bf16[128,384]{1,0:T(8,128)(2,1)S(1)} %get-tuple-element.24.w_ref, ...), custom_call_target="tpu_custom_call" | custom-call | tf_op jit(solution)/shard_map/pallas_call | solution.py:538
  82.9 13.5 %all_to_all.48.r_ref = f32[8,2,72,128]{3,2,1,0:T(8,128)S(1)} all-to-all(f32[8,2,72,128]{3,2,1,0:T(8,128)S(1)} %get-tuple-element.26), channel_id=1, replica_groups=mesh['gx'=8,'gy'=32] {'gx'}, dimensions={0} | all-to-all | bytes 1179648 | tf_op jit(solution)/shard_map/all_to_all | solution.py:514
  97.1 13.6 %all_to_all.49.v_ref = f32[32,2,8,128]{3,2,1,0:T(8,128)S(1)} all-to-all(f32[32,2,8,128]{3,2,1,0:T(8,128)S(1)} %get-tuple-element.27), channel_id=1, replica_groups=mesh['gx'=8,'gy'=32] {'gy'}, dimensions={0} | all-to-all | bytes 524288 | tf_op jit(solution)/shard_map/all_to_all | solution.py:515
  110.8 1.6 shard_map.126
  112.3 7.0 %all-to-all-start.6 = ((f32[8,4,8,128]{3,2,1,0:T(8,128)}), f32[8,4,8,128]{3,2,1,0:T(8,128)S(1)}, u32[]{:S(2)}, u32[]{:S(2)}) async-start(f32[8,4,8,128]{3,2,1,0:T(8,128)} %get-tuple-element.31), calls=%async_computation.6 | async-start | bytes 262144 | tf_op jit(solution)/shard_map/all_to_all | solution.py:514
  120.0 4.6 %all-to-all-done.6.g_ref = f32[8,4,8,128]{3,2,1,0:T(8,128)S(1)} async-done(((f32[8,4,8,128]{3,2,1,0:T(8,128)}), f32[8,4,8,128]{3,2,1,0:T(8,128)S(1)}, u32[]{:S(2)}, u32[]{:S(2)}) %all-to-all-start.6) | async-done | bytes 131104 | tf_op jit(solution)/shard_map/all_to_all | solution.py:514
  125.4 4.2 %all-to-all-start.7 = ((f32[32,3,8,128]{3,2,1,0:T(8,128)}), f32[32,3,8,128]{3,2,1,0:T(8,128)S(1)}, u32[]{:S(2)}, u32[]{:S(2)}) async-start(f32[32,3,8,128]{3,2,1,0:T(8,128)} %shard_map.128), calls=%async_computation.7 | async-start | bytes 786432 | tf_op jit(solution)/shard_map/all_to_all | solution.py:515
  129.5 11.1 %all-to-all-done.7.v_ref.m_ref = f32[32,3,8,128]{3,2,1,0:T(8,128)S(1)} async-done(((f32[32,3,8,128]{3,2,1,0:T(8,128)}), f32[32,3,8,128]{3,2,1,0:T(8,128)S(1)}, u32[]{:S(2)}, u32[]{:S(2)}) %all-to-all-start.7) | async-done | bytes 393248 | tf_op jit(solution)/shard_map/all_to_all | solution.py:515
  140.6 1.5 shard_map.129
  142.1 7.9 %all-to-all-start.8 = ((f32[8,2,72,128]{3,2,1,0:T(8,128)}), f32[8,2,72,128]{3,2,1,0:T(8,128)S(1)}, u32[]{:S(2)}, u32[]{:S(2)}) async-start(f32[8,2,72,128]{3,2,1,0:T(8,128)} %get-tuple-element.32), calls=%async_computation.8 | async-start | bytes 1179648 | tf_op jit(solution)/shard_map/all_to_all | solution.py:514
  150.7 1.8 %collective-permute-start.1 = (f32[4,32,256]{2,1,0:T(8,128)S(1)}, f32[4,32,256]{2,1,0:T(8,128)S(1)}, u32[]{:S(2)}, u32[]{:S(2)}) collective-permute-start(f32[4,32,256]{2,1,0:T(8,128)S(1)} %shard_map.131.refs_0_), channel_id=1, source_target_pairs={{0,16},{1,17},{2,18},{3,19},{4,20},{5,21},{6,22},{7,23},{8,24},{9,... | collective-permute-start | bytes 393224 | tf_op jit(solution)/shard_map/ppermute | solution.py:565
  153.2 1.2 collective-permute-start.2
  155.4 1.6 collective-permute-done.refs_1_
  157.4 1.4 collective-permute-done.1.refs_2_
  158.9 2.2 %collective-permute-start.6 = (f32[4,32,256]{2,1,0:T(8,128)S(1)}, f32[4,32,256]{2,1,0:T(8,128)S(1)}, u32[]{:S(2)}, u32[]{:S(2)}) collective-permute-start(f32[4,32,256]{2,1,0:T(8,128)S(1)} %shard_map.131.refs_0_), channel_id=1, source_target_pairs={{0,56},{1,57},{2,58},{3,59},{4,60},{5,61},{6,62},{7,63},{8,32},{9,... | collective-permute-start | bytes 393224 | tf_op jit(solution)/shard_map/ppermute | solution.py:565
  161.6 3.6 %shard_map.130 = f32[16,256,128]{2,1,0:T(8,128)} custom-call(f32[8,2,72,128]{3,2,1,0:T(8,128)S(1)} %all-to-all-done.8.r_ref, f32[16,256,128]{2,1,0:T(8,128)} %get-tuple-element.33.g_hbm, bf16[128,384]{1,0:T(8,128)(2,1)S(1)} %get-tuple-element.34.w_ref, bf16[256,256]{1,0:T(8,128)(2,1)S(1)} %copy-done.2), custom_call_target="tpu_custom_call" | custom-call | tf_op jit(solution)/shard_map/pallas_call | solution.py:554
  165.3 1.6 shard_map.132
  (35 shorter events, 9.0 us)
Async XLA Ops:
  0.6 0.9 copy-start.3
  1.5 31.1 %copy-start.1 = (f32[4,16,16,256]{3,2,1,0:T(8,128)S(1)}, f32[4,16,16,256]{3,2,1,0:T(8,128)}, u32[]{:S(2)}) copy-start(f32[4,16,16,256]{3,2,1,0:T(8,128)} %param.10) | copy-start | bytes 3145732
  1.5 31.2 %copy-start.5 = (f32[16,16]{1,0:T(8,128)S(1)}, f32[16,16]{1,0:T(8,128)}, u32[]{:S(2)}) copy-start(f32[16,16]{1,0:T(8,128)} %pw_ref.1) | copy-start | bytes 3076
  4.0 38.3 %copy-start = (f32[256,128]{1,0:T(8,128)S(1)}, f32[256,128]{1,0:T(8,128)}, u32[]{:S(2)}) copy-start(f32[256,128]{1,0:T(8,128)} %constant.20.clone.q_ref) | copy-start | bytes 393220
  21.6 20.7 %all-to-all-start.1 = ((f32[32,2,8,128]{3,2,1,0:T(8,128)}), f32[32,2,8,128]{3,2,1,0:T(8,128)S(1)}, u32[]{:S(2)}, u32[]{:S(2)}) async-start(f32[32,2,8,128]{3,2,1,0:T(8,128)} %shard_map.120), calls=%async_computation.1 | async-start | bytes 524288 | tf_op jit(solution)/shard_map/all_to_all | solution.py:515
  32.6 43.4 %copy-start.2 = (bf16[256,256]{1,0:T(8,128)(2,1)S(1)}, bf16[256,256]{1,0:T(8,128)(2,1)}, u32[]{:S(2)}) copy-start(bf16[256,256]{1,0:T(8,128)(2,1)} %constant.22.clone.up_ref) | copy-start | bytes 393220
  32.6 43.4 %copy-start.4 = (bf16[160,256]{1,0:T(8,128)(2,1)S(1)}, bf16[160,256]{1,0:T(8,128)(2,1)}, u32[]{:S(2)}) copy-start(bf16[160,256]{1,0:T(8,128)(2,1)} %constant.21.clone.down_ref) | copy-start | bytes 245764
  32.6 43.4 %copy-start.6 = (f32[16]{0:T(128)S(1)}, f32[16]{0:T(128)}, u32[]{:S(2)}) copy-start(f32[16]{0:T(128)} %bias_ref.1) | copy-start | bytes 196
  112.3 12.3 %all-to-all-start.6 = ((f32[8,4,8,128]{3,2,1,0:T(8,128)}), f32[8,4,8,128]{3,2,1,0:T(8,128)S(1)}, u32[]{:S(2)}, u32[]{:S(2)}) async-start(f32[8,4,8,128]{3,2,1,0:T(8,128)} %get-tuple-element.31), calls=%async_computation.6 | async-start | bytes 262144 | tf_op jit(solution)/shard_map/all_to_all | solution.py:514
  125.4 15.2 %all-to-all-start.7 = ((f32[32,3,8,128]{3,2,1,0:T(8,128)}), f32[32,3,8,128]{3,2,1,0:T(8,128)S(1)}, u32[]{:S(2)}, u32[]{:S(2)}) async-start(f32[32,3,8,128]{3,2,1,0:T(8,128)} %shard_map.128), calls=%async_computation.7 | async-start | bytes 786432 | tf_op jit(solution)/shard_map/all_to_all | solution.py:515
  142.1 19.6 %all-to-all-start.8 = ((f32[8,2,72,128]{3,2,1,0:T(8,128)}), f32[8,2,72,128]{3,2,1,0:T(8,128)S(1)}, u32[]{:S(2)}, u32[]{:S(2)}) async-start(f32[8,2,72,128]{3,2,1,0:T(8,128)} %get-tuple-element.32), calls=%async_computation.8 | async-start | bytes 1179648 | tf_op jit(solution)/shard_map/all_to_all | solution.py:514
  150.2 6.8 %collective-permute-start = (f32[4,32,256]{2,1,0:T(8,128)S(1)}, f32[4,32,256]{2,1,0:T(8,128)S(1)}, u32[]{:S(2)}, u32[]{:S(2)}) collective-permute-start(f32[4,32,256]{2,1,0:T(8,128)S(1)} %shard_map.131.refs_0_), channel_id=1, source_target_pairs={{0,8},{1,9},{2,10},{3,11},{4,12},{5,13},{6,14},{7,15},{8,16},{9,17... | collective-permute-start | bytes 393224 | tf_op jit(solution)/shard_map/ppermute | solution.py:565
  150.7 8.2 %collective-permute-start.1 = (f32[4,32,256]{2,1,0:T(8,128)S(1)}, f32[4,32,256]{2,1,0:T(8,128)S(1)}, u32[]{:S(2)}, u32[]{:S(2)}) collective-permute-start(f32[4,32,256]{2,1,0:T(8,128)S(1)} %shard_map.131.refs_0_), channel_id=1, source_target_pairs={{0,16},{1,17},{2,18},{3,19},{4,20},{5,21},{6,22},{7,23},{8,24},{9,... | collective-permute-start | bytes 393224 | tf_op jit(solution)/shard_map/ppermute | solution.py:565
  153.2 12.1 %collective-permute-start.2 = (f32[4,32,256]{2,1,0:T(8,128)S(1)}, f32[4,32,256]{2,1,0:T(8,128)S(1)}, u32[]{:S(2)}, u32[]{:S(2)}) collective-permute-start(f32[4,32,256]{2,1,0:T(8,128)S(1)} %shard_map.131.refs_0_), channel_id=1, source_target_pairs={{0,24},{1,25},{2,26},{3,27},{4,28},{5,29},{6,30},{7,31},{8,0},{9,1... | collective-permute-start | bytes 393224 | tf_op jit(solution)/shard_map/ppermute | solution.py:565
  154.4 10.9 %collective-permute-start.3 = (f32[4,32,256]{2,1,0:T(8,128)S(1)}, f32[4,32,256]{2,1,0:T(8,128)S(1)}, u32[]{:S(2)}, u32[]{:S(2)}) collective-permute-start(f32[4,32,256]{2,1,0:T(8,128)S(1)} %shard_map.131.refs_0_), channel_id=1, source_target_pairs={{0,32},{1,33},{2,34},{3,35},{4,36},{5,37},{6,38},{7,39},{8,40},{9,... | collective-permute-start | bytes 393224 | tf_op jit(solution)/shard_map/ppermute | solution.py:565
  155.3 10.0 %collective-permute-start.4 = (f32[4,32,256]{2,1,0:T(8,128)S(1)}, f32[4,32,256]{2,1,0:T(8,128)S(1)}, u32[]{:S(2)}, u32[]{:S(2)}) collective-permute-start(f32[4,32,256]{2,1,0:T(8,128)S(1)} %shard_map.131.refs_0_), channel_id=1, source_target_pairs={{0,40},{1,41},{2,42},{3,43},{4,44},{5,45},{6,46},{7,47},{8,48},{9,... | collective-permute-start | bytes 393224 | tf_op jit(solution)/shard_map/ppermute | solution.py:565
  157.1 8.2 %collective-permute-start.5 = (f32[4,32,256]{2,1,0:T(8,128)S(1)}, f32[4,32,256]{2,1,0:T(8,128)S(1)}, u32[]{:S(2)}, u32[]{:S(2)}) collective-permute-start(f32[4,32,256]{2,1,0:T(8,128)S(1)} %shard_map.131.refs_0_), channel_id=1, source_target_pairs={{0,48},{1,49},{2,50},{3,51},{4,52},{5,53},{6,54},{7,55},{8,56},{9,... | collective-permute-start | bytes 393224 | tf_op jit(solution)/shard_map/ppermute | solution.py:565
  158.9 6.4 %collective-permute-start.6 = (f32[4,32,256]{2,1,0:T(8,128)S(1)}, f32[4,32,256]{2,1,0:T(8,128)S(1)}, u32[]{:S(2)}, u32[]{:S(2)}) collective-permute-start(f32[4,32,256]{2,1,0:T(8,128)S(1)} %shard_map.131.refs_0_), channel_id=1, source_target_pairs={{0,56},{1,57},{2,58},{3,59},{4,60},{5,61},{6,62},{7,63},{8,32},{9,... | collective-permute-start | bytes 393224 | tf_op jit(solution)/shard_map/ppermute | solution.py:565

commit v7 on v6

--- a/solution.py
+++ b/solution.py
@@ -37,6 +37,7 @@
 HIGHEST = lax.Precision.HIGHEST
 F32 = jnp.float32
 BF16 = jnp.bfloat16
+MODE_ROUTES = [(1, 0), (0, 1), (0, 2), (1, 2), (0, 3), (1, 3), (1, 1)]
 
 
 def cell_tables():
@@ -481,13 +482,11 @@
 def gather_kernel(index_ref, *refs):
     parts, out_hbm, sems = refs[:8], refs[8], refs[9]
     copies = []
-    for flip in range(2):
-        for shift in range(4):
-            core = (index_ref[1] + flip) % 2
-            owner = core * 4 + (index_ref[0] // 8 + 4 - shift) % 4
-            to = out_hbm.at[:, pl.ds(pl.multiple_of(owner * 32, 32), 32), :]
-            k = flip * 4 + shift
-            copies.append(pltpu.make_async_copy(parts[k], to, sems.at[k]))
+    for k, (flip, shift) in enumerate(MODE_ROUTES + [(0, 0)]):
+        core = (index_ref[1] + flip) % 2
+        owner = core * 4 + (index_ref[0] // 8 + 4 - shift) % 4
+        to = out_hbm.at[:, pl.ds(pl.multiple_of(owner * 32, 32), 32), :]
+        copies.append(pltpu.make_async_copy(parts[k], to, sems.at[k]))
     for copy in copies:
         copy.start()
     for copy in copies:
@@ -555,8 +554,8 @@
         finish_kernel, "vavv", [(cells, "a")], [cells] * 2 + [parts], 5, 52
     )(swap_x(spread), grads, mix_back, up)
     (placed,) = call(modes_place_kernel, "v", [((4, 32, 256), "v")])(joined)
-    parts = [placed]
-    for flip, shift in [(f, k) for f in range(2) for k in range(4)][1:]:
+    parts = []
+    for flip, shift in MODE_ROUTES:
         routes = [
             (i * 32 + j, (i ^ flip) * 32 + (j + 8 * shift) % 32)
             for i in range(8)
@@ -566,7 +565,9 @@
     place, grad_field = lax.optimization_barrier(
         (jnp.stack([lax.axis_index("gy"), lax.axis_index("gx")]).astype(jnp.int32), grad_field)
     )
-    (modes,) = call(gather_kernel, "s" + "a" * 8, [((4, 256, 256), "a")], (), 8)(place, *parts)
+    (modes,) = call(gather_kernel, "s" + "a" * 8, [((4, 256, 256), "a")], (), 8)(
+        place, *parts, placed
+    )
 
     cell_count = flow_field.shape[3] * 256 * 256
     return (

time: 168 us -> 170 us (1.012)
  no operation moved by 1% of the time
where the time goes in v7:
time: 170 us; the launch traced here: 168 us
  blocking collectives  75.3 us (44%)
  starting transfers between devices  38.5 us (23%)
  waiting for transfers between devices  27.5 us (16%)
  Pallas kernels  23.8 us (14%)
    all_to_all x3, blocking collectives, local(): swap_x = lambda v: lax.all_to_all(v, 'gx', 0, 0, tiled=False)  46.1 us
    all_to_all x2, blocking collectives, local(): swap_y = lambda v: lax.all_to_all(v, 'gy', 0, 0, tiled=False)  29.2 us
    all_to_all x2, waiting for transfers between devices, local(): swap_y = lambda v: lax.all_to_all(v, 'gy', 0, 0, tiled=False)  19.9 us
    all_to_all x2, starting transfers between devices, local(): swap_y = lambda v: lax.all_to_all(v, 'gy', 0, 0, tiled=False)  15.2 us
    all_to_all x2, starting transfers between devices, local(): swap_x = lambda v: lax.all_to_all(v, 'gx', 0, 0, tiled=False)  14.9 us
    ppermute x7, starting transfers between devices, local(): parts.append(lax.ppermute(placed, ('gx', 'gy'), routes))  8.43 us
    pallas_call x1, Pallas kernels, local(): call(centre_kernel, 'vaavsvv', [(cells, 'a'), (cells, 'a'), packed], [cel...  6.78 us
    all_to_all x2, waiting for transfers between devices, local(): swap_x = lambda v: lax.all_to_all(v, 'gx', 0, 0, tiled=False)  4.89 us
  transfers between devices with their start and end apart: 11, of which 5 were waited for; matrix products, arithmetic and copies ran while one was open for 1% of the time, Pallas kernels for 3%

profile of v7, /device:TPU:1, one launch (start us, length us, event | category | flops | bytes accessed | tf_op | source)
XLA Modules:
  0.0 168.3 jit_solution(767324711762938518)
XLA Ops:
  1.5 2.5 %shard_map.119 = f32[8,2,72,128]{3,2,1,0:T(8,128)S(1)} custom-call(f32[16,256,128]{2,1,0:T(8,128)} %bitcast.11, bf16[160,256]{1,0:T(8,128)(2,1)S(1)} %copy-done.3), custom_call_target="tpu_custom_call" | custom-call | tf_op jit(solution)/shard_map/pallas_call | solution.py:531
  4.0 16.3 %all_to_all.45.r_ref = f32[8,2,72,128]{3,2,1,0:T(8,128)S(1)} all-to-all(f32[8,2,72,128]{3,2,1,0:T(8,128)S(1)} %shard_map.119), channel_id=1, replica_groups=mesh['gx'=8,'gy'=32] {'gx'}, dimensions={0} | all-to-all | bytes 1179648 | tf_op jit(solution)/shard_map/all_to_all | solution.py:513
  20.3 1.3 shard_map.120
  21.6 11.0 %all-to-all-start.1 = ((f32[32,2,8,128]{3,2,1,0:T(8,128)}), f32[32,2,8,128]{3,2,1,0:T(8,128)S(1)}, u32[]{:S(2)}, u32[]{:S(2)}) async-start(f32[32,2,8,128]{3,2,1,0:T(8,128)} %shard_map.120), calls=%async_computation.1 | async-start | bytes 524288 | tf_op jit(solution)/shard_map/all_to_all | solution.py:514
  33.4 8.9 %all-to-all-done.1.v_ref = f32[32,2,8,128]{3,2,1,0:T(8,128)S(1)} async-done(((f32[32,2,8,128]{3,2,1,0:T(8,128)}), f32[32,2,8,128]{3,2,1,0:T(8,128)S(1)}, u32[]{:S(2)}, u32[]{:S(2)}) %all-to-all-start.1) | async-done | bytes 262176 | tf_op jit(solution)/shard_map/all_to_all | solution.py:514
  43.5 15.5 %all_to_all.46.v_ref = f32[32,2,8,128]{3,2,1,0:T(8,128)S(1)} all-to-all(f32[32,2,8,128]{3,2,1,0:T(8,128)S(1)} %get-tuple-element.23), channel_id=1, replica_groups=mesh['gx'=8,'gy'=32] {'gy'}, dimensions={0} | all-to-all | bytes 524288 | tf_op jit(solution)/shard_map/all_to_all | solution.py:514
  59.6 16.4 %all_to_all.47.r_ref = f32[8,2,72,128]{3,2,1,0:T(8,128)S(1)} all-to-all(f32[8,2,72,128]{3,2,1,0:T(8,128)S(1)} %shard_map.123), channel_id=1, replica_groups=mesh['gx'=8,'gy'=32] {'gx'}, dimensions={0} | all-to-all | bytes 1179648 | tf_op jit(solution)/shard_map/all_to_all | solution.py:513
  76.1 6.8 %shard_map.124 = (f32[16,256,128]{2,1,0:T(8,128)}, f32[16,256,128]{2,1,0:T(8,128)}, f32[8,2,72,128]{3,2,1,0:T(8,128)S(1)}) custom-call(f32[8,2,72,128]{3,2,1,0:T(8,128)S(1)} %all_to_all.47.r_ref, f32[16,256,128]{2,1,0:T(8,128)} %bitcast.12, f32[16,256,128]{2,1,0:T(8,128)} %bitcast.14, bf16[128,384]{1,0:T(8,128)(2,1)S(1)} %get-tuple-element.24.w_ref, ...), custom_call_target="tpu_custom_call" | custom-call | tf_op jit(solution)/shard_map/pallas_call | solution.py:537
  82.9 13.5 %all_to_all.48.r_ref = f32[8,2,72,128]{3,2,1,0:T(8,128)S(1)} all-to-all(f32[8,2,72,128]{3,2,1,0:T(8,128)S(1)} %get-tuple-element.26), channel_id=1, replica_groups=mesh['gx'=8,'gy'=32] {'gx'}, dimensions={0} | all-to-all | bytes 1179648 | tf_op jit(solution)/shard_map/all_to_all | solution.py:513
  97.1 13.6 %all_to_all.49.v_ref = f32[32,2,8,128]{3,2,1,0:T(8,128)S(1)} all-to-all(f32[32,2,8,128]{3,2,1,0:T(8,128)S(1)} %get-tuple-element.27), channel_id=1, replica_groups=mesh['gx'=8,'gy'=32] {'gy'}, dimensions={0} | all-to-all | bytes 524288 | tf_op jit(solution)/shard_map/all_to_all | solution.py:514
  110.8 1.6 shard_map.126
  112.3 7.0 %all-to-all-start.6 = ((f32[8,4,8,128]{3,2,1,0:T(8,128)}), f32[8,4,8,128]{3,2,1,0:T(8,128)S(1)}, u32[]{:S(2)}, u32[]{:S(2)}) async-start(f32[8,4,8,128]{3,2,1,0:T(8,128)} %get-tuple-element.31), calls=%async_computation.6 | async-start | bytes 262144 | tf_op jit(solution)/shard_map/all_to_all | solution.py:513
  120.0 4.6 %all-to-all-done.6.g_ref = f32[8,4,8,128]{3,2,1,0:T(8,128)S(1)} async-done(((f32[8,4,8,128]{3,2,1,0:T(8,128)}), f32[8,4,8,128]{3,2,1,0:T(8,128)S(1)}, u32[]{:S(2)}, u32[]{:S(2)}) %all-to-all-start.6) | async-done | bytes 131104 | tf_op jit(solution)/shard_map/all_to_all | solution.py:513
  125.4 4.2 %all-to-all-start.7 = ((f32[32,3,8,128]{3,2,1,0:T(8,128)}), f32[32,3,8,128]{3,2,1,0:T(8,128)S(1)}, u32[]{:S(2)}, u32[]{:S(2)}) async-start(f32[32,3,8,128]{3,2,1,0:T(8,128)} %shard_map.128), calls=%async_computation.7 | async-start | bytes 786432 | tf_op jit(solution)/shard_map/all_to_all | solution.py:514
  129.5 11.1 %all-to-all-done.7.v_ref.m_ref = f32[32,3,8,128]{3,2,1,0:T(8,128)S(1)} async-done(((f32[32,3,8,128]{3,2,1,0:T(8,128)}), f32[32,3,8,128]{3,2,1,0:T(8,128)S(1)}, u32[]{:S(2)}, u32[]{:S(2)}) %all-to-all-start.7) | async-done | bytes 393248 | tf_op jit(solution)/shard_map/all_to_all | solution.py:514
  140.6 1.5 shard_map.129
  142.1 7.9 %all-to-all-start.8 = ((f32[8,2,72,128]{3,2,1,0:T(8,128)}), f32[8,2,72,128]{3,2,1,0:T(8,128)S(1)}, u32[]{:S(2)}, u32[]{:S(2)}) async-start(f32[8,2,72,128]{3,2,1,0:T(8,128)} %get-tuple-element.32), calls=%async_computation.8 | async-start | bytes 1179648 | tf_op jit(solution)/shard_map/all_to_all | solution.py:513
  151.4 1.8 %collective-permute-start.2 = (f32[4,32,256]{2,1,0:T(8,128)S(1)}, f32[4,32,256]{2,1,0:T(8,128)S(1)}, u32[]{:S(2)}, u32[]{:S(2)}) collective-permute-start(f32[4,32,256]{2,1,0:T(8,128)S(1)} %shard_map.131.refs_7_), channel_id=1, source_target_pairs={{0,16},{1,17},{2,18},{3,19},{4,20},{5,21},{6,22},{7,23},{8,24},{9,... | collective-permute-start | bytes 393224 | tf_op jit(solution)/shard_map/ppermute | solution.py:564
  153.2 2.0 %collective-permute-start.3 = (f32[4,32,256]{2,1,0:T(8,128)S(1)}, f32[4,32,256]{2,1,0:T(8,128)S(1)}, u32[]{:S(2)}, u32[]{:S(2)}) collective-permute-start(f32[4,32,256]{2,1,0:T(8,128)S(1)} %shard_map.131.refs_7_), channel_id=1, source_target_pairs={{0,48},{1,49},{2,50},{3,51},{4,52},{5,53},{6,54},{7,55},{8,56},{9,... | collective-permute-start | bytes 393224 | tf_op jit(solution)/shard_map/ppermute | solution.py:564
  155.2 2.4 %collective-permute-start.4 = (f32[4,32,256]{2,1,0:T(8,128)S(1)}, f32[4,32,256]{2,1,0:T(8,128)S(1)}, u32[]{:S(2)}, u32[]{:S(2)}) collective-permute-start(f32[4,32,256]{2,1,0:T(8,128)S(1)} %shard_map.131.refs_7_), channel_id=1, source_target_pairs={{0,24},{1,25},{2,26},{3,27},{4,28},{5,29},{6,30},{7,31},{8,0},{9,1... | collective-permute-start | bytes 393224 | tf_op jit(solution)/shard_map/ppermute | solution.py:564
  157.6 1.7 %collective-permute-start.6 = (f32[4,32,256]{2,1,0:T(8,128)S(1)}, f32[4,32,256]{2,1,0:T(8,128)S(1)}, u32[]{:S(2)}, u32[]{:S(2)}) collective-permute-start(f32[4,32,256]{2,1,0:T(8,128)S(1)} %shard_map.131.refs_7_), channel_id=1, source_target_pairs={{0,40},{1,41},{2,42},{3,43},{4,44},{5,45},{6,46},{7,47},{8,48},{9,... | collective-permute-start | bytes 393224 | tf_op jit(solution)/shard_map/ppermute | solution.py:564
  160.2 3.6 %shard_map.130 = f32[16,256,128]{2,1,0:T(8,128)} custom-call(f32[8,2,72,128]{3,2,1,0:T(8,128)S(1)} %all-to-all-done.8.r_ref, f32[16,256,128]{2,1,0:T(8,128)} %get-tuple-element.33.g_hbm, bf16[128,384]{1,0:T(8,128)(2,1)S(1)} %get-tuple-element.34.w_ref, bf16[256,256]{1,0:T(8,128)(2,1)S(1)} %copy-done.2), custom_call_target="tpu_custom_call" | custom-call | tf_op jit(solution)/shard_map/pallas_call | solution.py:553
  163.9 2.7 %collective-permute-done.5.refs_5_ = f32[4,32,256]{2,1,0:T(8,128)S(1)} collective-permute-done((f32[4,32,256]{2,1,0:T(8,128)S(1)}, f32[4,32,256]{2,1,0:T(8,128)S(1)}, u32[]{:S(2)}, u32[]{:S(2)}) %collective-permute-start.5) | collective-permute-done | bytes 131104 | tf_op jit(solution)/shard_map/ppermute | solution.py:564
  166.6 1.6 shard_map.132
  (35 shorter events, 8.0 us)
Async XLA Ops:
  0.6 0.9 copy-start.3
  1.5 31.1 %copy-start.1 = (f32[4,16,16,256]{3,2,1,0:T(8,128)S(1)}, f32[4,16,16,256]{3,2,1,0:T(8,128)}, u32[]{:S(2)}) copy-start(f32[4,16,16,256]{3,2,1,0:T(8,128)} %param.10) | copy-start | bytes 3145732
  1.5 31.2 %copy-start.5 = (f32[16,16]{1,0:T(8,128)S(1)}, f32[16,16]{1,0:T(8,128)}, u32[]{:S(2)}) copy-start(f32[16,16]{1,0:T(8,128)} %pw_ref.1) | copy-start | bytes 3076
  4.0 38.3 %copy-start = (f32[256,128]{1,0:T(8,128)S(1)}, f32[256,128]{1,0:T(8,128)}, u32[]{:S(2)}) copy-start(f32[256,128]{1,0:T(8,128)} %constant.20.clone.q_ref) | copy-start | bytes 393220
  21.6 20.7 %all-to-all-start.1 = ((f32[32,2,8,128]{3,2,1,0:T(8,128)}), f32[32,2,8,128]{3,2,1,0:T(8,128)S(1)}, u32[]{:S(2)}, u32[]{:S(2)}) async-start(f32[32,2,8,128]{3,2,1,0:T(8,128)} %shard_map.120), calls=%async_computation.1 | async-start | bytes 524288 | tf_op jit(solution)/shard_map/all_to_all | solution.py:514
  32.6 43.4 %copy-start.2 = (bf16[256,256]{1,0:T(8,128)(2,1)S(1)}, bf16[256,256]{1,0:T(8,128)(2,1)}, u32[]{:S(2)}) copy-start(bf16[256,256]{1,0:T(8,128)(2,1)} %constant.22.clone.up_ref) | copy-start | bytes 393220
  32.6 43.4 %copy-start.4 = (bf16[160,256]{1,0:T(8,128)(2,1)S(1)}, bf16[160,256]{1,0:T(8,128)(2,1)}, u32[]{:S(2)}) copy-start(bf16[160,256]{1,0:T(8,128)(2,1)} %constant.21.clone.down_ref) | copy-start | bytes 245764
  32.6 43.4 %copy-start.6 = (f32[16]{0:T(128)S(1)}, f32[16]{0:T(128)}, u32[]{:S(2)}) copy-start(f32[16]{0:T(128)} %bias_ref.1) | copy-start | bytes 196
  112.3 12.3 %all-to-all-start.6 = ((f32[8,4,8,128]{3,2,1,0:T(8,128)}), f32[8,4,8,128]{3,2,1,0:T(8,128)S(1)}, u32[]{:S(2)}, u32[]{:S(2)}) async-start(f32[8,4,8,128]{3,2,1,0:T(8,128)} %get-tuple-element.31), calls=%async_computation.6 | async-start | bytes 262144 | tf_op jit(solution)/shard_map/all_to_all | solution.py:513
  125.4 15.2 %all-to-all-start.7 = ((f32[32,3,8,128]{3,2,1,0:T(8,128)}), f32[32,3,8,128]{3,2,1,0:T(8,128)S(1)}, u32[]{:S(2)}, u32[]{:S(2)}) async-start(f32[32,3,8,128]{3,2,1,0:T(8,128)} %shard_map.128), calls=%async_computation.7 | async-start | bytes 786432 | tf_op jit(solution)/shard_map/all_to_all | solution.py:514
  142.1 18.1 %all-to-all-start.8 = ((f32[8,2,72,128]{3,2,1,0:T(8,128)}), f32[8,2,72,128]{3,2,1,0:T(8,128)S(1)}, u32[]{:S(2)}, u32[]{:S(2)}) async-start(f32[8,2,72,128]{3,2,1,0:T(8,128)} %get-tuple-element.32), calls=%async_computation.8 | async-start | bytes 1179648 | tf_op jit(solution)/shard_map/all_to_all | solution.py:513
  150.2 7.4 %collective-permute-start = (f32[4,32,256]{2,1,0:T(8,128)S(1)}, f32[4,32,256]{2,1,0:T(8,128)S(1)}, u32[]{:S(2)}, u32[]{:S(2)}) collective-permute-start(f32[4,32,256]{2,1,0:T(8,128)S(1)} %shard_map.131.refs_7_), channel_id=1, source_target_pairs={{0,32},{1,33},{2,34},{3,35},{4,36},{5,37},{6,38},{7,39},{8,40},{9,... | collective-permute-start | bytes 393224 | tf_op jit(solution)/shard_map/ppermute | solution.py:564
  150.4 7.2 %collective-permute-start.1 = (f32[4,32,256]{2,1,0:T(8,128)S(1)}, f32[4,32,256]{2,1,0:T(8,128)S(1)}, u32[]{:S(2)}, u32[]{:S(2)}) collective-permute-start(f32[4,32,256]{2,1,0:T(8,128)S(1)} %shard_map.131.refs_7_), channel_id=1, source_target_pairs={{0,8},{1,9},{2,10},{3,11},{4,12},{5,13},{6,14},{7,15},{8,16},{9,17... | collective-permute-start | bytes 393224 | tf_op jit(solution)/shard_map/ppermute | solution.py:564
  151.4 12.4 %collective-permute-start.2 = (f32[4,32,256]{2,1,0:T(8,128)S(1)}, f32[4,32,256]{2,1,0:T(8,128)S(1)}, u32[]{:S(2)}, u32[]{:S(2)}) collective-permute-start(f32[4,32,256]{2,1,0:T(8,128)S(1)} %shard_map.131.refs_7_), channel_id=1, source_target_pairs={{0,16},{1,17},{2,18},{3,19},{4,20},{5,21},{6,22},{7,23},{8,24},{9,... | collective-permute-start | bytes 393224 | tf_op jit(solution)/shard_map/ppermute | solution.py:564
  153.2 10.6 %collective-permute-start.3 = (f32[4,32,256]{2,1,0:T(8,128)S(1)}, f32[4,32,256]{2,1,0:T(8,128)S(1)}, u32[]{:S(2)}, u32[]{:S(2)}) collective-permute-start(f32[4,32,256]{2,1,0:T(8,128)S(1)} %shard_map.131.refs_7_), channel_id=1, source_target_pairs={{0,48},{1,49},{2,50},{3,51},{4,52},{5,53},{6,54},{7,55},{8,56},{9,... | collective-permute-start | bytes 393224 | tf_op jit(solution)/shard_map/ppermute | solution.py:564
  155.2 8.6 %collective-permute-start.4 = (f32[4,32,256]{2,1,0:T(8,128)S(1)}, f32[4,32,256]{2,1,0:T(8,128)S(1)}, u32[]{:S(2)}, u32[]{:S(2)}) collective-permute-start(f32[4,32,256]{2,1,0:T(8,128)S(1)} %shard_map.131.refs_7_), channel_id=1, source_target_pairs={{0,24},{1,25},{2,26},{3,27},{4,28},{5,29},{6,30},{7,31},{8,0},{9,1... | collective-permute-start | bytes 393224 | tf_op jit(solution)/shard_map/ppermute | solution.py:564
  157.6 8.9 %collective-permute-start.5 = (f32[4,32,256]{2,1,0:T(8,128)S(1)}, f32[4,32,256]{2,1,0:T(8,128)S(1)}, u32[]{:S(2)}, u32[]{:S(2)}) collective-permute-start(f32[4,32,256]{2,1,0:T(8,128)S(1)} %shard_map.131.refs_7_), channel_id=1, source_target_pairs={{0,56},{1,57},{2,58},{3,59},{4,60},{5,61},{6,62},{7,63},{8,32},{9,... | collective-permute-start | bytes 393224 | tf_op jit(solution)/shard_map/ppermute | solution.py:564
  157.6 8.9 %collective-permute-start.6 = (f32[4,32,256]{2,1,0:T(8,128)S(1)}, f32[4,32,256]{2,1,0:T(8,128)S(1)}, u32[]{:S(2)}, u32[]{:S(2)}) collective-permute-start(f32[4,32,256]{2,1,0:T(8,128)S(1)} %shard_map.131.refs_7_), channel_id=1, source_target_pairs={{0,40},{1,41},{2,42},{3,43},{4,44},{5,45},{6,46},{7,47},{8,48},{9,... | collective-permute-start | bytes 393224 | tf_op jit(solution)/shard_map/ppermute | solution.py:564

commit v8 on v7

--- a/solution.py
+++ b/solution.py
@@ -37,7 +37,7 @@
 HIGHEST = lax.Precision.HIGHEST
 F32 = jnp.float32
 BF16 = jnp.bfloat16
-MODE_ROUTES = [(1, 0), (0, 1), (0, 2), (1, 2), (0, 3), (1, 3), (1, 1)]
+MODE_ROUTES = [(0, 1), (0, 2), (0, 3), (1, 0), (1, 1), (1, 2), (1, 3)]
 
 
 def cell_tables():
@@ -554,14 +554,12 @@
         finish_kernel, "vavv", [(cells, "a")], [cells] * 2 + [parts], 5, 52
     )(swap_x(spread), grads, mix_back, up)
     (placed,) = call(modes_place_kernel, "v", [((4, 32, 256), "v")])(joined)
-    parts = []
-    for flip, shift in MODE_ROUTES:
-        routes = [
-            (i * 32 + j, (i ^ flip) * 32 + (j + 8 * shift) % 32)
-            for i in range(8)
-            for j in range(32)
-        ]
-        parts.append(lax.ppermute(placed, ("gx", "gy"), routes))
+    parts = [placed]
+    for shift in (1, 2, 3):
+        routes = [(j, (j + 8 * shift) % 32) for j in range(32)]
+        parts.append(lax.ppermute(placed, "gy", routes))
+    parts += [lax.ppermute(part, "gx", [(i, i ^ 1) for i in range(8)]) for part in parts]
+    parts = parts[1:]
     place, grad_field = lax.optimization_barrier(
         (jnp.stack([lax.axis_index("gy"), lax.axis_index("gx")]).astype(jnp.int32), grad_field)
     )

time: 170 us -> 167 us (0.982)
  transfers between devices with their start and end apart: 11 -> 11, of which waited for: 5 -> 4; matrix products, arithmetic and copies ran while one was open for 1% -> 1% of each run, Pallas kernels for 3% -> 3%
where the time goes in v8:
time: 167 us
  blocking collectives  75.3 us (45%)
  starting transfers between devices  38.3 us (23%)
  waiting for transfers between devices  26.3 us (16%)
  Pallas kernels  23.8 us (14%)
    all_to_all x3, blocking collectives, local(): swap_x = lambda v: lax.all_to_all(v, 'gx', 0, 0, tiled=False)  46.1 us
    all_to_all x2, blocking collectives, local(): swap_y = lambda v: lax.all_to_all(v, 'gy', 0, 0, tiled=False)  29.2 us
    all_to_all x2, waiting for transfers between devices, local(): swap_y = lambda v: lax.all_to_all(v, 'gy', 0, 0, tiled=False)  19.9 us
    all_to_all x2, starting transfers between devices, local(): swap_y = lambda v: lax.all_to_all(v, 'gy', 0, 0, tiled=False)  15.2 us
    all_to_all x2, starting transfers between devices, local(): swap_x = lambda v: lax.all_to_all(v, 'gx', 0, 0, tiled=False)  14.9 us
    pallas_call x1, Pallas kernels, local(): call(centre_kernel, 'vaavsvv', [(cells, 'a'), (cells, 'a'), packed], [cel...  6.78 us
    ppermute x4, starting transfers between devices, local(): lax.ppermute(part, 'gx', [(i, i ^ 1) for i in range(8)])  4.7 us
    all_to_all x2, waiting for transfers between devices, local(): swap_x = lambda v: lax.all_to_all(v, 'gx', 0, 0, tiled=False)  4.58 us
  transfers between devices with their start and end apart: 11, of which 4 were waited for; matrix products, arithmetic and copies ran while one was open for 1% of the time, Pallas kernels for 3%

profile of v8, /device:TPU:1, one launch (start us, length us, event | category | flops | bytes accessed | tf_op | source)
XLA Modules:
  0.0 166.6 jit_solution(3945657828216569537)
XLA Ops:
  1.5 2.5 %shard_map.119 = f32[8,2,72,128]{3,2,1,0:T(8,128)S(1)} custom-call(f32[16,256,128]{2,1,0:T(8,128)} %bitcast.11, bf16[160,256]{1,0:T(8,128)(2,1)S(1)} %copy-done.3), custom_call_target="tpu_custom_call" | custom-call | tf_op jit(solution)/shard_map/pallas_call | solution.py:531
  4.0 16.3 %all_to_all.45.r_ref = f32[8,2,72,128]{3,2,1,0:T(8,128)S(1)} all-to-all(f32[8,2,72,128]{3,2,1,0:T(8,128)S(1)} %shard_map.119), channel_id=1, replica_groups=mesh['gx'=8,'gy'=32] {'gx'}, dimensions={0} | all-to-all | bytes 1179648 | tf_op jit(solution)/shard_map/all_to_all | solution.py:513
  20.3 1.3 shard_map.120
  21.6 11.0 %all-to-all-start.1 = ((f32[32,2,8,128]{3,2,1,0:T(8,128)}), f32[32,2,8,128]{3,2,1,0:T(8,128)S(1)}, u32[]{:S(2)}, u32[]{:S(2)}) async-start(f32[32,2,8,128]{3,2,1,0:T(8,128)} %shard_map.120), calls=%async_computation.1 | async-start | bytes 524288 | tf_op jit(solution)/shard_map/all_to_all | solution.py:514
  33.4 8.9 %all-to-all-done.1.v_ref = f32[32,2,8,128]{3,2,1,0:T(8,128)S(1)} async-done(((f32[32,2,8,128]{3,2,1,0:T(8,128)}), f32[32,2,8,128]{3,2,1,0:T(8,128)S(1)}, u32[]{:S(2)}, u32[]{:S(2)}) %all-to-all-start.1) | async-done | bytes 262176 | tf_op jit(solution)/shard_map/all_to_all | solution.py:514
  42.3 1.2 shard_map.122
  43.5 15.5 %all_to_all.46.v_ref = f32[32,2,8,128]{3,2,1,0:T(8,128)S(1)} all-to-all(f32[32,2,8,128]{3,2,1,0:T(8,128)S(1)} %get-tuple-element.23), channel_id=1, replica_groups=mesh['gx'=8,'gy'=32] {'gy'}, dimensions={0} | all-to-all | bytes 524288 | tf_op jit(solution)/shard_map/all_to_all | solution.py:514
  59.6 16.4 %all_to_all.47.r_ref = f32[8,2,72,128]{3,2,1,0:T(8,128)S(1)} all-to-all(f32[8,2,72,128]{3,2,1,0:T(8,128)S(1)} %shard_map.123), channel_id=1, replica_groups=mesh['gx'=8,'gy'=32] {'gx'}, dimensions={0} | all-to-all | bytes 1179648 | tf_op jit(solution)/shard_map/all_to_all | solution.py:513
  76.1 6.8 %shard_map.124 = (f32[16,256,128]{2,1,0:T(8,128)}, f32[16,256,128]{2,1,0:T(8,128)}, f32[8,2,72,128]{3,2,1,0:T(8,128)S(1)}) custom-call(f32[8,2,72,128]{3,2,1,0:T(8,128)S(1)} %all_to_all.47.r_ref, f32[16,256,128]{2,1,0:T(8,128)} %bitcast.12, f32[16,256,128]{2,1,0:T(8,128)} %bitcast.14, bf16[128,384]{1,0:T(8,128)(2,1)S(1)} %get-tuple-element.24.w_ref, ...), custom_call_target="tpu_custom_call" | custom-call | tf_op jit(solution)/shard_map/pallas_call | solution.py:537
  82.9 13.5 %all_to_all.48.r_ref = f32[8,2,72,128]{3,2,1,0:T(8,128)S(1)} all-to-all(f32[8,2,72,128]{3,2,1,0:T(8,128)S(1)} %get-tuple-element.26), channel_id=1, replica_groups=mesh['gx'=8,'gy'=32] {'gx'}, dimensions={0} | all-to-all | bytes 1179648 | tf_op jit(solution)/shard_map/all_to_all | solution.py:513
  97.1 13.6 %all_to_all.49.v_ref = f32[32,2,8,128]{3,2,1,0:T(8,128)S(1)} all-to-all(f32[32,2,8,128]{3,2,1,0:T(8,128)S(1)} %get-tuple-element.27), channel_id=1, replica_groups=mesh['gx'=8,'gy'=32] {'gy'}, dimensions={0} | all-to-all | bytes 524288 | tf_op jit(solution)/shard_map/all_to_all | solution.py:514
  110.8 1.6 shard_map.126
  112.3 7.0 %all-to-all-start.6 = ((f32[8,4,8,128]{3,2,1,0:T(8,128)}), f32[8,4,8,128]{3,2,1,0:T(8,128)S(1)}, u32[]{:S(2)}, u32[]{:S(2)}) async-start(f32[8,4,8,128]{3,2,1,0:T(8,128)} %get-tuple-element.31), calls=%async_computation.6 | async-start | bytes 262144 | tf_op jit(solution)/shard_map/all_to_all | solution.py:513
  120.0 4.6 %all-to-all-done.6.g_ref = f32[8,4,8,128]{3,2,1,0:T(8,128)S(1)} async-done(((f32[8,4,8,128]{3,2,1,0:T(8,128)}), f32[8,4,8,128]{3,2,1,0:T(8,128)S(1)}, u32[]{:S(2)}, u32[]{:S(2)}) %all-to-all-start.6) | async-done | bytes 131104 | tf_op jit(solution)/shard_map/all_to_all | solution.py:513
  125.4 4.2 %all-to-all-start.7 = ((f32[32,3,8,128]{3,2,1,0:T(8,128)}), f32[32,3,8,128]{3,2,1,0:T(8,128)S(1)}, u32[]{:S(2)}, u32[]{:S(2)}) async-start(f32[32,3,8,128]{3,2,1,0:T(8,128)} %shard_map.128), calls=%async_computation.7 | async-start | bytes 786432 | tf_op jit(solution)/shard_map/all_to_all | solution.py:514
  129.5 11.1 %all-to-all-done.7.v_ref.m_ref = f32[32,3,8,128]{3,2,1,0:T(8,128)S(1)} async-done(((f32[32,3,8,128]{3,2,1,0:T(8,128)}), f32[32,3,8,128]{3,2,1,0:T(8,128)S(1)}, u32[]{:S(2)}, u32[]{:S(2)}) %all-to-all-start.7) | async-done | bytes 393248 | tf_op jit(solution)/shard_map/all_to_all | solution.py:514
  140.6 1.5 shard_map.129
  142.1 7.9 %all-to-all-start.8 = ((f32[8,2,72,128]{3,2,1,0:T(8,128)}), f32[8,2,72,128]{3,2,1,0:T(8,128)S(1)}, u32[]{:S(2)}, u32[]{:S(2)}) async-start(f32[8,2,72,128]{3,2,1,0:T(8,128)} %get-tuple-element.32), calls=%async_computation.8 | async-start | bytes 1179648 | tf_op jit(solution)/shard_map/all_to_all | solution.py:513
  150.7 1.8 %collective-permute-start.1 = (f32[4,32,256]{2,1,0:T(8,128)S(1)}, f32[4,32,256]{2,1,0:T(8,128)S(1)}, u32[]{:S(2)}, u32[]{:S(2)}) collective-permute-start(f32[4,32,256]{2,1,0:T(8,128)S(1)} %shard_map.131.refs_7_), channel_id=1, source_target_pairs={{0,16},{1,17},{2,18},{3,19},{4,20},{5,21},{6,22},{7,23},{8,24},{9,... | collective-permute-start | bytes 393224 | tf_op jit(solution)/shard_map/ppermute | solution.py:560
  152.5 1.2 collective-permute-start.2
  155.3 1.7 %collective-permute-done.refs_0_ = f32[4,32,256]{2,1,0:T(8,128)S(1)} collective-permute-done((f32[4,32,256]{2,1,0:T(8,128)S(1)}, f32[4,32,256]{2,1,0:T(8,128)S(1)}, u32[]{:S(2)}, u32[]{:S(2)}) %collective-permute-start) | collective-permute-done | bytes 131104 | tf_op jit(solution)/shard_map/ppermute | solution.py:560
  157.1 3.2 %collective-permute-start.4 = (f32[4,32,256]{2,1,0:T(8,128)S(1)}, f32[4,32,256]{2,1,0:T(8,128)S(1)}, u32[]{:S(2)}, u32[]{:S(2)}) collective-permute-start(f32[4,32,256]{2,1,0:T(8,128)S(1)} %collective-permute-done.refs_0_), channel_id=1, source_target_pairs={{0,32},{32,0},{64,96},{96,64},{128,160},{160,128},{192,224},{224,1... | collective-permute-start | bytes 393224 | tf_op jit(solution)/shard_map/ppermute | solution.py:561
  161.4 3.6 %shard_map.130 = f32[16,256,128]{2,1,0:T(8,128)} custom-call(f32[8,2,72,128]{3,2,1,0:T(8,128)S(1)} %all-to-all-done.8.r_ref, f32[16,256,128]{2,1,0:T(8,128)} %get-tuple-element.33.g_hbm, bf16[128,384]{1,0:T(8,128)(2,1)S(1)} %get-tuple-element.34.w_ref, bf16[256,256]{1,0:T(8,128)(2,1)S(1)} %copy-done.2), custom_call_target="tpu_custom_call" | custom-call | tf_op jit(solution)/shard_map/pallas_call | solution.py:553
  165.0 1.6 shard_map.132
  (35 shorter events, 7.9 us)
Async XLA Ops:
  0.6 0.9 copy-start.3
  1.5 31.1 %copy-start.1 = (f32[4,16,16,256]{3,2,1,0:T(8,128)S(1)}, f32[4,16,16,256]{3,2,1,0:T(8,128)}, u32[]{:S(2)}) copy-start(f32[4,16,16,256]{3,2,1,0:T(8,128)} %param.10) | copy-start | bytes 3145732
  1.5 31.2 %copy-start.5 = (f32[16,16]{1,0:T(8,128)S(1)}, f32[16,16]{1,0:T(8,128)}, u32[]{:S(2)}) copy-start(f32[16,16]{1,0:T(8,128)} %pw_ref.1) | copy-start | bytes 3076
  4.0 38.3 %copy-start = (f32[256,128]{1,0:T(8,128)S(1)}, f32[256,128]{1,0:T(8,128)}, u32[]{:S(2)}) copy-start(f32[256,128]{1,0:T(8,128)} %constant.20.clone.q_ref) | copy-start | bytes 393220
  21.6 20.7 %all-to-all-start.1 = ((f32[32,2,8,128]{3,2,1,0:T(8,128)}), f32[32,2,8,128]{3,2,1,0:T(8,128)S(1)}, u32[]{:S(2)}, u32[]{:S(2)}) async-start(f32[32,2,8,128]{3,2,1,0:T(8,128)} %shard_map.120), calls=%async_computation.1 | async-start | bytes 524288 | tf_op jit(solution)/shard_map/all_to_all | solution.py:514
  32.6 43.4 %copy-start.2 = (bf16[256,256]{1,0:T(8,128)(2,1)S(1)}, bf16[256,256]{1,0:T(8,128)(2,1)}, u32[]{:S(2)}) copy-start(bf16[256,256]{1,0:T(8,128)(2,1)} %constant.22.clone.up_ref) | copy-start | bytes 393220
  32.6 43.4 %copy-start.4 = (bf16[160,256]{1,0:T(8,128)(2,1)S(1)}, bf16[160,256]{1,0:T(8,128)(2,1)}, u32[]{:S(2)}) copy-start(bf16[160,256]{1,0:T(8,128)(2,1)} %constant.21.clone.down_ref) | copy-start | bytes 245764
  32.6 43.4 %copy-start.6 = (f32[16]{0:T(128)S(1)}, f32[16]{0:T(128)}, u32[]{:S(2)}) copy-start(f32[16]{0:T(128)} %bias_ref.1) | copy-start | bytes 196
  112.3 12.3 %all-to-all-start.6 = ((f32[8,4,8,128]{3,2,1,0:T(8,128)}), f32[8,4,8,128]{3,2,1,0:T(8,128)S(1)}, u32[]{:S(2)}, u32[]{:S(2)}) async-start(f32[8,4,8,128]{3,2,1,0:T(8,128)} %get-tuple-element.31), calls=%async_computation.6 | async-start | bytes 262144 | tf_op jit(solution)/shard_map/all_to_all | solution.py:513
  125.4 15.2 %all-to-all-start.7 = ((f32[32,3,8,128]{3,2,1,0:T(8,128)}), f32[32,3,8,128]{3,2,1,0:T(8,128)S(1)}, u32[]{:S(2)}, u32[]{:S(2)}) async-start(f32[32,3,8,128]{3,2,1,0:T(8,128)} %shard_map.128), calls=%async_computation.7 | async-start | bytes 786432 | tf_op jit(solution)/shard_map/all_to_all | solution.py:514
  142.1 19.3 %all-to-all-start.8 = ((f32[8,2,72,128]{3,2,1,0:T(8,128)}), f32[8,2,72,128]{3,2,1,0:T(8,128)S(1)}, u32[]{:S(2)}, u32[]{:S(2)}) async-start(f32[8,2,72,128]{3,2,1,0:T(8,128)} %get-tuple-element.32), calls=%async_computation.8 | async-start | bytes 1179648 | tf_op jit(solution)/shard_map/all_to_all | solution.py:513
  150.2 6.8 %collective-permute-start = (f32[4,32,256]{2,1,0:T(8,128)S(1)}, f32[4,32,256]{2,1,0:T(8,128)S(1)}, u32[]{:S(2)}, u32[]{:S(2)}) collective-permute-start(f32[4,32,256]{2,1,0:T(8,128)S(1)} %shard_map.131.refs_7_), channel_id=1, source_target_pairs={{0,8},{1,9},{2,10},{3,11},{4,12},{5,13},{6,14},{7,15},{8,16},{9,17... | collective-permute-start | bytes 393224 | tf_op jit(solution)/shard_map/ppermute | solution.py:560
  150.7 9.6 %collective-permute-start.1 = (f32[4,32,256]{2,1,0:T(8,128)S(1)}, f32[4,32,256]{2,1,0:T(8,128)S(1)}, u32[]{:S(2)}, u32[]{:S(2)}) collective-permute-start(f32[4,32,256]{2,1,0:T(8,128)S(1)} %shard_map.131.refs_7_), channel_id=1, source_target_pairs={{0,16},{1,17},{2,18},{3,19},{4,20},{5,21},{6,22},{7,23},{8,24},{9,... | collective-permute-start | bytes 393224 | tf_op jit(solution)/shard_map/ppermute | solution.py:560
  152.5 7.8 %collective-permute-start.2 = (f32[4,32,256]{2,1,0:T(8,128)S(1)}, f32[4,32,256]{2,1,0:T(8,128)S(1)}, u32[]{:S(2)}, u32[]{:S(2)}) collective-permute-start(f32[4,32,256]{2,1,0:T(8,128)S(1)} %shard_map.131.refs_7_), channel_id=1, source_target_pairs={{0,24},{1,25},{2,26},{3,27},{4,28},{5,29},{6,30},{7,31},{8,0},{9,1... | collective-permute-start | bytes 393224 | tf_op jit(solution)/shard_map/ppermute | solution.py:560
  154.4 10.6 %collective-permute-start.3 = (f32[4,32,256]{2,1,0:T(8,128)S(1)}, f32[4,32,256]{2,1,0:T(8,128)S(1)}, u32[]{:S(2)}, u32[]{:S(2)}) collective-permute-start(f32[4,32,256]{2,1,0:T(8,128)S(1)} %shard_map.131.refs_7_), channel_id=1, source_target_pairs={{0,32},{32,0},{64,96},{96,64},{128,160},{160,128},{192,224},{224,1... | collective-permute-start | bytes 393224 | tf_op jit(solution)/shard_map/ppermute | solution.py:561
  157.1 7.9 %collective-permute-start.4 = (f32[4,32,256]{2,1,0:T(8,128)S(1)}, f32[4,32,256]{2,1,0:T(8,128)S(1)}, u32[]{:S(2)}, u32[]{:S(2)}) collective-permute-start(f32[4,32,256]{2,1,0:T(8,128)S(1)} %collective-permute-done.refs_0_), channel_id=1, source_target_pairs={{0,32},{32,0},{64,96},{96,64},{128,160},{160,128},{192,224},{224,1... | collective-permute-start | bytes 393224 | tf_op jit(solution)/shard_map/ppermute | solution.py:561
  160.3 4.8 %collective-permute-start.5 = (f32[4,32,256]{2,1,0:T(8,128)S(1)}, f32[4,32,256]{2,1,0:T(8,128)S(1)}, u32[]{:S(2)}, u32[]{:S(2)}) collective-permute-start(f32[4,32,256]{2,1,0:T(8,128)S(1)} %collective-permute-done.1.refs_1_), channel_id=1, source_target_pairs={{0,32},{32,0},{64,96},{96,64},{128,160},{160,128},{192,224},{224,1... | collective-permute-start | bytes 393224 | tf_op jit(solution)/shard_map/ppermute | solution.py:561
  160.3 4.8 %collective-permute-start.6 = (f32[4,32,256]{2,1,0:T(8,128)S(1)}, f32[4,32,256]{2,1,0:T(8,128)S(1)}, u32[]{:S(2)}, u32[]{:S(2)}) collective-permute-start(f32[4,32,256]{2,1,0:T(8,128)S(1)} %collective-permute-done.2.refs_2_), channel_id=1, source_target_pairs={{0,32},{32,0},{64,96},{96,64},{128,160},{160,128},{192,224},{224,1... | collective-permute-start | bytes 393224 | tf_op jit(solution)/shard_map/ppermute | solution.py:561
